TPU v7x, 32 devices: a whole 2x2x4 slice. The times are simulated.
32 devices in a mesh: row: 8 (over z, x), col: 4 (over y, core).
Axes of the slice: x: 2, y: 2, z: 4, core: 2. Of those that a mesh axis runs over, the one named last changes fastest.
Arguments:
- features: bfloat16 [32768, 1024], P(('row', 'col')), may hold values from -12 to 12
- cotangent: bfloat16 [32768, 1024], P(('row', 'col')), may hold values from -6 to 6
- loader: int32 [32768], replicated, may hold values from 0 to 32767, as said below
- w_query: bfloat16 [1024, 1024], replicated, may hold values from -2 to 2
- w_key: bfloat16 [1024, 1024], replicated, may hold values from -2 to 2
- w_value: bfloat16 [1024, 1024], replicated, may hold values from -0.1875 to 0.1875
- norm_gain: float32 [1024], replicated, may hold values from 0.25 to 1.75
- send_blocks: int32 [32, 4, 2], replicated, may hold values from -1 to 7, as said below
- tile_lists: int32 [256, 3], P(('row', 'col')), may hold values from 0 to 15, as said below
Outputs:
- layer_out: bfloat16 [32768, 1024], P(('row', 'col'))
- grad_features: bfloat16 [32768, 1024], P(('row', 'col'))
Inputs may be any that keep to these rules, and one draw needn't show every extreme that they name: `loader`: a permutation of the 32768 node numbers; the 1024 rows of each device hold exactly 32 nodes owned by each device. `send_blocks`: entry [e, p, s] is a block of device e (a number below 8) sent to the device of e's row group with col index p in slot s, or -1 for an empty slot; the nonempty slots of one (e, p) come first and name distinct blocks; slots toward e's own col index are empty; all 2 slots toward the next col index (cyclically) are filled. `tile_lists`: row b names 3 distinct entries of the tile table of b's device, never b's own block and never an empty slot; every nonempty received slot is named by some block of its device.
All inputs are finite; a program needn't handle non-finite values.
Results may differ from a plain program's by a relative error of at most 0.012.
The roundings to bfloat16 on the way count: a program that leaves them out, or rounds other values in their place, can miss the bound.
Values may be sent and summed in bfloat16 or wider, within the bound.
No kernel may reach another device: no remote copies, remote signals or barrier semaphores. Data moves between devices by JAX's collectives and lax.ppermute only.
A program may use at most 256 MiB of HBM per device.

v0:
```python
import jax
import jax.numpy as jnp
from jax import lax
from jax.sharding import PartitionSpec as P

HEADS = 8
HEAD_DIM = 128


def attend(queries, key_rows, value_rows, cot_rows, gain_row):
    count = queries.shape[0]
    width = queries.shape[2]
    q_heads = queries.reshape(count, -1, HEADS, HEAD_DIM)
    k_heads = key_rows.reshape(count, -1, HEADS, HEAD_DIM)
    v_heads = value_rows.reshape(count, -1, HEADS, HEAD_DIM)
    score_scale = HEAD_DIM ** (-0.5)
    scores = (
        jnp.einsum("bqhd,bkhd->bhqk", q_heads, k_heads, preferred_element_type=jnp.float32)
        * score_scale
    )
    row_max = jnp.max(scores, axis=-1, keepdims=True)
    expo = jnp.exp(scores - row_max)
    prob_full = expo / jnp.sum(expo, axis=-1, keepdims=True)
    prob_half = prob_full.astype(jnp.bfloat16)
    mixed_out = jnp.einsum(
        "bhqk,bkhd->bqhd", prob_half, v_heads, preferred_element_type=jnp.float32
    ).reshape(count, -1, width)
    inv_rms = lax.rsqrt(jnp.mean(mixed_out * mixed_out, axis=-1, keepdims=True) + 1e-06)
    normed = (mixed_out * inv_rms * gain_row).astype(jnp.bfloat16)
    grad_in = cot_rows.astype(jnp.float32) * gain_row
    inner = jnp.mean(grad_in * mixed_out, axis=-1, keepdims=True)
    grad_mix = (inv_rms * (grad_in - mixed_out * inv_rms * inv_rms * inner)).astype(jnp.bfloat16)
    grad_heads = grad_mix.reshape(count, -1, HEADS, HEAD_DIM)
    grad_prob = jnp.einsum(
        "bqhd,bkhd->bhqk", grad_heads, v_heads, preferred_element_type=jnp.float32
    )
    delta = jnp.sum(prob_full * grad_prob, axis=-1, keepdims=True)
    grad_score = (prob_full * (grad_prob - delta) * score_scale).astype(jnp.bfloat16)
    grad_query = jnp.einsum(
        "bhqk,bkhd->bqhd", grad_score, k_heads, preferred_element_type=jnp.float32
    )
    grad_query = grad_query.reshape(count, -1, width).astype(jnp.bfloat16)
    grad_key = jnp.einsum(
        "bhqk,bqhd->bkhd", grad_score, q_heads, preferred_element_type=jnp.float32
    ).reshape(count, -1, width)
    grad_value = jnp.einsum(
        "bhqk,bqhd->bkhd", prob_half, grad_heads, preferred_element_type=jnp.float32
    ).reshape(count, -1, width)
    return (normed, grad_query, grad_key, grad_value)


def project_back(kv_rows, w_key, w_value, width):
    contract = (((1,), (1,)), ((), ()))
    total = lax.dot_general(kv_rows[:, :width], w_key, contract, preferred_element_type=jnp.float32)
    return total + lax.dot_general(
        kv_rows[:, width:], w_value, contract, preferred_element_type=jnp.float32
    )


def body(features, cotangent, loader, w_query, w_key, w_value, norm_gain, send_blocks, tile_lists):
    row_count = lax.axis_size("row")
    col_count = lax.axis_size("col")
    devices = row_count * col_count
    self_index = lax.axis_index("row") * col_count + lax.axis_index("col")
    rows_dev = features.shape[0]
    width = features.shape[1]
    per_peer = rows_dev // devices
    block_count = tile_lists.shape[0]
    block_rows = rows_dev // block_count
    capacity = send_blocks.shape[2]
    slots = block_count + col_count * capacity
    my_nodes = lax.dynamic_slice_in_dim(loader, self_index * rows_dev, rows_dev)
    send_order = jnp.argsort(my_nodes // rows_dev, stable=True)
    back_order = jnp.argsort(send_order)
    all_owners = (loader // rows_dev).reshape(devices, rows_dev)
    arrive_pos = jnp.argsort(jnp.where(all_owners == self_index, 0, 1), axis=1, stable=True)[
        :, :per_peer
    ]
    arriving = (
        jnp.take_along_axis(loader.reshape(devices, rows_dev), arrive_pos, axis=1).reshape(rows_dev)
        - self_index * rows_dev
    )
    placing = jnp.argsort(arriving)

    def regroup(buffer):
        return lax.all_to_all(buffer, ("row", "col"), split_axis=0, concat_axis=0, tiled=True)

    outgoing = jnp.concatenate([features[send_order], cotangent[send_order]], axis=1).reshape(
        devices, per_peer, 2 * width
    )
    incoming = regroup(outgoing).reshape(rows_dev, 2 * width)[placing]
    owned_rows = incoming[:, :width]
    owned_cot = incoming[:, width:]
    queries = jnp.dot(owned_rows, w_query, preferred_element_type=jnp.float32).astype(jnp.bfloat16)
    key_all = jnp.dot(owned_rows, w_key, preferred_element_type=jnp.float32).astype(jnp.bfloat16)
    value_all = jnp.dot(owned_rows, w_value, preferred_element_type=jnp.float32).astype(
        jnp.bfloat16
    )
    kv_local = jnp.concatenate([key_all, value_all], axis=1).reshape(
        block_count, block_rows, 2 * width
    )
    send_row = lax.dynamic_index_in_dim(send_blocks, self_index, 0, keepdims=False)
    filled = (send_row >= 0)[:, :, None, None]
    picked = jnp.maximum(send_row, 0)
    outbound = jnp.where(filled, kv_local[picked], jnp.zeros((), jnp.bfloat16))
    arrived_kv = lax.all_to_all(outbound, "col", split_axis=0, concat_axis=0, tiled=True).reshape(
        col_count * capacity, block_rows, 2 * width
    )
    tile_table = jnp.concatenate([kv_local, arrived_kv], axis=0)
    read_entries = jnp.concatenate(
        [jnp.arange(block_count, dtype=jnp.int32)[:, None], tile_lists], axis=1
    )
    group_size = 4
    group_count = block_count // group_size

    def per_group(totals, inputs):
        q_group, cot_group, read_group = inputs
        picked_kv = tile_table[read_group].reshape(group_size, -1, 2 * width)
        normed, grad_query, grad_key, grad_value = attend(
            q_group, picked_kv[:, :, :width], picked_kv[:, :, width:], cot_group, norm_gain
        )
        grad_tiles = jnp.concatenate(
            [grad_key.reshape(-1, block_rows, width), grad_value.reshape(-1, block_rows, width)],
            axis=2,
        )
        totals = totals.at[read_group.reshape(-1)].add(grad_tiles)
        return (totals, (normed, grad_query))

    group_inputs = (
        queries.reshape(group_count, group_size, block_rows, width),
        owned_cot.reshape(group_count, group_size, block_rows, width),
        read_entries.reshape(group_count, group_size, -1),
    )
    start = jnp.zeros((slots, block_rows, 2 * width), jnp.float32)
    entry_grads, (normed_all, grad_query_all) = lax.scan(per_group, start, group_inputs)
    remote_kv = entry_grads[block_count:].astype(jnp.bfloat16)
    back_hot = (
        send_row[:, :, None] == jnp.arange(block_count, dtype=jnp.int32)[None, None, :]
    ).astype(jnp.float32)
    back_hot = back_hot.reshape(col_count * capacity, block_count)
    remote_rows = remote_kv.reshape(col_count * capacity * block_rows, 2 * width)
    remote_proj = project_back(remote_rows, w_key, w_value, width).astype(jnp.bfloat16)
    remote_proj = remote_proj.reshape(col_count, capacity, block_rows * width)
    returned = lax.all_to_all(remote_proj, "col", split_axis=0, concat_axis=0, tiled=True)
    returned = returned.reshape(col_count * capacity, block_rows * width).astype(jnp.float32)
    back_sum = lax.dot_general(
        back_hot, returned, (((0,), (0,)), ((), ())), precision=lax.Precision.HIGHEST
    )
    local_kv = entry_grads[:block_count].reshape(rows_dev, 2 * width).astype(jnp.bfloat16)
    grad_query_rows = grad_query_all.reshape(rows_dev, width)
    contract = (((1,), (1,)), ((), ()))
    grad_owned = lax.dot_general(
        grad_query_rows, w_query, contract, preferred_element_type=jnp.float32
    )
    grad_owned = grad_owned + project_back(local_kv, w_key, w_value, width)
    grad_owned = (grad_owned + back_sum.reshape(rows_dev, width)).astype(jnp.bfloat16)
    layer_rows = normed_all.reshape(rows_dev, width)
    layer_back = regroup(layer_rows[arriving].reshape(devices, per_peer, width)).reshape(
        rows_dev, width
    )[back_order]
    grad_back = regroup(grad_owned[arriving].reshape(devices, per_peer, width)).reshape(
        rows_dev, width
    )[back_order]
    return (layer_back, grad_back)


def solution(mesh):
    in_specs = (
        P(("row", "col"), None),
        P(("row", "col"), None),
        P(),
        P(),
        P(),
        P(),
        P(),
        P(),
        P(("row", "col"), None),
    )
    out_specs = (P(("row", "col"), None), P(("row", "col"), None))
    return jax.shard_map(body, mesh=mesh, in_specs=in_specs, out_specs=out_specs, check_vma=False)
```

profile of v0, /device:TPU:0, one launch (start us, length us, event | category | flops | bytes accessed | tf_op | source)
XLA Modules:
  0.0 880.3 jit_solution(3138944694689780795)
XLA Ops:
  62.4 72.3 %all-to-all-done = bf16[32,32,2048]{2,1,0:T(8,128)(2,1)} async-done(((bf16[32,32,2048]{2,1,0:T(8,128)(2,1)}), bf16[32,32,2048]{2,1,0:T(8,128)(2,1)}, u32[]{:S(2)}, u32[]{:S(2)}) %all-to-all-start) | async-done | bytes 4194336 | tf_op jit(solution)/shard_map/all_to_all | solution.py:86
  134.7 11.6 %gather_fusion.3 = bf16[1024,2048]{1,0:T(8,128)(2,1)} fusion(bf16[1024,2048]{1,0:T(8,128)(2,1)} %bitcast.16, s32[1024]{0:T(1024)S(1)} %fusion.62), kind=kCustom, calls=%fused_computation.3 | custom fusion | bytes 8392704 | tf_op jit(solution)/shard_map/gather | solution.py:91
  171.2 20.7 %all-to-all-start.1 = ((bf16[4,2,128,2048]{3,2,1,0:T(8,128)(2,1)}), bf16[4,2,128,2048]{3,2,1,0:T(8,128)(2,1)}, u32[]{:S(2)}, u32[]{:S(2)}) async-start(bf16[4,2,128,2048]{3,2,1,0:T(8,128)(2,1)} %broadcast_select_fusion), calls=%async_computation.1 | async-start | bytes 8388608 | tf_op jit(solution)/shard_map/all_to_all | solution.py:106
  200.5 39.6 %all-to-all-done.1 = bf16[4,2,128,2048]{3,2,1,0:T(8,128)(2,1)} async-done(((bf16[4,2,128,2048]{3,2,1,0:T(8,128)(2,1)}), bf16[4,2,128,2048]{3,2,1,0:T(8,128)(2,1)}, u32[]{:S(2)}, u32[]{:S(2)}) %all-to-all-start.1) | async-done | bytes 4194336 | tf_op jit(solution)/shard_map/all_to_all | solution.py:106
  255.3 454.3 %while.14 = (s32[]{:T(128)}, f32[16,128,2048]{2,1,0:T(8,128)}, bf16[2,4,128,1024]{3,2,1,0:T(8,128)(2,1)}, bf16[2,4,128,1024]{3,2,1,0:T(8,128)(2,1)}, s32[2,4,4]{...) while((s32[]{:T(128)}, f32[16,128,2048]{2,1,0:T(8,128)}, ...), condition=%wide.region_10.11_spmd, body=%wide.region_3.10_spmd.sunk | while | flops 3283102720 | bytes 372362752 | solution.py:135
  309.6 35.2 %fusion.127 = bf16[4,8,128,128]{3,2,1,0:T(8,128)(2,1)} fusion(bf16[4,512,8,128]{1,3,2,0:T(8,128)(2,1)} %bitcast.135, f32[4,8,128,512]{3,2,1,0:T(8,128)} %fusion.125, f32[4,8,128,512]{3,2,1,0:T(8,128)} %get-tuple-element.201, f32[4,8,128]{2,1,0:T(8,128)S(1)} %get-tuple-element.202), kind=kOutput, calls=%fused_computation.43.clone.1 | convolution fusion | flops 552079872 | bytes 22036480 | tf_op jit(solution)/shard_map/while/body/eval_jaxpr/bhqk,bkhd->bqhd/dot_general | solution.py:39
  354.2 35.9 %fusion.126 = f32[4,512,8,128]{1,3,2,0:T(8,128)} fusion(bf16[4,128,8,128]{1,3,2,0:T(8,128)(2,1)} %bitcast.140, f32[4,8,128,512]{3,2,1,0:T(8,128)} %fusion.125, f32[4,8,128,512]{3,2,1,0:T(8,128)} %get-tuple-element.201, f32[4,8,128]{2,1,0:T(8,128)S(1)} %get-tuple-element.202), kind=kOutput, calls=%fused_computation.24.clone.1 | convolution fusion | flops 551555584 | bytes 26230784 | tf_op jit(solution)/shard_map/while/body/eval_jaxpr/bhqk,bqhd->bkhd/dot_general | solution.py:43
  390.1 9.9 %copy.103 = f32[4,512,8,128]{3,2,1,0:T(8,128)} copy(f32[4,512,8,128]{1,3,2,0:T(8,128)} %fusion.126) | data formatting | bytes 16777216 | tf_op jit(solution)/shard_map/while/body/eval_jaxpr/bhqk,bqhd->bkhd/transpose | solution.py:43
  400.1 9.3 %reshape.404 = f32[16,128,1024]{2,1,0:T(8,128)} reshape(f32[4,512,8,128]{3,2,1,0:T(8,128)} %copy.103) | data formatting | bytes 16777216 | tf_op jit(solution)/shard_map/while/body/eval_jaxpr/reshape;while/body/eval_jaxpr/reshape | solution.py:123
  417.3 9.9 %copy.102 = f32[4,512,8,128]{3,2,1,0:T(8,128)} copy(f32[4,512,8,128]{1,3,2,0:T(8,128)} %convolution_bitcast_fusion.3) | data formatting | bytes 16777216 | tf_op jit(solution)/shard_map/while/body/eval_jaxpr/bhqk,bqhd->bkhd/transpose | solution.py:46
  427.2 9.2 %reshape.403 = f32[16,128,1024]{2,1,0:T(8,128)} reshape(f32[4,512,8,128]{3,2,1,0:T(8,128)} %copy.102) | data formatting | bytes 16777216 | tf_op jit(solution)/shard_map/while/body/eval_jaxpr/reshape;while/body/eval_jaxpr/reshape | solution.py:123
  436.5 11.7 %pad_maximum_fusion.5 = f32[16,128,2048]{2,1,0:T(8,128)} fusion(f32[16,128,1024]{2,1,0:T(8,128)} %reshape.403, f32[16,128,1024]{2,1,0:T(8,128)} %reshape.404), kind=kLoop, calls=%fused_computation.13.clone.1 | loop fusion | flops 4194304 | bytes 33554432 | tf_op jit(solution)/shard_map/while/body/eval_jaxpr/concatenate | solution.py:122
  448.2 34.3 %scatter_fusion = f32[16,128,2048]{2,1,0:T(8,128)} fusion(f32[16,128,2048]{2,1,0:T(8,128)} %get-tuple-element.219, s32[16]{0:T(128)S(1)} %fusion.120, f32[16,128,2048]{2,1,0:T(8,128)} %pad_maximum_fusion.5), kind=kCustom, calls=%fused_computation.10.clone.1 | custom fusion | flops 4194304 | bytes 50331712 | tf_op jit(solution)/shard_map/while/body/eval_jaxpr/scatter-add | solution.py:126
  536.9 35.2 %fusion.127 = bf16[4,8,128,128]{3,2,1,0:T(8,128)(2,1)} fusion(bf16[4,512,8,128]{1,3,2,0:T(8,128)(2,1)} %bitcast.135, f32[4,8,128,512]{3,2,1,0:T(8,128)} %fusion.125, f32[4,8,128,512]{3,2,1,0:T(8,128)} %get-tuple-element.201, f32[4,8,128]{2,1,0:T(8,128)S(1)} %get-tuple-element.202), kind=kOutput, calls=%fused_computation.43.clone.1 | convolution fusion | flops 552079872 | bytes 22036480 | tf_op jit(solution)/shard_map/while/body/eval_jaxpr/bhqk,bkhd->bqhd/dot_general | solution.py:39
  581.5 35.9 %fusion.126 = f32[4,512,8,128]{1,3,2,0:T(8,128)} fusion(bf16[4,128,8,128]{1,3,2,0:T(8,128)(2,1)} %bitcast.140, f32[4,8,128,512]{3,2,1,0:T(8,128)} %fusion.125, f32[4,8,128,512]{3,2,1,0:T(8,128)} %get-tuple-element.201, f32[4,8,128]{2,1,0:T(8,128)S(1)} %get-tuple-element.202), kind=kOutput, calls=%fused_computation.24.clone.1 | convolution fusion | flops 551555584 | bytes 26230784 | tf_op jit(solution)/shard_map/while/body/eval_jaxpr/bhqk,bqhd->bkhd/dot_general | solution.py:43
  617.4 9.9 %copy.103 = f32[4,512,8,128]{3,2,1,0:T(8,128)} copy(f32[4,512,8,128]{1,3,2,0:T(8,128)} %fusion.126) | data formatting | bytes 16777216 | tf_op jit(solution)/shard_map/while/body/eval_jaxpr/bhqk,bqhd->bkhd/transpose | solution.py:43
  627.3 9.3 %reshape.404 = f32[16,128,1024]{2,1,0:T(8,128)} reshape(f32[4,512,8,128]{3,2,1,0:T(8,128)} %copy.103) | data formatting | bytes 16777216 | tf_op jit(solution)/shard_map/while/body/eval_jaxpr/reshape;while/body/eval_jaxpr/reshape | solution.py:123
  644.6 9.9 %copy.102 = f32[4,512,8,128]{3,2,1,0:T(8,128)} copy(f32[4,512,8,128]{1,3,2,0:T(8,128)} %convolution_bitcast_fusion.3) | data formatting | bytes 16777216 | tf_op jit(solution)/shard_map/while/body/eval_jaxpr/bhqk,bqhd->bkhd/transpose | solution.py:46
  663.7 11.7 %pad_maximum_fusion.5 = f32[16,128,2048]{2,1,0:T(8,128)} fusion(f32[16,128,1024]{2,1,0:T(8,128)} %reshape.403, f32[16,128,1024]{2,1,0:T(8,128)} %reshape.404), kind=kLoop, calls=%fused_computation.13.clone.1 | loop fusion | flops 4194304 | bytes 33554432 | tf_op jit(solution)/shard_map/while/body/eval_jaxpr/concatenate | solution.py:122
  675.5 34.1 %scatter_fusion = f32[16,128,2048]{2,1,0:T(8,128)} fusion(f32[16,128,2048]{2,1,0:T(8,128)} %get-tuple-element.219, s32[16]{0:T(128)S(1)} %fusion.120, f32[16,128,2048]{2,1,0:T(8,128)} %pad_maximum_fusion.5), kind=kCustom, calls=%fused_computation.10.clone.1 | custom fusion | flops 4194304 | bytes 50331712 | tf_op jit(solution)/shard_map/while/body/eval_jaxpr/scatter-add | solution.py:126
  741.8 17.7 %all-to-all-done.3 = bf16[4,2,131072]{2,1,0:T(2,128)(2,1)} async-done(((bf16[4,2,131072]{2,1,0:T(2,128)(2,1)}), bf16[4,2,131072]{2,1,0:T(2,128)(2,1)}, u32[]{:S(2)}, u32[]{:S(2)}) %all-to-all-start.3) | async-done | bytes 2097184 | tf_op jit(solution)/shard_map/all_to_all | solution.py:144
  784.9 9.6 %add_convert_fusion = bf16[1024,1024]{1,0:T(8,128)(2,1)} fusion(f32[1024,1024]{1,0:T(8,128)} %reshape.283, f32[1024,1024]{1,0:T(8,128)} %fusion.48, f32[1024,1024]{1,0:T(8,128)} %fusion.46, bf16[1024,1024]{1,0:T(8,128)(2,1)} %bitcast.159, bf16[1024,1024]{1,0:T(8,128)(2,1)} %param.14), kind=kOutput, calls=%fused_computation.65 | convolution fusion | flops 2151677952 | bytes 18874368 | tf_op jit(solution)/shard_map/dot_general | solution.py:152
  802.4 9.9 %all-to-all-done.2 = bf16[32,32,1024]{2,1,0:T(8,128)(2,1)} async-done(((bf16[32,32,1024]{2,1,0:T(8,128)(2,1)}), bf16[32,32,1024]{2,1,0:T(8,128)(2,1)}, u32[]{:S(2)}, u32[]{:S(2)}) %all-to-all-start.2) | async-done | bytes 2097184 | tf_op jit(solution)/shard_map/all_to_all | solution.py:86
  828.8 36.5 %all-to-all-done.4 = bf16[32,32,1024]{2,1,0:T(8,128)(2,1)} async-done(((bf16[32,32,1024]{2,1,0:T(8,128)(2,1)}), bf16[32,32,1024]{2,1,0:T(8,128)(2,1)}, u32[]{:S(2)}, u32[]{:S(2)}) %all-to-all-start.4) | async-done | bytes 2097184 | tf_op jit(solution)/shard_map/all_to_all | solution.py:86
  (170 shorter events, 346.2 us)
Async XLA Ops:
  7.2 139.1 %copy-start = (bf16[1024,1024]{1,0:T(8,128)(2,1)S(1)}, bf16[1024,1024]{1,0:T(8,128)(2,1)}, u32[]{:S(2)}) copy-start(bf16[1024,1024]{1,0:T(8,128)(2,1)} %param.16) | copy-start | bytes 6291460
  12.4 7.9 copy-start.13
  32.9 7.5 copy-start.9
  32.9 9.0 %copy-start.17 = (s32[32,4,2]{0,2,1:T(2,128)S(1)}, s32[32,4,2]{0,2,1:T(2,128)}, u32[]{:S(2)}) copy-start(s32[32,4,2]{0,2,1:T(2,128)} %param.18) | copy-start | bytes 3076
  32.9 101.8 %all-to-all-start = ((bf16[32,32,2048]{2,1,0:T(8,128)(2,1)}), bf16[32,32,2048]{2,1,0:T(8,128)(2,1)}, u32[]{:S(2)}, u32[]{:S(2)}) async-start(bf16[32,32,2048]{2,1,0:T(8,128)(2,1)} %bitcast.146), calls=%async_computation | async-start | bytes 8388608 | tf_op jit(solution)/shard_map/all_to_all | solution.py:86
  40.3 7.5 sort.70.cloned.1.call-start
  57.9 88.3 %copy-start.11 = (s32[32,32]{1,0:T(8,128)}, s32[32,32]{1,0:T(8,128)S(1)}, u32[]{:S(2)}) copy-start(s32[32,32]{1,0:T(8,128)S(1)} %select_subtract_fusion) | copy-start | bytes 12292
  146.2 4.1 copy-start.6
  146.2 4.2 copy-start.19
  171.1 20.7 %copy-start.18 = (s32[8,3]{0,1:T(4,128)S(1)}, s32[8,3]{0,1:T(4,128)}, u32[]{:S(2)}) copy-start(s32[8,3]{0,1:T(4,128)} %param.19) | copy-start | bytes 292
  171.2 68.9 %all-to-all-start.1 = ((bf16[4,2,128,2048]{3,2,1,0:T(8,128)(2,1)}), bf16[4,2,128,2048]{3,2,1,0:T(8,128)(2,1)}, u32[]{:S(2)}, u32[]{:S(2)}) async-start(bf16[4,2,128,2048]{3,2,1,0:T(8,128)(2,1)} %broadcast_select_fusion), calls=%async_computation.1 | async-start | bytes 8388608 | tf_op jit(solution)/shard_map/all_to_all | solution.py:106
  247.5 7.8 copy-start.10
  295.6 7.9 copy-start.3
  400.0 9.3 %copy-start.5 = (bf16[4,128,8,128]{1,3,2,0:T(8,128)(2,1)S(1)}, bf16[4,128,8,128]{1,3,2,0:T(8,128)(2,1)}, u32[]{:S(2)}) copy-start(bf16[4,128,8,128]{1,3,2,0:T(8,128)(2,1)} %copy-done.4) | copy-start | bytes 3145732 | tf_op jit(solution)/shard_map/while
  522.8 7.9 copy-start.3
  627.3 9.3 %copy-start.5 = (bf16[4,128,8,128]{1,3,2,0:T(8,128)(2,1)S(1)}, bf16[4,128,8,128]{1,3,2,0:T(8,128)(2,1)}, u32[]{:S(2)}) copy-start(bf16[4,128,8,128]{1,3,2,0:T(8,128)(2,1)} %copy-done.4) | copy-start | bytes 3145732 | tf_op jit(solution)/shard_map/while
  724.8 9.0 %copy-start.12 = (s32[32,32]{1,0:T(8,128)S(1)}, s32[32,32]{1,0:T(8,128)}, u32[]{:S(2)}) copy-start(s32[32,32]{1,0:T(8,128)} %copy-done.11) | copy-start | bytes 12292
  729.3 30.3 %all-to-all-start.3 = ((bf16[4,2,131072]{2,1,0:T(2,128)(2,1)}), bf16[4,2,131072]{2,1,0:T(2,128)(2,1)}, u32[]{:S(2)}, u32[]{:S(2)}) async-start(bf16[4,2,131072]{2,1,0:T(2,128)(2,1)} %reshape.282), calls=%async_computation.3 | async-start | bytes 4194304 | tf_op jit(solution)/shard_map/all_to_all | solution.py:144
  759.6 52.7 %all-to-all-start.2 = ((bf16[32,32,1024]{2,1,0:T(8,128)(2,1)}), bf16[32,32,1024]{2,1,0:T(8,128)(2,1)}, u32[]{:S(2)}, u32[]{:S(2)}) async-start(bf16[32,32,1024]{2,1,0:T(8,128)(2,1)} %bitcast.148), calls=%async_computation.2 | async-start | bytes 4194304 | tf_op jit(solution)/shard_map/all_to_all | solution.py:86
  763.6 6.1 copy-start.8
  763.6 6.1 copy-start.21
  769.7 4.3 copy-start.16
  802.4 14.2 %copy-start.14 = (s32[1024]{0:T(1024)S(1)}, s32[1024]{0:T(1024)}, u32[]{:S(2)}) copy-start(s32[1024]{0:T(1024)} %copy-done.13) | copy-start | bytes 12292
  812.3 53.0 %all-to-all-start.4 = ((bf16[32,32,1024]{2,1,0:T(8,128)(2,1)}), bf16[32,32,1024]{2,1,0:T(8,128)(2,1)}, u32[]{:S(2)}, u32[]{:S(2)}) async-start(bf16[32,32,1024]{2,1,0:T(8,128)(2,1)} %bitcast.149), calls=%async_computation.4 | async-start | bytes 4194304 | tf_op jit(solution)/shard_map/all_to_all | solution.py:86
  (9 other events, 17.1 us)
Sparse Core Ops, SparseCore 0:
  44.2 3.2 sort.72.cloned.1.call-done
  (1 shorter events, 0.0 us)
where the time goes:
time: 893 us; the launch traced here: 880 us
  local copies, waits for them, and re-layouts  268 us (30%)
  matrix products  241 us (27%)
  waiting for transfers between devices  176 us (20%)
  other arithmetic  140 us (16%)
  starting transfers between devices  40.8 us (5%)
  between operations  14.5 us (2%)
    all_to_all x3, waiting for transfers between devices, regroup(): lax.all_to_all(buffer, ('row', 'col'), split_axis=0, concat_axis=0, tiled...  119 us
    dot_general x2, matrix products, attend(): jnp.einsum('bhqk,bqhd->bkhd', grad_score, q_heads, preferred_element_type...  71.7 us
    dot_general x2, matrix products, attend(): jnp.einsum('bhqk,bkhd->bqhd', grad_score, k_heads, preferred_element_type...  70.4 us
    scatter-add x2, other arithmetic, per_group(): totals = totals.at[read_group.reshape(-1)].add(grad_tiles)  68.5 us
    all_to_all x1, waiting for transfers between devices, body(): lax.all_to_all(outbound, 'col', split_axis=0, concat_axis=0, tiled=True)  39.6 us
    slice x4, local copies, waits for them, and re-layouts, per_group(): picked_kv[:, :, :width]  24.2 us
    concatenate x2, other arithmetic, per_group(): jnp.concatenate([grad_key.reshape(-1, block_rows, width), grad_value.resh...  23.3 us
    all_to_all x1, starting transfers between devices, body(): lax.all_to_all(outbound, 'col', split_axis=0, concat_axis=0, tiled=True)  20.7 us
  transfers between devices with their start and end apart: 5, of which 5 were waited for; matrix products, arithmetic and copies ran while one was open for 10% of the time, Pallas kernels for 0%

commit v1 on v0

v1 whole, which is shorter than its diff:
```python
import functools

import jax
import jax.numpy as jnp
from jax import lax
from jax.experimental import pallas as pl
from jax.experimental.pallas import tpu as pltpu
from jax.sharding import PartitionSpec as P

HEADS = 8
HEAD_DIM = 128
SCALE = HEAD_DIM ** (-0.5)
LANE = 128
VMEM_LIMIT = 60 * 1024 * 1024

NT = (((1,), (1,)), ((), ()))
TN = (((0,), (0,)), ((), ()))
bf16 = jnp.bfloat16
f32 = jnp.float32


def params(steps=1):
    return pltpu.CompilerParams(
        dimension_semantics=("arbitrary",) * steps, vmem_limit_bytes=VMEM_LIMIT
    )


def whole(shape):
    zeros = (0,) * len(shape)
    return pl.BlockSpec(shape, lambda *_: zeros, pipeline_mode=pl.Buffered(1))


def matmul(left, right):
    return jnp.dot(left, right, preferred_element_type=f32)


def iota(shape, axis):
    return lax.broadcasted_iota(jnp.int32, shape, axis)


def lane_rank(mask):
    rows, count = mask.shape
    before = (iota((LANE, LANE), 0) < iota((LANE, LANE), 1)).astype(f32).astype(bf16)
    carry = jnp.zeros((rows, 1), f32)
    pieces = []
    for at in range(0, count, LANE):
        part = mask[:, at : at + LANE]
        pieces.append(matmul(part.astype(bf16), before) + carry)
        carry = carry + jnp.sum(part, axis=1, keepdims=True)
    return jnp.concatenate(pieces, axis=1)


def send_slots(nodes, devices):
    rows_dev = nodes.shape[1]
    per_peer = rows_dev // devices
    owner = lax.shift_right_logical(nodes, rows_dev.bit_length() - 1)
    owners = iota((devices, rows_dev), 0)
    mask = (owner == owners).astype(f32)
    slot = mask * (lane_rank(mask) + (owners * per_peer).astype(f32))
    return jnp.sum(slot, axis=0, keepdims=True).astype(jnp.int32)


def one_hot(cond):
    return jnp.where(cond, 1.0, 0.0)


def send_kernel(self_ref, loader_ref, rows_ref, out_ref, slot_ref):
    step = pl.program_id(0)
    chunk = out_ref.shape[0]
    rows_dev = rows_ref.shape[0]

    @pl.when(step == 0)
    def _():
        nodes = loader_ref[pl.ds(self_ref[0], 1), :]
        slot_ref[...] = send_slots(nodes, loader_ref.shape[0])

    pick = one_hot(slot_ref[...] == iota((chunk, rows_dev), 0) + step * chunk)
    out_ref[...] = matmul(pick.astype(bf16), rows_ref[...]).astype(bf16)


def send_permute(self_id, loader, rows):
    rows_dev, width = rows.shape
    chunk = 256
    return pl.pallas_call(
        send_kernel,
        out_shape=jax.ShapeDtypeStruct((rows_dev, width), bf16),
        grid_spec=pltpu.PrefetchScalarGridSpec(
            num_scalar_prefetch=1,
            grid=(rows_dev // chunk,),
            in_specs=[whole(loader.shape), whole(rows.shape)],
            out_specs=pl.BlockSpec((chunk, width), lambda i, _: (i, 0)),
            scratch_shapes=[pltpu.VMEM((1, rows_dev), jnp.int32)],
        ),
        compiler_params=params(),
        name="send_permute",
    )(self_id, loader, rows)


def index_kernel(self_ref, loader_ref, to_node_ref, from_node_ref, to_row_ref, slot_ref, key_ref):
    step = pl.program_id(0)
    devices, rows_dev = loader_ref.shape
    per_peer = rows_dev // devices
    chunk = from_node_ref.shape[0]
    sources = chunk // per_peer
    me = self_ref[0]

    @pl.when(step == 0)
    def _():
        slot_ref[...] = send_slots(loader_ref[pl.ds(me, 1), :], devices)
        owner = lax.shift_right_logical(loader_ref[...], rows_dev.bit_length() - 1)
        mask = (owner == me).astype(f32)
        rank = lane_rank(mask).astype(jnp.int32)
        key_ref[...] = jnp.where(owner == me, rank, -1)

    pieces = []
    for t in range(sources):
        source = step * sources + t
        key = key_ref[pl.ds(source, 1), :]
        local = loader_ref[pl.ds(source, 1), :] - me * rows_dev
        hit = key == iota((per_peer, rows_dev), 0)
        pieces.append(jnp.sum(jnp.where(hit, local.astype(f32), 0.0), axis=1, keepdims=True))
    arriving = jnp.concatenate(pieces, axis=0).astype(jnp.int32)
    pick = one_hot(arriving == iota((chunk, rows_dev), 1))
    from_node_ref[...] = pick.astype(bf16)
    to_node_ref[...] = pick.T.astype(bf16)
    back = one_hot(slot_ref[...] == iota((chunk, rows_dev), 0) + step * chunk)
    to_row_ref[...] = back.T.astype(bf16)


def index_tables(self_id, loader, rows_dev):
    chunk = LANE
    square = jax.ShapeDtypeStruct((rows_dev, rows_dev), bf16)
    return pl.pallas_call(
        index_kernel,
        out_shape=(square, square, square),
        grid_spec=pltpu.PrefetchScalarGridSpec(
            num_scalar_prefetch=1,
            grid=(rows_dev // chunk,),
            in_specs=[whole(loader.shape)],
            out_specs=(
                pl.BlockSpec((rows_dev, chunk), lambda i, _: (0, i)),
                pl.BlockSpec((chunk, rows_dev), lambda i, _: (i, 0)),
                pl.BlockSpec((rows_dev, chunk), lambda i, _: (0, i)),
            ),
            scratch_shapes=[
                pltpu.VMEM((1, rows_dev), jnp.int32),
                pltpu.VMEM(loader.shape, jnp.int32),
            ],
        ),
        compiler_params=params(),
        name="index_tables",
    )(self_id, loader)


def permute_kernel(pick_ref, rows_ref, out_ref):
    out_ref[...] = matmul(pick_ref[...], rows_ref[...]).astype(bf16)


def permute(pick, rows):
    rows_dev, width = rows.shape
    chunk = 256
    return pl.pallas_call(
        permute_kernel,
        out_shape=jax.ShapeDtypeStruct((rows_dev, width), bf16),
        grid=(rows_dev // chunk,),
        in_specs=[pl.BlockSpec((chunk, rows_dev), lambda i: (i, 0)), whole(rows.shape)],
        out_specs=pl.BlockSpec((chunk, width), lambda i: (i, 0)),
        compiler_params=params(),
        name="permute",
    )(pick, rows)


def outbound_kernel(capacity, block, picks_ref, to_node_ref, rows_ref, *out_refs):
    for at, out_ref in enumerate(out_refs):
        for slot in range(capacity):
            start = pl.multiple_of(jnp.maximum(picks_ref[at * capacity + slot], 0) * block, block)
            picked = matmul(to_node_ref[pl.ds(start, block), :], rows_ref[...])
            out_ref[slot * block : (slot + 1) * block, :] = picked.astype(bf16)


def outbound_blocks(picks, to_node, rows, shifts, capacity, block):
    width = rows.shape[1]
    shape = (capacity * block, width)
    return pl.pallas_call(
        functools.partial(outbound_kernel, capacity, block),
        out_shape=[jax.ShapeDtypeStruct(shape, bf16)] * shifts,
        grid_spec=pltpu.PrefetchScalarGridSpec(
            num_scalar_prefetch=1,
            grid=(1,),
            in_specs=[whole(to_node.shape), whole(rows.shape)],
            out_specs=[whole(shape)] * shifts,
        ),
        compiler_params=params(),
        name="outbound",
    )(picks, to_node, rows)


def project_kernel(to_node_ref, rows_ref, wq_ref, wk_ref, wv_ref, q_ref, k_ref, v_ref):
    owned = matmul(to_node_ref[...], rows_ref[...]).astype(bf16)
    q_ref[...] = matmul(owned, wq_ref[...]).astype(bf16)
    k_ref[...] = matmul(owned, wk_ref[...]).astype(bf16)
    v_ref[...] = matmul(owned, wv_ref[...]).astype(bf16)


def project(to_node, rows, w_query, w_key, w_value, table_rows):
    rows_dev, width = rows.shape
    chunk = 256
    out_spec = pl.BlockSpec((chunk, width), lambda i: (i, 0))
    table = jax.ShapeDtypeStruct((table_rows, width), bf16)
    return pl.pallas_call(
        project_kernel,
        out_shape=(jax.ShapeDtypeStruct((rows_dev, width), bf16), table, table),
        grid=(rows_dev // chunk,),
        in_specs=[
            pl.BlockSpec((chunk, rows_dev), lambda i: (i, 0)),
            whole(rows.shape),
            whole(w_query.shape),
            whole(w_key.shape),
            whole(w_value.shape),
        ],
        out_specs=(out_spec, out_spec, out_spec),
        compiler_params=params(),
        name="project",
    )(to_node, rows, w_query, w_key, w_value)


def remote_kernel(rows_ref, wk_ref, wv_ref, k_in, v_in, k_ref, v_ref):
    k_ref[...] = matmul(rows_ref[...], wk_ref[...]).astype(bf16)
    v_ref[...] = matmul(rows_ref[...], wv_ref[...]).astype(bf16)


def remote_project(rows, w_key, w_value, k_table, v_table, first_row):
    chunk, width = rows.shape
    at = first_row // chunk
    out_spec = pl.BlockSpec((chunk, width), lambda i: (at, 0))
    any_spec = pl.BlockSpec(memory_space=pl.ANY)
    return pl.pallas_call(
        remote_kernel,
        out_shape=(
            jax.ShapeDtypeStruct(k_table.shape, bf16),
            jax.ShapeDtypeStruct(v_table.shape, bf16),
        ),
        grid=(1,),
        in_specs=[
            whole(rows.shape),
            whole(w_key.shape),
            whole(w_value.shape),
            any_spec,
            any_spec,
        ],
        out_specs=(out_spec, out_spec),
        input_output_aliases={3: 0, 4: 1},
        compiler_params=params(),
        name="remote_project",
    )(rows, w_key, w_value, k_table, v_table)


def block_starts(entries_ref, block, reads):
    at = pl.program_id(0) * reads
    return [pl.multiple_of(entries_ref[at + j] * block, block) for j in range(reads)]


def forward_kernel(
    reads,
    entries_ref,
    q_ref,
    k_ref,
    v_ref,
    gain_ref,
    from_node_ref,
    out_ref,
    mixed_ref,
    stats_ref,
    layer_ref,
):
    block, width = q_ref.shape
    step = pl.program_id(0)
    starts = block_starts(entries_ref, block, reads)
    lanes = iota((block, LANE), 1)
    stats = jnp.zeros((block, LANE), f32)
    for head in range(HEADS):
        cols = slice(head * HEAD_DIM, (head + 1) * HEAD_DIM)
        keys = jnp.concatenate([k_ref[pl.ds(at, block), cols] for at in starts], axis=0)
        vals = jnp.concatenate([v_ref[pl.ds(at, block), cols] for at in starts], axis=0)
        scores = lax.dot_general(q_ref[:, cols], keys, NT, preferred_element_type=f32) * SCALE
        top = jnp.max(scores, axis=1, keepdims=True)
        expo = jnp.exp(scores - top)
        inv = 1.0 / jnp.sum(expo, axis=1, keepdims=True)
        mixed_ref[:, cols] = matmul((expo * inv).astype(bf16), vals)
        stats = jnp.where(lanes == head, top, stats)
        stats = jnp.where(lanes == HEADS + head, inv, stats)
    mixed = mixed_ref[...]
    inv_rms = lax.rsqrt(jnp.mean(mixed * mixed, axis=1, keepdims=True) + 1e-06)
    stats_ref[...] = jnp.where(lanes == 2 * HEADS, inv_rms, stats)
    rows = pl.ds(pl.multiple_of(step * block, block), block)
    layer_ref[rows, :] = (mixed * inv_rms * gain_ref[...]).astype(bf16)

    @pl.when(step == pl.num_programs(0) - 1)
    def _():
        out_ref[...] = matmul(from_node_ref[...], layer_ref[...]).astype(bf16)


def forward(entries, queries, k_table, v_table, gain, from_node, block, reads):
    rows_dev, width = queries.shape
    return pl.pallas_call(
        functools.partial(forward_kernel, reads),
        out_shape=(
            jax.ShapeDtypeStruct((rows_dev, width), bf16),
            jax.ShapeDtypeStruct((rows_dev, width), f32),
            jax.ShapeDtypeStruct((rows_dev, LANE), f32),
        ),
        grid_spec=pltpu.PrefetchScalarGridSpec(
            num_scalar_prefetch=1,
            grid=(rows_dev // block,),
            in_specs=[
                pl.BlockSpec((block, width), lambda i, _: (i, 0)),
                whole(k_table.shape),
                whole(v_table.shape),
                whole(gain.shape),
                whole(from_node.shape),
            ],
            out_specs=(
                whole((rows_dev, width)),
                pl.BlockSpec((block, width), lambda i, _: (i, 0)),
                pl.BlockSpec((block, LANE), lambda i, _: (i, 0)),
            ),
            scratch_shapes=[pltpu.VMEM((rows_dev, width), bf16)],
        ),
        compiler_params=params(),
        name="forward",
    )(entries, queries, k_table, v_table, gain, from_node)


def backward_kernel(
    reads,
    entries_ref,
    to_node_ref,
    cot_ref,
    gain_ref,
    mixed_ref,
    stats_ref,
    q_ref,
    k_ref,
    v_ref,
    gq_ref,
    own_k_ref,
    own_v_ref,
    far_k_ref,
    far_v_ref,
    sum_k_ref,
    sum_v_ref,
):
    block, width = q_ref.shape
    step = pl.program_id(0)
    own = own_k_ref.shape[0]

    @pl.when(step == 0)
    def _():
        sum_k_ref[...] = jnp.zeros_like(sum_k_ref)
        sum_v_ref[...] = jnp.zeros_like(sum_v_ref)

    starts = block_starts(entries_ref, block, reads)
    stats = stats_ref[...]
    turned = stats.T
    inv_rms = stats[:, 2 * HEADS : 2 * HEADS + 1]
    mixed = mixed_ref[...]
    grad_in = matmul(to_node_ref[...], cot_ref[...]) * gain_ref[...]
    inner = jnp.mean(grad_in * mixed, axis=1, keepdims=True)
    grad_mix = (inv_rms * (grad_in - mixed * (inv_rms * inv_rms * inner))).astype(bf16)
    for head in range(HEADS):
        cols = slice(head * HEAD_DIM, (head + 1) * HEAD_DIM)
        keys = jnp.concatenate([k_ref[pl.ds(at, block), cols] for at in starts], axis=0)
        vals = jnp.concatenate([v_ref[pl.ds(at, block), cols] for at in starts], axis=0)
        queries = q_ref[:, cols]
        grads = grad_mix[:, cols]
        scores = lax.dot_general(keys, queries, NT, preferred_element_type=f32) * SCALE
        prob = jnp.exp(scores - turned[head : head + 1]) * turned[HEADS + head : HEADS + head + 1]
        grad_prob = lax.dot_general(vals, grads, NT, preferred_element_type=f32)
        delta = jnp.sum(prob * grad_prob, axis=0, keepdims=True)
        grad_score = (prob * (grad_prob - delta) * SCALE).astype(bf16)
        gq = lax.dot_general(grad_score, keys, TN, preferred_element_type=f32)
        gq_ref[:, cols] = gq.astype(bf16)
        key_term = matmul(grad_score, queries)
        value_term = matmul(prob.astype(bf16), grads)
        for j, at in enumerate(starts):
            part = slice(j * block, (j + 1) * block)
            sum_k_ref[pl.ds(at, block), cols] += key_term[part]
            sum_v_ref[pl.ds(at, block), cols] += value_term[part]

    @pl.when(step == pl.num_programs(0) - 1)
    def _():
        own_k_ref[...] = sum_k_ref[:own, :].astype(bf16)
        own_v_ref[...] = sum_v_ref[:own, :].astype(bf16)
        far_k_ref[...] = sum_k_ref[own:, :].astype(bf16)
        far_v_ref[...] = sum_v_ref[own:, :].astype(bf16)


def backward(
    entries, to_node, cot_rows, gain, mixed, stats, queries, k_table, v_table, block, reads
):
    rows_dev, width = queries.shape
    table_rows = k_table.shape[0]
    own = jax.ShapeDtypeStruct((rows_dev, width), bf16)
    far = jax.ShapeDtypeStruct((table_rows - rows_dev, width), bf16)
    row_spec = pl.BlockSpec((block, width), lambda i, _: (i, 0))
    return pl.pallas_call(
        functools.partial(backward_kernel, reads),
        out_shape=(own, own, own, far, far),
        grid_spec=pltpu.PrefetchScalarGridSpec(
            num_scalar_prefetch=1,
            grid=(rows_dev // block,),
            in_specs=[
                pl.BlockSpec((block, rows_dev), lambda i, _: (i, 0)),
                whole(cot_rows.shape),
                whole(gain.shape),
                row_spec,
                pl.BlockSpec((block, LANE), lambda i, _: (i, 0)),
                row_spec,
                whole(k_table.shape),
                whole(v_table.shape),
            ],
            out_specs=(
                row_spec,
                whole(own.shape),
                whole(own.shape),
                whole(far.shape),
                whole(far.shape),
            ),
            scratch_shapes=[
                pltpu.VMEM((table_rows, width), f32),
                pltpu.VMEM((table_rows, width), f32),
            ],
        ),
        compiler_params=params(),
        name="backward",
    )(entries, to_node, cot_rows, gain, mixed, stats, queries, k_table, v_table)


def far_kernel(k_ref, v_ref, wk_ref, wv_ref, *out_refs):
    chunk = out_refs[0].shape[0]
    for at, out_ref in enumerate(out_refs):
        rows = slice(at * chunk, (at + 1) * chunk)
        total = lax.dot_general(k_ref[rows, :], wk_ref[...], NT, preferred_element_type=f32)
        total += lax.dot_general(v_ref[rows, :], wv_ref[...], NT, preferred_element_type=f32)
        out_ref[...] = total.astype(bf16)


def far_project(far_k, far_v, w_key, w_value, shifts):
    rows, width = far_k.shape
    shape = (rows // shifts, width)
    return pl.pallas_call(
        far_kernel,
        out_shape=[jax.ShapeDtypeStruct(shape, bf16)] * shifts,
        grid=(1,),
        in_specs=[whole(far_k.shape), whole(far_v.shape), whole(w_key.shape), whole(w_value.shape)],
        out_specs=[whole(shape)] * shifts,
        compiler_params=params(),
        name="far_project",
    )(far_k, far_v, w_key, w_value)


def own_kernel(q_ref, k_ref, v_ref, wq_ref, wk_ref, wv_ref, out_ref):
    total = lax.dot_general(q_ref[...], wq_ref[...], NT, preferred_element_type=f32)
    total += lax.dot_general(k_ref[...], wk_ref[...], NT, preferred_element_type=f32)
    total += lax.dot_general(v_ref[...], wv_ref[...], NT, preferred_element_type=f32)
    out_ref[...] = total


def own_project(grad_q, own_k, own_v, w_query, w_key, w_value):
    rows_dev, width = grad_q.shape
    chunk = 256
    spec = pl.BlockSpec((chunk, width), lambda i: (i, 0))
    return pl.pallas_call(
        own_kernel,
        out_shape=jax.ShapeDtypeStruct((rows_dev, width), f32),
        grid=(rows_dev // chunk,),
        in_specs=[spec, spec, spec] + [whole(w_query.shape)] * 3,
        out_specs=spec,
        compiler_params=params(),
        name="own_project",
    )(grad_q, own_k, own_v, w_query, w_key, w_value)


def collect_kernel(capacity, block, picks_ref, own_ref, from_node_ref, *refs):
    returned, (out_ref, total_ref) = refs[:-2], refs[-2:]
    total_ref[...] = own_ref[...]
    for at, ref in enumerate(returned):
        for slot in range(capacity):
            pick = picks_ref[at * capacity + slot]

            @pl.when(pick >= 0)
            def _():
                rows = pl.ds(pl.multiple_of(pick * block, block), block)
                part = ref[slot * block : (slot + 1) * block, :]
                total_ref[rows, :] += part.astype(f32)

    out_ref[...] = matmul(from_node_ref[...], total_ref[...].astype(bf16)).astype(bf16)


def collect(picks, own, from_node, returned, capacity, block):
    rows_dev, width = own.shape
    return pl.pallas_call(
        functools.partial(collect_kernel, capacity, block),
        out_shape=jax.ShapeDtypeStruct((rows_dev, width), bf16),
        grid_spec=pltpu.PrefetchScalarGridSpec(
            num_scalar_prefetch=1,
            grid=(1,),
            in_specs=[whole(own.shape), whole(from_node.shape)]
            + [whole(part.shape) for part in returned],
            out_specs=whole((rows_dev, width)),
            scratch_shapes=[pltpu.VMEM((rows_dev, width), f32)],
        ),
        compiler_params=params(),
        name="collect",
    )(picks, own, from_node, *returned)


def body(
    features, cotangent, loader, w_query, w_key, w_value, norm_gain, send_blocks, tile_lists
):
    row_count = lax.axis_size("row")
    col_count = lax.axis_size("col")
    devices = row_count * col_count
    col = lax.axis_index("col")
    self_index = lax.axis_index("row") * col_count + col
    self_id = self_index.astype(jnp.int32).reshape(1)
    rows_dev, width = features.shape
    per_peer = rows_dev // devices
    block_count = tile_lists.shape[0]
    block = rows_dev // block_count
    capacity = send_blocks.shape[2]
    shifts = col_count - 1
    table_rows = rows_dev + shifts * capacity * block
    reads = 1 + tile_lists.shape[1]
    loader = loader.reshape(devices, rows_dev)
    gain = norm_gain.reshape(1, width)

    def exchange(rows):
        buffer = rows.reshape(devices, per_peer, width)
        out = lax.all_to_all(buffer, ("row", "col"), split_axis=0, concat_axis=0, tiled=True)
        return out.reshape(rows_dev, width)

    send_row = lax.dynamic_index_in_dim(send_blocks, self_index, 0, keepdims=False)
    peers = (col + 1 + jnp.arange(shifts, dtype=jnp.int32)) % col_count
    picks = send_row[peers].reshape(-1)
    source = (tile_lists - block_count) // capacity
    shift = (col - source) % col_count
    moved = block_count + (shift - 1) * capacity + (tile_lists - block_count) % capacity
    entries = jnp.where(tile_lists < block_count, tile_lists, moved)
    entries = jnp.concatenate(
        [jnp.arange(block_count, dtype=jnp.int32)[:, None], entries], axis=1
    ).reshape(-1)

    feature_rows = exchange(send_permute(self_id, loader, features))
    cot_out = send_permute(self_id, loader, cotangent)
    to_node, from_node, to_row = index_tables(self_id, loader, rows_dev)
    cot_rows = exchange(cot_out)

    outgoing = outbound_blocks(picks, to_node, feature_rows, shifts, capacity, block)
    queries, k_table, v_table = project(
        to_node, feature_rows, w_query, w_key, w_value, table_rows
    )
    for at in range(shifts):
        perm = [(c, (c + at + 1) % col_count) for c in range(col_count)]
        arrived = lax.ppermute(outgoing[at], "col", perm)
        first = rows_dev + at * capacity * block
        k_table, v_table = remote_project(arrived, w_key, w_value, k_table, v_table, first)

    layer_rows, mixed, stats = forward(
        entries, queries, k_table, v_table, gain, from_node, block, reads
    )
    layer_back = exchange(layer_rows)
    grad_q, own_k, own_v, far_k, far_v = backward(
        entries, to_node, cot_rows, gain, mixed, stats, queries, k_table, v_table, block, reads
    )
    far = far_project(far_k, far_v, w_key, w_value, shifts)
    returned = []
    for at in range(shifts):
        perm = [(c, (c - at - 1) % col_count) for c in range(col_count)]
        returned.append(lax.ppermute(far[at], "col", perm))
    own = own_project(grad_q, own_k, own_v, w_query, w_key, w_value)
    grad_back = exchange(collect(picks, own, from_node, returned, capacity, block))
    return (permute(to_row, layer_back), permute(to_row, grad_back))


def solution(mesh):
    split = P(("row", "col"), None)
    in_specs = (split, split, P(), P(), P(), P(), P(), P(), split)
    return jax.shard_map(
        body, mesh=mesh, in_specs=in_specs, out_specs=(split, split), check_vma=False
    )
```

time: 893 us -> 317 us (0.35); the launches traced: 880 us -> 317 us
  local copies, waits for them, and re-layouts: 268 us -> 10.3 us
  matrix products: 241 us -> 0 us
  Pallas kernels: 0 us -> 169 us
  other arithmetic: 140 us -> 0.05 us
  waiting for transfers between devices: 176 us -> 104 us
  between operations: 14.5 us -> 0.73 us
    dot_general x19 -> x0, matrix products: 224 us -> none  [the longest x2 71.7 us: attend(): jnp.einsum('bhqk,bqhd->bkhd', grad_score, q_heads, preferred_element_type...]
    pallas_call x0 -> x15, Pallas kernels: none -> 169 us  [the longest x1 45.2 us: backward(): pl.pallas_call(functools.partial(backward_kernel, reads), out_shape=(own,...]
    all_to_all x5 -> x4, waiting for transfers between devices: 176 us -> 85.9 us  [exchange(): lax.all_to_all(buffer, ('row', 'col'), split_axis=0, concat_axis=0, tiled...]
    gather x13 -> x1, local copies, waits for them, and re-layouts: 88.8 us -> 0.56 us  [body(): picks = send_row[peers].reshape(-1)]
    scatter-add x2 -> x0, other arithmetic: 68.5 us -> none  [per_group(): totals = totals.at[read_group.reshape(-1)].add(grad_tiles)]
    reshape x10 -> x3, local copies, waits for them, and re-layouts: 53.2 us -> 2.79 us  [the longest x1 1.57 us: body(): loader = loader.reshape(devices, rows_dev)]
    slice x8 -> x0, local copies, waits for them, and re-layouts: 42.4 us -> none  [the longest x4 24.2 us: per_group(): picked_kv[:, :, :width]]
    transpose x4 -> x0, local copies, waits for them, and re-layouts: 39.7 us -> none  [the longest x2 19.9 us: attend(): jnp.einsum('bhqk,bqhd->bkhd', grad_score, q_heads, preferred_element_type...]
  transfers between devices with their start and end apart: 5 -> 10, of which waited for: 5 -> 6; matrix products, arithmetic and copies ran while one was open for 10% -> 1% of each run, Pallas kernels for 0% -> 50%
where the time goes in v1:
time: 317 us
  Pallas kernels  169 us (53%)
  waiting for transfers between devices  104 us (33%)
  starting transfers between devices  32.9 us (10%)
  local copies, waits for them, and re-layouts  10.3 us (3%)
    all_to_all x4, waiting for transfers between devices, exchange(): lax.all_to_all(buffer, ('row', 'col'), split_axis=0, concat_axis=0, tiled...  85.9 us
    pallas_call x1, Pallas kernels, backward(): pl.pallas_call(functools.partial(backward_kernel, reads), out_shape=(own,...  45.2 us
    pallas_call x1, Pallas kernels, forward(): pl.pallas_call(functools.partial(forward_kernel, reads), out_shape=(jax.S...  33.8 us
    all_to_all x4, starting transfers between devices, exchange(): lax.all_to_all(buffer, ('row', 'col'), split_axis=0, concat_axis=0, tiled...  27.8 us
    pallas_call x1, Pallas kernels, project(): pl.pallas_call(project_kernel, out_shape=(jax.ShapeDtypeStruct((rows_dev,...  13.9 us
    pallas_call x3, Pallas kernels, remote_project(): pl.pallas_call(remote_kernel, out_shape=(jax.ShapeDtypeStruct(k_table.sha...  13.3 us
    pallas_call x2, Pallas kernels, permute(): pl.pallas_call(permute_kernel, out_shape=jax.ShapeDtypeStruct((rows_dev,...  12 us
    ppermute x3, waiting for transfers between devices, body(): returned.append(lax.ppermute(far[at], 'col', perm))  12 us
  transfers between devices with their start and end apart: 10, of which 6 were waited for; matrix products, arithmetic and copies ran while one was open for 1% of the time, Pallas kernels for 50%

profile of v1, /device:TPU:0, one launch (start us, length us, event | category | flops | bytes accessed | tf_op | source)
XLA Modules:
  0.0 316.7 jit_solution(8382209133268667928)
XLA Ops:
  2.2 5.6 %send_permute.2 = bf16[1024,1024]{1,0:T(8,128)(2,1)} custom-call(s32[1]{0:T(128)} %bitcast.self_ref, s32[32,1024]{1,0:T(8,128)} %reshape.93.loader_ref, bf16[1024,1024]{1,0:T(8,128)(2,1)} %rows_ref.2), custom_call_target="tpu_custom_call" | custom-call | tf_op jit(solution)/shard_map/send_permute/pallas_call | solution.py:84
  7.8 7.3 %all-to-all-start = ((bf16[32,32,1024]{2,1,0:T(8,128)(2,1)}), bf16[32,32,1024]{2,1,0:T(8,128)(2,1)S(1)}, u32[]{:S(2)}, u32[]{:S(2)}) async-start(bf16[32,32,1024]{2,1,0:T(8,128)(2,1)} %bitcast.18), calls=%async_computation | async-start | bytes 4194304 | tf_op jit(solution)/shard_map/all_to_all | solution.py:540
  15.1 5.7 %send_permute.3 = bf16[1024,1024]{1,0:T(8,128)(2,1)} custom-call(s32[1]{0:T(128)} %bitcast.self_ref, s32[32,1024]{1,0:T(8,128)} %reshape.93.loader_ref, bf16[1024,1024]{1,0:T(8,128)(2,1)} %rows_ref.3), custom_call_target="tpu_custom_call" | custom-call | tf_op jit(solution)/shard_map/send_permute/pallas_call | solution.py:84
  20.8 43.1 %all-to-all-done = bf16[32,32,1024]{2,1,0:T(8,128)(2,1)S(1)} async-done(((bf16[32,32,1024]{2,1,0:T(8,128)(2,1)}), bf16[32,32,1024]{2,1,0:T(8,128)(2,1)S(1)}, u32[]{:S(2)}, u32[]{:S(2)}) %all-to-all-start) | async-done | bytes 2097184 | tf_op jit(solution)/shard_map/all_to_all | solution.py:540
  65.3 4.2 %all-to-all-start.2 = ((bf16[32,32,1024]{2,1,0:T(8,128)(2,1)}), bf16[32,32,1024]{2,1,0:T(8,128)(2,1)}, u32[]{:S(2)}, u32[]{:S(2)}) async-start(bf16[32,32,1024]{2,1,0:T(8,128)(2,1)} %bitcast.17), calls=%async_computation.2 | async-start | bytes 4194304 | tf_op jit(solution)/shard_map/all_to_all | solution.py:540
  69.5 6.6 %index_tables.1 = (bf16[1024,1024]{1,0:T(8,128)(2,1)}, bf16[1024,1024]{1,0:T(8,128)(2,1)}, bf16[1024,1024]{1,0:T(8,128)(2,1)}) custom-call(s32[1]{0:T(128)} %bitcast.self_ref, s32[32,1024]{1,0:T(8,128)} %reshape.93.loader_ref), custom_call_target="tpu_custom_call" | custom-call | tf_op jit(solution)/shard_map/index_tables/pallas_call | solution.py:133
  77.6 5.7 %outbound.1 = (bf16[256,1024]{1,0:T(8,128)(2,1)}, bf16[256,1024]{1,0:T(8,128)(2,1)}, bf16[256,1024]{1,0:T(8,128)(2,1)}) custom-call(s32[6]{0:T(128)} %reshape.97.picks_ref, bf16[1024,1024]{1,0:T(8,128)(2,1)} %get-tuple-element.29.to_node_ref, bf16[1024,1024]{1,0:T(8,128)(2,1)} %bitcast.13), custom_call_target="tpu_custom_call" | custom-call | tf_op jit(solution)/shard_map/outbound/pallas_call | solution.py:184
  87.2 13.9 %project.1 = (bf16[1024,1024]{1,0:T(8,128)(2,1)}, bf16[1792,1024]{1,0:T(8,128)(2,1)}, bf16[1792,1024]{1,0:T(8,128)(2,1)}) custom-call(bf16[1024,1024]{1,0:T(8,128)(2,1)} %get-tuple-element.29.to_node_ref, bf16[1024,1024]{1,0:T(8,128)(2,1)} %bitcast.14, bf16[1024,1024]{1,0:T(8,128)(2,1)} %wq_ref.3, bf16[1024,1024]{1,0:T(8,128)(2,1)} %wk_ref.11, ...), custom_call_target="tpu_custom_call" | custom-call | tf_op jit(solution)/shard_map/project/pallas_call | solution.py:210
  101.0 2.9 collective-permute-done.2.rows_ref
  104.8 4.5 %remote_project.3 = (bf16[1792,1024]{1,0:T(8,128)(2,1)}, bf16[1792,1024]{1,0:T(8,128)(2,1)}) custom-call(bf16[256,1024]{1,0:T(8,128)(2,1)} %copy-done.6, bf16[1024,1024]{1,0:T(8,128)(2,1)} %wk_ref.11, bf16[1024,1024]{1,0:T(8,128)(2,1)} %wv_ref.11, bf16[1792,1024]{1,0:T(8,128)(2,1)} %get-tuple-element.34.k_in, ...), custom_call_target="tpu_custom_call", output_to_operand_aliasing={{0}: (3, {}), {1}: (4, {})} | custom-call | tf_op jit(solution)/shard_map/remote_project/pallas_call | solution.py:237
  110.0 4.4 %remote_project.4 = (bf16[1792,1024]{1,0:T(8,128)(2,1)}, bf16[1792,1024]{1,0:T(8,128)(2,1)}) custom-call(bf16[256,1024]{1,0:T(8,128)(2,1)} %copy-done.5, bf16[1024,1024]{1,0:T(8,128)(2,1)} %wk_ref.11, bf16[1024,1024]{1,0:T(8,128)(2,1)} %wv_ref.11, bf16[1792,1024]{1,0:T(8,128)(2,1)} %get-tuple-element.36.k_in, ...), custom_call_target="tpu_custom_call", output_to_operand_aliasing={{0}: (3, {}), {1}: (4, {})} | custom-call | tf_op jit(solution)/shard_map/remote_project/pallas_call | solution.py:237
  114.5 2.9 collective-permute-done.rows_ref
  118.2 4.4 %remote_project.5 = (bf16[1792,1024]{1,0:T(8,128)(2,1)}, bf16[1792,1024]{1,0:T(8,128)(2,1)}) custom-call(bf16[256,1024]{1,0:T(8,128)(2,1)} %copy-done.4, bf16[1024,1024]{1,0:T(8,128)(2,1)} %wk_ref.11, bf16[1024,1024]{1,0:T(8,128)(2,1)} %wv_ref.11, bf16[1792,1024]{1,0:T(8,128)(2,1)} %get-tuple-element.38.k_in, ...), custom_call_target="tpu_custom_call", output_to_operand_aliasing={{0}: (3, {}), {1}: (4, {})} | custom-call | tf_op jit(solution)/shard_map/remote_project/pallas_call | solution.py:237
  122.6 33.8 %forward.1 = (bf16[1024,1024]{1,0:T(8,128)(2,1)}, f32[1024,1024]{1,0:T(8,128)}, f32[1024,128]{1,0:T(8,128)}) custom-call(s32[32]{0:T(128)} %reshape.94.entries_ref, bf16[1024,1024]{1,0:T(8,128)(2,1)} %get-tuple-element.30.q_ref, bf16[1792,1024]{1,0:T(8,128)(2,1)} %get-tuple-element.40.k_ref, bf16[1792,1024]{1,0:T(8,128)(2,1)} %get-tuple-element.41.v_ref, ...), custom_call_target="tpu_custom_call" | custom-call | tf_op jit(solution)/shard_map/forward/pallas_call | solution.py:305
  156.4 10.3 %all-to-all-start.1 = ((bf16[32,32,1024]{2,1,0:T(8,128)(2,1)}), bf16[32,32,1024]{2,1,0:T(8,128)(2,1)S(1)}, u32[]{:S(2)}, u32[]{:S(2)}) async-start(bf16[32,32,1024]{2,1,0:T(8,128)(2,1)} %bitcast.19), calls=%async_computation.1 | async-start | bytes 4194304 | tf_op jit(solution)/shard_map/all_to_all | solution.py:540
  166.7 45.2 %backward.1 = (bf16[1024,1024]{1,0:T(8,128)(2,1)}, bf16[1024,1024]{1,0:T(8,128)(2,1)}, bf16[1024,1024]{1,0:T(8,128)(2,1)}, bf16[768,1024]{1,0:T(8,128)(2,1)}, bf16[768,1024]{1,0:T(8,128)(2,1)}) custom-call(s32[32]{0:T(128)} %reshape.94.entries_ref, bf16[1024,1024]{1,0:T(8,128)(2,1)} %get-tuple-element.29.to_node_ref, bf16[1024,1024]{1,0:T(8,128)(2,1)} %bitcast.9.cot_ref, ...), custom_call_target="tpu_custom_call" | custom-call | tf_op jit(solution)/shard_map/backward/pallas_call | solution.py:406
  212.0 7.4 %far_project.1 = (bf16[256,1024]{1,0:T(8,128)(2,1)}, bf16[256,1024]{1,0:T(8,128)(2,1)}, bf16[256,1024]{1,0:T(8,128)(2,1)}) custom-call(bf16[768,1024]{1,0:T(8,128)(2,1)} %get-tuple-element.49.k_ref, bf16[768,1024]{1,0:T(8,128)(2,1)} %get-tuple-element.50.v_ref, bf16[1024,1024]{1,0:T(8,128)(2,1)} %wk_ref.11, bf16[1024,1024]{1,0:T(8,128)(2,1)} %wv_ref.11), custom_call_target="tpu_custom_call" | custom-call | tf_op jit(solution)/shard_map/far_project/pallas_call | solution.py:451
  221.4 11.8 %own_project.1.own_ref = f32[1024,1024]{1,0:T(8,128)} custom-call(bf16[1024,1024]{1,0:T(8,128)(2,1)} %get-tuple-element.46.q_ref, bf16[1024,1024]{1,0:T(8,128)(2,1)} %get-tuple-element.47.k_ref, bf16[1024,1024]{1,0:T(8,128)(2,1)} %get-tuple-element.48.v_ref, bf16[1024,1024]{1,0:T(8,128)(2,1)} %wq_ref.3, bf16[1024,1024]{1,0:T(8,128)(2,1)} %wk_ref.11, ...), custom_call_target="tpu_custom_call" | custom-call | tf_op jit(solution)/shard_map/own_project/pallas_call | solution.py:473
  233.5 11.6 %collective-permute-done.4.refs_1_ = bf16[256,1024]{1,0:T(8,128)(2,1)S(1)} collective-permute-done((bf16[256,1024]{1,0:T(8,128)(2,1)}, bf16[256,1024]{1,0:T(8,128)(2,1)S(1)}, u32[]{:S(2)}, u32[]{:S(2)}) %collective-permute-start.4) | collective-permute-done | bytes 524320 | tf_op jit(solution)/shard_map/ppermute | solution.py:580
  246.8 7.9 %collect.1 = bf16[1024,1024]{1,0:T(8,128)(2,1)} custom-call(s32[6]{0:T(128)} %reshape.97.picks_ref, f32[1024,1024]{1,0:T(8,128)} %own_project.1.own_ref, bf16[1024,1024]{1,0:T(8,128)(2,1)} %get-tuple-element.42.from_node_ref, bf16[256,1024]{1,0:T(8,128)(2,1)} %copy-done.7, bf16[256,1024]{1,0:T(8,128)(2,1)} %copy-done.8, bf16[256,1024]{1,0:T(8,128)(2,1)} %copy-done.9), custom_call_target="tpu_custom_call" | custom-call | tf_op jit(solution)/shard_map/collect/pallas_call | solution.py:502
  256.0 5.9 %all-to-all-start.3 = ((bf16[32,32,1024]{2,1,0:T(8,128)(2,1)}), bf16[32,32,1024]{2,1,0:T(8,128)(2,1)}, u32[]{:S(2)}, u32[]{:S(2)}) async-start(bf16[32,32,1024]{2,1,0:T(8,128)(2,1)} %bitcast.16), calls=%async_computation.3 | async-start | bytes 4194304 | tf_op jit(solution)/shard_map/all_to_all | solution.py:540
  262.0 6.0 %permute.2 = bf16[1024,1024]{1,0:T(8,128)(2,1)} custom-call(bf16[1024,1024]{1,0:T(8,128)(2,1)} %get-tuple-element.28.pick_ref, bf16[1024,1024]{1,0:T(8,128)(2,1)} %bitcast.15), custom_call_target="tpu_custom_call" | custom-call | tf_op jit(solution)/shard_map/permute/pallas_call | solution.py:162
  268.0 42.7 %all-to-all-done.3 = bf16[32,32,1024]{2,1,0:T(8,128)(2,1)} async-done(((bf16[32,32,1024]{2,1,0:T(8,128)(2,1)}), bf16[32,32,1024]{2,1,0:T(8,128)(2,1)}, u32[]{:S(2)}, u32[]{:S(2)}) %all-to-all-start.3) | async-done | bytes 2097184 | tf_op jit(solution)/shard_map/all_to_all | solution.py:540
  310.7 6.0 %permute.3 = bf16[1024,1024]{1,0:T(8,128)(2,1)} custom-call(bf16[1024,1024]{1,0:T(8,128)(2,1)} %get-tuple-element.28.pick_ref, bf16[1024,1024]{1,0:T(8,128)(2,1)} %bitcast.11.rows_ref), custom_call_target="tpu_custom_call" | custom-call | tf_op jit(solution)/shard_map/permute/pallas_call | solution.py:162
  (46 shorter events, 15.9 us)
Async XLA Ops:
  0.6 75.5 %copy-start = (s32[32,4,2]{0,2,1:T(2,128)S(1)}, s32[32,4,2]{0,2,1:T(2,128)}, u32[]{:S(2)}) copy-start(s32[32,4,2]{0,2,1:T(2,128)} %param.16) | copy-start | bytes 3076
  7.8 56.1 %all-to-all-start = ((bf16[32,32,1024]{2,1,0:T(8,128)(2,1)}), bf16[32,32,1024]{2,1,0:T(8,128)(2,1)S(1)}, u32[]{:S(2)}, u32[]{:S(2)}) async-start(bf16[32,32,1024]{2,1,0:T(8,128)(2,1)} %bitcast.18), calls=%async_computation | async-start | bytes 4194304 | tf_op jit(solution)/shard_map/all_to_all | solution.py:540
  63.9 1.4 copy-start.2
  65.3 91.1 %all-to-all-start.2 = ((bf16[32,32,1024]{2,1,0:T(8,128)(2,1)}), bf16[32,32,1024]{2,1,0:T(8,128)(2,1)}, u32[]{:S(2)}, u32[]{:S(2)}) async-start(bf16[32,32,1024]{2,1,0:T(8,128)(2,1)} %bitcast.17), calls=%async_computation.2 | async-start | bytes 4194304 | tf_op jit(solution)/shard_map/all_to_all | solution.py:540
  77.6 8.9 %copy-start.10 = (s32[8,3]{0,1:T(4,128)S(1)}, s32[8,3]{0,1:T(4,128)}, u32[]{:S(2)}) copy-start(s32[8,3]{0,1:T(4,128)} %param.17) | copy-start | bytes 292
  83.3 20.7 %collective-permute-start.2 = (bf16[256,1024]{1,0:T(8,128)(2,1)}, bf16[256,1024]{1,0:T(8,128)(2,1)S(1)}, u32[]{:S(2)}, u32[]{:S(2)}) collective-permute-start(bf16[256,1024]{1,0:T(8,128)(2,1)} %get-tuple-element.33), channel_id=1, source_target_pairs={{0,1},{1,2},{2,3},{3,0},{4,5},{5,6},{6,7},{7,4},{8,9},{9,10},{10,1... | collective-permute-start | bytes 1572872 | tf_op jit(solution)/shard_map/ppermute | solution.py:565
  83.5 25.8 %collective-permute-start.1 = (bf16[256,1024]{1,0:T(8,128)(2,1)}, bf16[256,1024]{1,0:T(8,128)(2,1)S(1)}, u32[]{:S(2)}, u32[]{:S(2)}) collective-permute-start(bf16[256,1024]{1,0:T(8,128)(2,1)} %get-tuple-element.32), channel_id=1, source_target_pairs={{0,2},{1,3},{2,0},{3,1},{4,6},{5,7},{6,4},{7,5},{8,10},{9,11},{10,... | collective-permute-start | bytes 1572872 | tf_op jit(solution)/shard_map/ppermute | solution.py:565
  85.1 32.3 %collective-permute-start = (bf16[256,1024]{1,0:T(8,128)(2,1)}, bf16[256,1024]{1,0:T(8,128)(2,1)S(1)}, u32[]{:S(2)}, u32[]{:S(2)}) collective-permute-start(bf16[256,1024]{1,0:T(8,128)(2,1)} %get-tuple-element.31), channel_id=1, source_target_pairs={{0,3},{1,0},{2,1},{3,2},{4,7},{5,4},{6,5},{7,6},{8,11},{9,8},{10,9... | collective-permute-start | bytes 1572872 | tf_op jit(solution)/shard_map/ppermute | solution.py:565
  104.0 0.8 copy-start.6
  109.2 0.8 copy-start.5
  117.4 0.8 copy-start.4
  156.4 98.3 %all-to-all-start.1 = ((bf16[32,32,1024]{2,1,0:T(8,128)(2,1)}), bf16[32,32,1024]{2,1,0:T(8,128)(2,1)S(1)}, u32[]{:S(2)}, u32[]{:S(2)}) async-start(bf16[32,32,1024]{2,1,0:T(8,128)(2,1)} %bitcast.19), calls=%async_computation.1 | async-start | bytes 4194304 | tf_op jit(solution)/shard_map/all_to_all | solution.py:540
  219.4 14.2 %collective-permute-start.3 = (bf16[256,1024]{1,0:T(8,128)(2,1)}, bf16[256,1024]{1,0:T(8,128)(2,1)S(1)}, u32[]{:S(2)}, u32[]{:S(2)}) collective-permute-start(bf16[256,1024]{1,0:T(8,128)(2,1)} %get-tuple-element.51), channel_id=1, source_target_pairs={{0,3},{1,0},{2,1},{3,2},{4,7},{5,4},{6,5},{7,6},{8,11},{9,8},{10,9... | collective-permute-start | bytes 1572872 | tf_op jit(solution)/shard_map/ppermute | solution.py:580
  220.9 24.3 %collective-permute-start.4 = (bf16[256,1024]{1,0:T(8,128)(2,1)}, bf16[256,1024]{1,0:T(8,128)(2,1)S(1)}, u32[]{:S(2)}, u32[]{:S(2)}) collective-permute-start(bf16[256,1024]{1,0:T(8,128)(2,1)} %get-tuple-element.52), channel_id=1, source_target_pairs={{0,2},{1,3},{2,0},{3,1},{4,6},{5,7},{6,4},{7,5},{8,10},{9,11},{10,... | collective-permute-start | bytes 1572872 | tf_op jit(solution)/shard_map/ppermute | solution.py:580
  221.2 23.9 %collective-permute-start.5 = (bf16[256,1024]{1,0:T(8,128)(2,1)}, bf16[256,1024]{1,0:T(8,128)(2,1)S(1)}, u32[]{:S(2)}, u32[]{:S(2)}) collective-permute-start(bf16[256,1024]{1,0:T(8,128)(2,1)} %get-tuple-element.53), channel_id=1, source_target_pairs={{0,1},{1,2},{2,3},{3,0},{4,5},{5,6},{6,7},{7,4},{8,9},{9,10},{10,1... | collective-permute-start | bytes 1572872 | tf_op jit(solution)/shard_map/ppermute | solution.py:580
  233.5 11.7 %copy-start.7 = (bf16[256,1024]{1,0:T(8,128)(2,1)}, bf16[256,1024]{1,0:T(8,128)(2,1)S(1)}, u32[]{:S(2)}) copy-start(bf16[256,1024]{1,0:T(8,128)(2,1)S(1)} %collective-permute-done.3.refs_0_) | copy-start | bytes 1572868
  245.2 0.8 copy-start.8
  246.0 0.8 copy-start.9
  254.7 1.3 copy-start.3
  256.0 54.7 %all-to-all-start.3 = ((bf16[32,32,1024]{2,1,0:T(8,128)(2,1)}), bf16[32,32,1024]{2,1,0:T(8,128)(2,1)}, u32[]{:S(2)}, u32[]{:S(2)}) async-start(bf16[32,32,1024]{2,1,0:T(8,128)(2,1)} %bitcast.16), calls=%async_computation.3 | async-start | bytes 4194304 | tf_op jit(solution)/shard_map/all_to_all | solution.py:540
  310.7 6.0 %copy-start.1 = (s32[32,4,2]{0,2,1:T(2,128)S(1)}, s32[32,4,2]{0,2,1:T(2,128)}, u32[]{:S(2)}) copy-start(s32[32,4,2]{0,2,1:T(2,128)} %param.16) | copy-start | bytes 3076

commit v2 on v1

--- a/solution.py
+++ b/solution.py
@@ -1,4 +1,5 @@
 import functools
+import math
 
 import jax
 import jax.numpy as jnp
@@ -11,7 +12,10 @@
 HEAD_DIM = 128
 SCALE = HEAD_DIM ** (-0.5)
 LANE = 128
-VMEM_LIMIT = 60 * 1024 * 1024
+EXPO = SCALE * math.log2(math.e)
+MIB = 1024 * 1024
+SUBLANES = 8
+CHUNK = 64
 
 NT = (((1,), (1,)), ((), ()))
 TN = (((0,), (0,)), ((), ()))
@@ -19,10 +23,12 @@
 f32 = jnp.float32
 
 
-def params(steps=1):
-    return pltpu.CompilerParams(
-        dimension_semantics=("arbitrary",) * steps, vmem_limit_bytes=VMEM_LIMIT
-    )
+def hbm(shape, dtype):
+    return pltpu.HBM(shape, jnp.dtype(dtype))
+
+
+def params(mib):
+    return pltpu.CompilerParams(dimension_semantics=("arbitrary",), vmem_limit_bytes=mib * MIB)
 
 
 def whole(shape):
@@ -83,7 +89,7 @@
     chunk = 256
     return pl.pallas_call(
         send_kernel,
-        out_shape=jax.ShapeDtypeStruct((rows_dev, width), bf16),
+        out_shape=hbm((rows_dev, width), bf16),
         grid_spec=pltpu.PrefetchScalarGridSpec(
             num_scalar_prefetch=1,
             grid=(rows_dev // chunk,),
@@ -91,7 +97,7 @@
             out_specs=pl.BlockSpec((chunk, width), lambda i, _: (i, 0)),
             scratch_shapes=[pltpu.VMEM((1, rows_dev), jnp.int32)],
         ),
-        compiler_params=params(),
+        compiler_params=params(10),
         name="send_permute",
     )(self_id, loader, rows)
 
@@ -129,7 +135,7 @@
 
 def index_tables(self_id, loader, rows_dev):
     chunk = LANE
-    square = jax.ShapeDtypeStruct((rows_dev, rows_dev), bf16)
+    square = hbm((rows_dev, rows_dev), bf16)
     return pl.pallas_call(
         index_kernel,
         out_shape=(square, square, square),
@@ -147,7 +153,7 @@
                 pltpu.VMEM(loader.shape, jnp.int32),
             ],
         ),
-        compiler_params=params(),
+        compiler_params=params(10),
         name="index_tables",
     )(self_id, loader)
 
@@ -161,11 +167,11 @@
     chunk = 256
     return pl.pallas_call(
         permute_kernel,
-        out_shape=jax.ShapeDtypeStruct((rows_dev, width), bf16),
+        out_shape=hbm((rows_dev, width), bf16),
         grid=(rows_dev // chunk,),
         in_specs=[pl.BlockSpec((chunk, rows_dev), lambda i: (i, 0)), whole(rows.shape)],
         out_specs=pl.BlockSpec((chunk, width), lambda i: (i, 0)),
-        compiler_params=params(),
+        compiler_params=params(8),
         name="permute",
     )(pick, rows)
 
@@ -183,14 +189,14 @@
     shape = (capacity * block, width)
     return pl.pallas_call(
         functools.partial(outbound_kernel, capacity, block),
-        out_shape=[jax.ShapeDtypeStruct(shape, bf16)] * shifts,
+        out_shape=[hbm(shape, bf16)] * shifts,
         grid_spec=pltpu.PrefetchScalarGridSpec(
             num_scalar_prefetch=1,
             grid=(1,),
             in_specs=[whole(to_node.shape), whole(rows.shape)],
             out_specs=[whole(shape)] * shifts,
         ),
-        compiler_params=params(),
+        compiler_params=params(12),
         name="outbound",
     )(picks, to_node, rows)
 
@@ -206,10 +212,10 @@
     rows_dev, width = rows.shape
     chunk = 256
     out_spec = pl.BlockSpec((chunk, width), lambda i: (i, 0))
-    table = jax.ShapeDtypeStruct((table_rows, width), bf16)
+    table = hbm((table_rows, width), bf16)
     return pl.pallas_call(
         project_kernel,
-        out_shape=(jax.ShapeDtypeStruct((rows_dev, width), bf16), table, table),
+        out_shape=(hbm((rows_dev, width), bf16), table, table),
         grid=(rows_dev // chunk,),
         in_specs=[
             pl.BlockSpec((chunk, rows_dev), lambda i: (i, 0)),
@@ -219,7 +225,7 @@
             whole(w_value.shape),
         ],
         out_specs=(out_spec, out_spec, out_spec),
-        compiler_params=params(),
+        compiler_params=params(20),
         name="project",
     )(to_node, rows, w_query, w_key, w_value)
 
@@ -237,8 +243,8 @@
     return pl.pallas_call(
         remote_kernel,
         out_shape=(
-            jax.ShapeDtypeStruct(k_table.shape, bf16),
-            jax.ShapeDtypeStruct(v_table.shape, bf16),
+            hbm(k_table.shape, bf16),
+            hbm(v_table.shape, bf16),
         ),
         grid=(1,),
         in_specs=[
@@ -250,9 +256,20 @@
         ],
         out_specs=(out_spec, out_spec),
         input_output_aliases={3: 0, 4: 1},
-        compiler_params=params(),
+        compiler_params=params(12),
         name="remote_project",
     )(rows, w_key, w_value, k_table, v_table)
+
+
+def split_dot(left, right):
+    return lax.dot_general(left, right, NT, preferred_element_type=f32)
+
+
+def fold(rows, op):
+    total = rows[:SUBLANES]
+    for at in range(SUBLANES, rows.shape[0], SUBLANES):
+        total = op(total, rows[at : at + SUBLANES])
+    return total
 
 
 def block_starts(entries_ref, block, reads):
@@ -272,26 +289,42 @@
     mixed_ref,
     stats_ref,
     layer_ref,
+    score_ref,
+    prob_ref,
 ):
     block, width = q_ref.shape
     step = pl.program_id(0)
+    keys = reads * block
     starts = block_starts(entries_ref, block, reads)
-    lanes = iota((block, LANE), 1)
-    stats = jnp.zeros((block, LANE), f32)
     for head in range(HEADS):
         cols = slice(head * HEAD_DIM, (head + 1) * HEAD_DIM)
-        keys = jnp.concatenate([k_ref[pl.ds(at, block), cols] for at in starts], axis=0)
+        for j, at in enumerate(starts):
+            part = slice(j * block, (j + 1) * block)
+            score_ref[head, part, :] = split_dot(k_ref[pl.ds(at, block), cols], q_ref[:, cols])
+    for head in range(HEADS):
+        top = fold(score_ref[head, :CHUNK, :], jnp.maximum)
+        for at in range(CHUNK, keys, CHUNK):
+            top = jnp.maximum(top, fold(score_ref[head, at : at + CHUNK, :], jnp.maximum))
+        top = jnp.max(top, axis=0, keepdims=True)
+        total = jnp.zeros((SUBLANES, block), f32)
+        for at in range(0, keys, CHUNK):
+            expo = jnp.exp2((score_ref[head, at : at + CHUNK, :] - top) * EXPO)
+            score_ref[head, at : at + CHUNK, :] = expo
+            total = total + fold(expo, jnp.add)
+        inv = 1.0 / jnp.sum(total, axis=0, keepdims=True)
+        for at in range(0, keys, CHUNK):
+            part = slice(at, at + CHUNK)
+            prob_ref[head, part, :] = (score_ref[head, part, :] * inv).astype(bf16)
+        stats_ref[2 * head : 2 * head + 1, :] = top
+        stats_ref[2 * head + 1 : 2 * head + 2, :] = inv
+    for head in range(HEADS):
+        cols = slice(head * HEAD_DIM, (head + 1) * HEAD_DIM)
         vals = jnp.concatenate([v_ref[pl.ds(at, block), cols] for at in starts], axis=0)
-        scores = lax.dot_general(q_ref[:, cols], keys, NT, preferred_element_type=f32) * SCALE
-        top = jnp.max(scores, axis=1, keepdims=True)
-        expo = jnp.exp(scores - top)
-        inv = 1.0 / jnp.sum(expo, axis=1, keepdims=True)
-        mixed_ref[:, cols] = matmul((expo * inv).astype(bf16), vals)
-        stats = jnp.where(lanes == head, top, stats)
-        stats = jnp.where(lanes == HEADS + head, inv, stats)
+        mixed_ref[:, cols] = lax.dot_general(
+            prob_ref[head], vals, TN, preferred_element_type=f32
+        )
     mixed = mixed_ref[...]
     inv_rms = lax.rsqrt(jnp.mean(mixed * mixed, axis=1, keepdims=True) + 1e-06)
-    stats_ref[...] = jnp.where(lanes == 2 * HEADS, inv_rms, stats)
     rows = pl.ds(pl.multiple_of(step * block, block), block)
     layer_ref[rows, :] = (mixed * inv_rms * gain_ref[...]).astype(bf16)
 
@@ -305,9 +338,9 @@
     return pl.pallas_call(
         functools.partial(forward_kernel, reads),
         out_shape=(
-            jax.ShapeDtypeStruct((rows_dev, width), bf16),
-            jax.ShapeDtypeStruct((rows_dev, width), f32),
-            jax.ShapeDtypeStruct((rows_dev, LANE), f32),
+            hbm((rows_dev, width), bf16),
+            hbm((rows_dev, width), f32),
+            hbm((rows_dev // block * 2 * HEADS, block), f32),
         ),
         grid_spec=pltpu.PrefetchScalarGridSpec(
             num_scalar_prefetch=1,
@@ -322,11 +355,15 @@
             out_specs=(
                 whole((rows_dev, width)),
                 pl.BlockSpec((block, width), lambda i, _: (i, 0)),
-                pl.BlockSpec((block, LANE), lambda i, _: (i, 0)),
+                pl.BlockSpec((2 * HEADS, block), lambda i, _: (i, 0)),
             ),
-            scratch_shapes=[pltpu.VMEM((rows_dev, width), bf16)],
-        ),
-        compiler_params=params(),
+            scratch_shapes=[
+                pltpu.VMEM((rows_dev, width), bf16),
+                pltpu.VMEM((HEADS, reads * block, block), f32),
+                pltpu.VMEM((HEADS, reads * block, block), bf16),
+            ],
+        ),
+        compiler_params=params(32),
         name="forward",
     )(entries, queries, k_table, v_table, gain, from_node)
 
@@ -349,10 +386,16 @@
     far_v_ref,
     sum_k_ref,
     sum_v_ref,
+    prob_ref,
+    grad_prob_ref,
+    prob_half_ref,
+    grad_score_ref,
+    grad_mix_ref,
 ):
     block, width = q_ref.shape
     step = pl.program_id(0)
     own = own_k_ref.shape[0]
+    keys = reads * block
 
     @pl.when(step == 0)
     def _():
@@ -360,32 +403,44 @@
         sum_v_ref[...] = jnp.zeros_like(sum_v_ref)
 
     starts = block_starts(entries_ref, block, reads)
-    stats = stats_ref[...]
-    turned = stats.T
-    inv_rms = stats[:, 2 * HEADS : 2 * HEADS + 1]
     mixed = mixed_ref[...]
+    inv_rms = lax.rsqrt(jnp.mean(mixed * mixed, axis=1, keepdims=True) + 1e-06)
     grad_in = matmul(to_node_ref[...], cot_ref[...]) * gain_ref[...]
     inner = jnp.mean(grad_in * mixed, axis=1, keepdims=True)
-    grad_mix = (inv_rms * (grad_in - mixed * (inv_rms * inv_rms * inner))).astype(bf16)
+    grad_mix = inv_rms * (grad_in - mixed * (inv_rms * inv_rms * inner))
+    grad_mix_ref[...] = grad_mix.astype(bf16)
     for head in range(HEADS):
         cols = slice(head * HEAD_DIM, (head + 1) * HEAD_DIM)
-        keys = jnp.concatenate([k_ref[pl.ds(at, block), cols] for at in starts], axis=0)
-        vals = jnp.concatenate([v_ref[pl.ds(at, block), cols] for at in starts], axis=0)
-        queries = q_ref[:, cols]
-        grads = grad_mix[:, cols]
-        scores = lax.dot_general(keys, queries, NT, preferred_element_type=f32) * SCALE
-        prob = jnp.exp(scores - turned[head : head + 1]) * turned[HEADS + head : HEADS + head + 1]
-        grad_prob = lax.dot_general(vals, grads, NT, preferred_element_type=f32)
-        delta = jnp.sum(prob * grad_prob, axis=0, keepdims=True)
-        grad_score = (prob * (grad_prob - delta) * SCALE).astype(bf16)
-        gq = lax.dot_general(grad_score, keys, TN, preferred_element_type=f32)
-        gq_ref[:, cols] = gq.astype(bf16)
-        key_term = matmul(grad_score, queries)
-        value_term = matmul(prob.astype(bf16), grads)
         for j, at in enumerate(starts):
             part = slice(j * block, (j + 1) * block)
-            sum_k_ref[pl.ds(at, block), cols] += key_term[part]
-            sum_v_ref[pl.ds(at, block), cols] += value_term[part]
+            rows = pl.ds(at, block)
+            prob_ref[head, part, :] = split_dot(k_ref[rows, cols], q_ref[:, cols])
+            grad_prob_ref[head, part, :] = split_dot(v_ref[rows, cols], grad_mix_ref[:, cols])
+    for head in range(HEADS):
+        top = stats_ref[2 * head : 2 * head + 1, :]
+        inv = stats_ref[2 * head + 1 : 2 * head + 2, :]
+        total = jnp.zeros((SUBLANES, block), f32)
+        for at in range(0, keys, CHUNK):
+            part = slice(at, at + CHUNK)
+            prob = jnp.exp2((prob_ref[head, part, :] - top) * EXPO) * inv
+            prob_ref[head, part, :] = prob
+            prob_half_ref[head, part, :] = prob.astype(bf16)
+            total = total + fold(prob * grad_prob_ref[head, part, :], jnp.add)
+        delta = jnp.sum(total, axis=0, keepdims=True)
+        for at in range(0, keys, CHUNK):
+            part = slice(at, at + CHUNK)
+            centred = (grad_prob_ref[head, part, :] - delta) * SCALE
+            grad_score_ref[head, part, :] = (prob_ref[head, part, :] * centred).astype(bf16)
+    for head in range(HEADS):
+        cols = slice(head * HEAD_DIM, (head + 1) * HEAD_DIM)
+        key_rows = jnp.concatenate([k_ref[pl.ds(at, block), cols] for at in starts], axis=0)
+        gq = lax.dot_general(grad_score_ref[head], key_rows, TN, preferred_element_type=f32)
+        gq_ref[:, cols] = gq.astype(bf16)
+        for j, at in enumerate(starts):
+            part = slice(j * block, (j + 1) * block)
+            rows = pl.ds(at, block)
+            sum_k_ref[rows, cols] += matmul(grad_score_ref[head, part, :], q_ref[:, cols])
+            sum_v_ref[rows, cols] += matmul(prob_half_ref[head, part, :], grad_mix_ref[:, cols])
 
     @pl.when(step == pl.num_programs(0) - 1)
     def _():
@@ -400,8 +455,8 @@
 ):
     rows_dev, width = queries.shape
     table_rows = k_table.shape[0]
-    own = jax.ShapeDtypeStruct((rows_dev, width), bf16)
-    far = jax.ShapeDtypeStruct((table_rows - rows_dev, width), bf16)
+    own = hbm((rows_dev, width), bf16)
+    far = hbm((table_rows - rows_dev, width), bf16)
     row_spec = pl.BlockSpec((block, width), lambda i, _: (i, 0))
     return pl.pallas_call(
         functools.partial(backward_kernel, reads),
@@ -414,7 +469,7 @@
                 whole(cot_rows.shape),
                 whole(gain.shape),
                 row_spec,
-                pl.BlockSpec((block, LANE), lambda i, _: (i, 0)),
+                pl.BlockSpec((2 * HEADS, block), lambda i, _: (i, 0)),
                 row_spec,
                 whole(k_table.shape),
                 whole(v_table.shape),
@@ -429,9 +484,14 @@
             scratch_shapes=[
                 pltpu.VMEM((table_rows, width), f32),
                 pltpu.VMEM((table_rows, width), f32),
+                pltpu.VMEM((HEADS, reads * block, block), f32),
+                pltpu.VMEM((HEADS, reads * block, block), f32),
+                pltpu.VMEM((HEADS, reads * block, block), bf16),
+                pltpu.VMEM((HEADS, reads * block, block), bf16),
+                pltpu.VMEM((block, width), bf16),
             ],
         ),
-        compiler_params=params(),
+        compiler_params=params(60),
         name="backward",
     )(entries, to_node, cot_rows, gain, mixed, stats, queries, k_table, v_table)
 
@@ -450,11 +510,11 @@
     shape = (rows // shifts, width)
     return pl.pallas_call(
         far_kernel,
-        out_shape=[jax.ShapeDtypeStruct(shape, bf16)] * shifts,
+        out_shape=[hbm(shape, bf16)] * shifts,
         grid=(1,),
         in_specs=[whole(far_k.shape), whole(far_v.shape), whole(w_key.shape), whole(w_value.shape)],
         out_specs=[whole(shape)] * shifts,
-        compiler_params=params(),
+        compiler_params=params(14),
         name="far_project",
     )(far_k, far_v, w_key, w_value)
 
@@ -472,11 +532,11 @@
     spec = pl.BlockSpec((chunk, width), lambda i: (i, 0))
     return pl.pallas_call(
         own_kernel,
-        out_shape=jax.ShapeDtypeStruct((rows_dev, width), f32),
+        out_shape=hbm((rows_dev, width), f32),
         grid=(rows_dev // chunk,),
         in_specs=[spec, spec, spec] + [whole(w_query.shape)] * 3,
         out_specs=spec,
-        compiler_params=params(),
+        compiler_params=params(16),
         name="own_project",
     )(grad_q, own_k, own_v, w_query, w_key, w_value)
 
@@ -501,7 +561,7 @@
     rows_dev, width = own.shape
     return pl.pallas_call(
         functools.partial(collect_kernel, capacity, block),
-        out_shape=jax.ShapeDtypeStruct((rows_dev, width), bf16),
+        out_shape=hbm((rows_dev, width), bf16),
         grid_spec=pltpu.PrefetchScalarGridSpec(
             num_scalar_prefetch=1,
             grid=(1,),
@@ -510,7 +570,7 @@
             out_specs=whole((rows_dev, width)),
             scratch_shapes=[pltpu.VMEM((rows_dev, width), f32)],
         ),
-        compiler_params=params(),
+        compiler_params=params(20),
         name="collect",
     )(picks, own, from_node, *returned)
 
@@ -554,9 +614,13 @@
     feature_rows = exchange(send_permute(self_id, loader, features))
     cot_out = send_permute(self_id, loader, cotangent)
     to_node, from_node, to_row = index_tables(self_id, loader, rows_dev)
+    feature_rows, cot_out, to_node, from_node, to_row, picks, entries = lax.optimization_barrier(
+        (feature_rows, cot_out, to_node, from_node, to_row, picks, entries)
+    )
+    outgoing = outbound_blocks(picks, to_node, feature_rows, shifts, capacity, block)
+    cot_out, outgoing = lax.optimization_barrier((cot_out, outgoing))
     cot_rows = exchange(cot_out)
 
-    outgoing = outbound_blocks(picks, to_node, feature_rows, shifts, capacity, block)
     queries, k_table, v_table = project(
         to_node, feature_rows, w_query, w_key, w_value, table_rows
     )

time: 317 us -> 289 us (0.912)
  Pallas kernels: 169 us -> 119 us
  local copies, waits for them, and re-layouts: 10.3 us -> 24.4 us
  waiting for transfers between devices: 104 us -> 114 us
    pallas_call x11, Pallas kernels: 103 us -> 67.3 us  [the longest x1 17.8 us: forward(): pl.pallas_call(functools.partial(forward_kernel, reads), out_shape=(hbm((...]
    unnamed x22 -> x58, local copies, waits for them, and re-layouts: 6.65 us -> 22.4 us
    ppermute x3, waiting for transfers between devices: 5.89 us -> 21.5 us  [body(): arrived = lax.ppermute(outgoing[at], 'col', perm)]
    pallas_call x1, Pallas kernels: 45.2 us -> 36 us  [backward(): pl.pallas_call(functools.partial(backward_kernel, reads), out_shape=(own,...]
    all_to_all x4, waiting for transfers between devices: 85.9 us -> 79.6 us  [exchange(): lax.all_to_all(buffer, ('row', 'col'), split_axis=0, concat_axis=0, tiled...]
    pallas_call x1, Pallas kernels: 7.93 us -> 4.76 us  [collect(): pl.pallas_call(functools.partial(collect_kernel, capacity, block), out_sh...]
  transfers between devices with their start and end apart: 10 -> 10, of which waited for: 6 -> 6; matrix products, arithmetic and copies ran while one was open for 1% -> 0% of each run, Pallas kernels for 50% -> 36%
where the time goes in v2:
time: 289 us; the launch traced here: 288 us
  Pallas kernels  119 us (41%)
  waiting for transfers between devices  114 us (39%)
  starting transfers between devices  30.8 us (11%)
  local copies, waits for them, and re-layouts  24.4 us (8%)
    all_to_all x4, waiting for transfers between devices, exchange(): lax.all_to_all(buffer, ('row', 'col'), split_axis=0, concat_axis=0, tiled...  79.6 us
    pallas_call x1, Pallas kernels, backward(): pl.pallas_call(functools.partial(backward_kernel, reads), out_shape=(own,...  36 us
    all_to_all x4, starting transfers between devices, exchange(): lax.all_to_all(buffer, ('row', 'col'), split_axis=0, concat_axis=0, tiled...  25.8 us
    unnamed x58, local copies, waits for them, and re-layouts  22.4 us
    ppermute x3, waiting for transfers between devices, body(): arrived = lax.ppermute(outgoing[at], 'col', perm)  21.5 us
    pallas_call x1, Pallas kernels, forward(): pl.pallas_call(functools.partial(forward_kernel, reads), out_shape=(hbm((...  17.8 us
    ppermute x3, waiting for transfers between devices, body(): returned.append(lax.ppermute(far[at], 'col', perm))  12.5 us
    pallas_call x1, Pallas kernels, project(): pl.pallas_call(project_kernel, out_shape=(hbm((rows_dev, width), bf16), t...  12 us
  transfers between devices with their start and end apart: 10, of which 6 were waited for; matrix products, arithmetic and copies ran while one was open for 0% of the time, Pallas kernels for 36%

profile of v2, /device:TPU:0, one launch (start us, length us, event | category | flops | bytes accessed | tf_op | source)
XLA Modules:
  0.0 288.2 jit_solution(6285883475376614512)
XLA Ops:
  3.2 4.0 %send_permute.2 = bf16[1024,1024]{1,0:T(8,128)(2,1)} custom-call(s32[1]{0:T(128)} %bitcast.self_ref, s32[32,1024]{1,0:T(8,128)S(1)} %reshape.93.loader_ref, bf16[1024,1024]{1,0:T(8,128)(2,1)S(1)} %copy-done.17), custom_call_target="tpu_custom_call" | custom-call | tf_op jit(solution)/shard_map/send_permute/pallas_call | solution.py:90
  7.2 7.4 %all-to-all-start = ((bf16[32,32,1024]{2,1,0:T(8,128)(2,1)}), bf16[32,32,1024]{2,1,0:T(8,128)(2,1)}, u32[]{:S(2)}, u32[]{:S(2)}) async-start(bf16[32,32,1024]{2,1,0:T(8,128)(2,1)} %bitcast.17), calls=%async_computation | async-start | bytes 4194304 | tf_op jit(solution)/shard_map/all_to_all | solution.py:600
  14.7 5.7 %index_tables.1 = (bf16[1024,1024]{1,0:T(8,128)(2,1)}, bf16[1024,1024]{1,0:T(8,128)(2,1)}, bf16[1024,1024]{1,0:T(8,128)(2,1)}) custom-call(s32[1]{0:T(128)} %bitcast.self_ref, s32[32,1024]{1,0:T(8,128)S(1)} %reshape.93.loader_ref), custom_call_target="tpu_custom_call" | custom-call | tf_op jit(solution)/shard_map/index_tables/pallas_call | solution.py:139
  21.9 4.0 %send_permute.3 = bf16[1024,1024]{1,0:T(8,128)(2,1)} custom-call(s32[1]{0:T(128)} %bitcast.self_ref, s32[32,1024]{1,0:T(8,128)S(1)} %reshape.93.loader_ref, bf16[1024,1024]{1,0:T(8,128)(2,1)S(1)} %copy-done.18), custom_call_target="tpu_custom_call" | custom-call | tf_op jit(solution)/shard_map/send_permute/pallas_call | solution.py:90
  27.1 36.3 %all-to-all-done = bf16[32,32,1024]{2,1,0:T(8,128)(2,1)} async-done(((bf16[32,32,1024]{2,1,0:T(8,128)(2,1)}), bf16[32,32,1024]{2,1,0:T(8,128)(2,1)}, u32[]{:S(2)}, u32[]{:S(2)}) %all-to-all-start) | async-done | bytes 2097184 | tf_op jit(solution)/shard_map/all_to_all | solution.py:600
  63.4 4.8 %outbound.1 = (bf16[256,1024]{1,0:T(8,128)(2,1)}, bf16[256,1024]{1,0:T(8,128)(2,1)}, bf16[256,1024]{1,0:T(8,128)(2,1)}) custom-call(s32[6]{0:T(128)S(1)} %reshape.96.picks_ref, bf16[1024,1024]{1,0:T(8,128)(2,1)S(1)} %copy-done.8, bf16[1024,1024]{1,0:T(8,128)(2,1)} %bitcast.2.rows_ref), custom_call_target="tpu_custom_call" | custom-call | tf_op jit(solution)/shard_map/outbound/pallas_call | solution.py:190
  68.2 4.2 %all-to-all-start.2 = ((bf16[32,32,1024]{2,1,0:T(8,128)(2,1)}), bf16[32,32,1024]{2,1,0:T(8,128)(2,1)}, u32[]{:S(2)}, u32[]{:S(2)}) async-start(bf16[32,32,1024]{2,1,0:T(8,128)(2,1)} %bitcast.16), calls=%async_computation.2 | async-start | bytes 4194304 | tf_op jit(solution)/shard_map/all_to_all | solution.py:600
  80.5 12.0 %project.1 = (bf16[1024,1024]{1,0:T(8,128)(2,1)}, bf16[1792,1024]{1,0:T(8,128)(2,1)}, bf16[1792,1024]{1,0:T(8,128)(2,1)}) custom-call(bf16[1024,1024]{1,0:T(8,128)(2,1)S(1)} %copy-done.9, bf16[1024,1024]{1,0:T(8,128)(2,1)} %bitcast.2.rows_ref, bf16[1024,1024]{1,0:T(8,128)(2,1)S(1)} %copy-done.15, bf16[1024,1024]{1,0:T(8,128)(2,1)S(1)} %copy-done.4, ...), custom_call_target="tpu_custom_call" | custom-call | tf_op jit(solution)/shard_map/project/pallas_call | solution.py:216
  92.4 12.5 %collective-permute-done.2.rows_ref = bf16[256,1024]{1,0:T(8,128)(2,1)S(1)} collective-permute-done((bf16[256,1024]{1,0:T(8,128)(2,1)}, bf16[256,1024]{1,0:T(8,128)(2,1)S(1)}, u32[]{:S(2)}, u32[]{:S(2)}) %collective-permute-start.2) | collective-permute-done | bytes 524320 | tf_op jit(solution)/shard_map/ppermute | solution.py:629
  104.9 2.1 remote_project.3
  109.0 9.0 %collective-permute-done.rows_ref = bf16[256,1024]{1,0:T(8,128)(2,1)S(1)} collective-permute-done((bf16[256,1024]{1,0:T(8,128)(2,1)S(1)}, bf16[256,1024]{1,0:T(8,128)(2,1)S(1)}, u32[]{:S(2)}, u32[]{:S(2)}) %collective-permute-start) | collective-permute-done | bytes 524320 | tf_op jit(solution)/shard_map/ppermute | solution.py:629
  118.0 2.1 remote_project.5
  124.7 17.8 %forward.1 = (bf16[1024,1024]{1,0:T(8,128)(2,1)}, f32[1024,1024]{1,0:T(8,128)}, f32[128,128]{1,0:T(8,128)}) custom-call(s32[32]{0:T(128)S(1)} %reshape.97.entries_ref, bf16[1024,1024]{1,0:T(8,128)(2,1)S(1)} %copy-done.14, bf16[1792,1024]{1,0:T(8,128)(2,1)S(1)} %copy-done.2, bf16[1792,1024]{1,0:T(8,128)(2,1)S(1)} %copy-done.3, f32[1,1024]{1,0:T(1,128)S(1)} %bitcast.14, ...), custom_call_target="tpu_custom_call" | custom-call | tf_op jit(solution)/shard_map/forward/pallas_call | solution.py:338
  142.5 8.4 %all-to-all-start.1 = ((bf16[32,32,1024]{2,1,0:T(8,128)(2,1)}), bf16[32,32,1024]{2,1,0:T(8,128)(2,1)}, u32[]{:S(2)}, u32[]{:S(2)}) async-start(bf16[32,32,1024]{2,1,0:T(8,128)(2,1)} %bitcast.18), calls=%async_computation.1 | async-start | bytes 4194304 | tf_op jit(solution)/shard_map/all_to_all | solution.py:600
  150.9 36.0 %backward.1 = (bf16[1024,1024]{1,0:T(8,128)(2,1)}, bf16[1024,1024]{1,0:T(8,128)(2,1)}, bf16[1024,1024]{1,0:T(8,128)(2,1)}, bf16[768,1024]{1,0:T(8,128)(2,1)}, bf16[768,1024]{1,0:T(8,128)(2,1)}) custom-call(s32[32]{0:T(128)} %copy-done.25, bf16[1024,1024]{1,0:T(8,128)(2,1)} %get-tuple-element.44.to_node_ref, bf16[1024,1024]{1,0:T(8,128)(2,1)} %bitcast.9.cot_ref, ...), custom_call_target="tpu_custom_call" | custom-call | tf_op jit(solution)/shard_map/backward/pallas_call | solution.py:461
  191.3 4.3 %far_project.1 = (bf16[256,1024]{1,0:T(8,128)(2,1)}, bf16[256,1024]{1,0:T(8,128)(2,1)}, bf16[256,1024]{1,0:T(8,128)(2,1)}) custom-call(bf16[768,1024]{1,0:T(8,128)(2,1)S(1)} %copy-done.22, bf16[768,1024]{1,0:T(8,128)(2,1)S(1)} %copy-done.23, bf16[1024,1024]{1,0:T(8,128)(2,1)S(1)} %copy-done.4, bf16[1024,1024]{1,0:T(8,128)(2,1)S(1)} %copy-done.6), custom_call_target="tpu_custom_call" | custom-call | tf_op jit(solution)/shard_map/far_project/pallas_call | solution.py:511
  200.6 8.3 %own_project.1.own_ref = f32[1024,1024]{1,0:T(8,128)} custom-call(bf16[1024,1024]{1,0:T(8,128)(2,1)S(1)} %copy-done.19, bf16[1024,1024]{1,0:T(8,128)(2,1)S(1)} %copy-done.20, bf16[1024,1024]{1,0:T(8,128)(2,1)S(1)} %copy-done.21, bf16[1024,1024]{1,0:T(8,128)(2,1)S(1)} %copy-done.16, bf16[1024,1024]{1,0:T(8,128)(2,1)S(1)} %copy-done.4, ...), custom_call_target="tpu_custom_call" | custom-call | tf_op jit(solution)/shard_map/own_project/pallas_call | solution.py:533
  209.5 11.9 %collective-permute-done.4.refs_1_ = bf16[256,1024]{1,0:T(8,128)(2,1)S(1)} collective-permute-done((bf16[256,1024]{1,0:T(8,128)(2,1)}, bf16[256,1024]{1,0:T(8,128)(2,1)S(1)}, u32[]{:S(2)}, u32[]{:S(2)}) %collective-permute-start.4) | collective-permute-done | bytes 524320 | tf_op jit(solution)/shard_map/ppermute | solution.py:644
  221.4 2.2 copy-done.10
  223.6 4.8 %collect.1 = bf16[1024,1024]{1,0:T(8,128)(2,1)} custom-call(s32[6]{0:T(128)S(1)} %reshape.96.picks_ref, f32[1024,1024]{1,0:T(8,128)S(1)} %copy-done.10, bf16[1024,1024]{1,0:T(8,128)(2,1)S(1)} %copy-done.13, bf16[256,1024]{1,0:T(8,128)(2,1)S(1)} %collective-permute-done.3.refs_0_, bf16[256,1024]{1,0:T(8,128)(2,1)S(1)} %collective-permute-done.4.refs_1_, ...), custom_call_target="tpu_custom_call" | custom-call | tf_op jit(solution)/shard_map/collect/pallas_call | solution.py:562
  228.3 5.7 %all-to-all-start.3 = ((bf16[32,32,1024]{2,1,0:T(8,128)(2,1)}), bf16[32,32,1024]{2,1,0:T(8,128)(2,1)}, u32[]{:S(2)}, u32[]{:S(2)}) async-start(bf16[32,32,1024]{2,1,0:T(8,128)(2,1)} %bitcast.15), calls=%async_computation.3 | async-start | bytes 4194304 | tf_op jit(solution)/shard_map/all_to_all | solution.py:600
  234.0 5.4 %permute.2 = bf16[1024,1024]{1,0:T(8,128)(2,1)} custom-call(bf16[1024,1024]{1,0:T(8,128)(2,1)S(1)} %copy-done.11, bf16[1024,1024]{1,0:T(8,128)(2,1)} %bitcast.7.rows_ref), custom_call_target="tpu_custom_call" | custom-call | tf_op jit(solution)/shard_map/permute/pallas_call | solution.py:168
  239.4 43.4 %all-to-all-done.3 = bf16[32,32,1024]{2,1,0:T(8,128)(2,1)} async-done(((bf16[32,32,1024]{2,1,0:T(8,128)(2,1)}), bf16[32,32,1024]{2,1,0:T(8,128)(2,1)}, u32[]{:S(2)}, u32[]{:S(2)}) %all-to-all-start.3) | async-done | bytes 2097184 | tf_op jit(solution)/shard_map/all_to_all | solution.py:600
  282.8 5.4 %permute.3 = bf16[1024,1024]{1,0:T(8,128)(2,1)} custom-call(bf16[1024,1024]{1,0:T(8,128)(2,1)S(1)} %copy-done.11, bf16[1024,1024]{1,0:T(8,128)(2,1)} %bitcast.11.rows_ref), custom_call_target="tpu_custom_call" | custom-call | tf_op jit(solution)/shard_map/permute/pallas_call | solution.py:168
  (82 shorter events, 29.9 us)
Async XLA Ops:
  0.6 25.3 %copy-start = (s32[32,4,2]{0,2,1:T(2,128)S(1)}, s32[32,4,2]{0,2,1:T(2,128)}, u32[]{:S(2)}) copy-start(s32[32,4,2]{0,2,1:T(2,128)} %param.16) | copy-start | bytes 3076
  7.2 56.2 %all-to-all-start = ((bf16[32,32,1024]{2,1,0:T(8,128)(2,1)}), bf16[32,32,1024]{2,1,0:T(8,128)(2,1)}, u32[]{:S(2)}, u32[]{:S(2)}) async-start(bf16[32,32,1024]{2,1,0:T(8,128)(2,1)} %bitcast.17), calls=%async_computation | async-start | bytes 4194304 | tf_op jit(solution)/shard_map/all_to_all | solution.py:600
  21.9 5.0 %copy-start.26 = (s32[8,3]{0,1:T(4,128)S(1)}, s32[8,3]{0,1:T(4,128)}, u32[]{:S(2)}) copy-start(s32[8,3]{0,1:T(4,128)} %param.17) | copy-start | bytes 292
  21.9 41.5 %copy-start.8 = (bf16[1024,1024]{1,0:T(8,128)(2,1)S(1)}, bf16[1024,1024]{1,0:T(8,128)(2,1)}, u32[]{:S(2)}) copy-start(bf16[1024,1024]{1,0:T(8,128)(2,1)} %get-tuple-element.44.to_node_ref) | copy-start | bytes 6291460
  27.1 92.9 %copy-start.25 = (s32[32]{0:T(128)}, s32[32]{0:T(128)S(1)}, u32[]{:S(2)}) copy-start(s32[32]{0:T(128)S(1)} %reshape.97.entries_ref) | copy-start | bytes 388
  68.2 4.5 %copy-start.28 = (bf16[256,1024]{1,0:T(8,128)(2,1)S(1)}, bf16[256,1024]{1,0:T(8,128)(2,1)}, u32[]{:S(2)}) copy-start(bf16[256,1024]{1,0:T(8,128)(2,1)} %get-tuple-element.53) | copy-start | bytes 1572868
  68.2 6.1 %copy-start.27 = (bf16[256,1024]{1,0:T(8,128)(2,1)S(1)}, bf16[256,1024]{1,0:T(8,128)(2,1)}, u32[]{:S(2)}) copy-start(bf16[256,1024]{1,0:T(8,128)(2,1)} %get-tuple-element.52) | copy-start | bytes 1572868
  68.2 7.5 %copy-start.4 = (bf16[1024,1024]{1,0:T(8,128)(2,1)S(1)}, bf16[1024,1024]{1,0:T(8,128)(2,1)}, u32[]{:S(2)}) copy-start(bf16[1024,1024]{1,0:T(8,128)(2,1)} %wk_ref.11) | copy-start | bytes 6291460
  68.2 74.2 %all-to-all-start.2 = ((bf16[32,32,1024]{2,1,0:T(8,128)(2,1)}), bf16[32,32,1024]{2,1,0:T(8,128)(2,1)}, u32[]{:S(2)}, u32[]{:S(2)}) async-start(bf16[32,32,1024]{2,1,0:T(8,128)(2,1)} %bitcast.16), calls=%async_computation.2 | async-start | bytes 4194304 | tf_op jit(solution)/shard_map/all_to_all | solution.py:600
  72.5 32.4 %collective-permute-start.2 = (bf16[256,1024]{1,0:T(8,128)(2,1)}, bf16[256,1024]{1,0:T(8,128)(2,1)S(1)}, u32[]{:S(2)}, u32[]{:S(2)}) collective-permute-start(bf16[256,1024]{1,0:T(8,128)(2,1)} %get-tuple-element.54), channel_id=1, source_target_pairs={{0,1},{1,2},{2,3},{3,0},{4,5},{5,6},{6,7},{7,4},{8,9},{9,10},{10,1... | collective-permute-start | bytes 1572872 | tf_op jit(solution)/shard_map/ppermute | solution.py:629
  72.7 34.3 %collective-permute-start.1 = (bf16[256,1024]{1,0:T(8,128)(2,1)S(1)}, bf16[256,1024]{1,0:T(8,128)(2,1)S(1)}, u32[]{:S(2)}, u32[]{:S(2)}) collective-permute-start(bf16[256,1024]{1,0:T(8,128)(2,1)S(1)} %copy-done.28), channel_id=1, source_target_pairs={{0,2},{1,3},{2,0},{3,1},{4,6},{5,7},{6,4},{7,5},{8,10},{9,11},{10,... | collective-permute-start | bytes 1572872 | tf_op jit(solution)/shard_map/ppermute | solution.py:629
  74.4 43.7 %collective-permute-start = (bf16[256,1024]{1,0:T(8,128)(2,1)S(1)}, bf16[256,1024]{1,0:T(8,128)(2,1)S(1)}, u32[]{:S(2)}, u32[]{:S(2)}) collective-permute-start(bf16[256,1024]{1,0:T(8,128)(2,1)S(1)} %copy-done.27), channel_id=1, source_target_pairs={{0,3},{1,0},{2,1},{3,2},{4,7},{5,4},{6,5},{7,6},{8,11},{9,8},{10,9... | collective-permute-start | bytes 1572872 | tf_op jit(solution)/shard_map/ppermute | solution.py:629
  118.0 2.6 copy-start.24
  142.5 85.9 %all-to-all-start.1 = ((bf16[32,32,1024]{2,1,0:T(8,128)(2,1)}), bf16[32,32,1024]{2,1,0:T(8,128)(2,1)}, u32[]{:S(2)}, u32[]{:S(2)}) async-start(bf16[32,32,1024]{2,1,0:T(8,128)(2,1)} %bitcast.18), calls=%async_computation.1 | async-start | bytes 4194304 | tf_op jit(solution)/shard_map/all_to_all | solution.py:600
  191.3 6.0 %copy-start.7 = (bf16[1024,1024]{1,0:T(8,128)(2,1)S(1)}, bf16[1024,1024]{1,0:T(8,128)(2,1)}, u32[]{:S(2)}) copy-start(bf16[1024,1024]{1,0:T(8,128)(2,1)} %wv_ref.11) | copy-start | bytes 6291460
  191.3 6.0 %copy-start.16 = (bf16[1024,1024]{1,0:T(8,128)(2,1)S(1)}, bf16[1024,1024]{1,0:T(8,128)(2,1)}, u32[]{:S(2)}) copy-start(bf16[1024,1024]{1,0:T(8,128)(2,1)} %wq_ref.3) | copy-start | bytes 6291460
  191.3 6.0 %copy-start.19 = (bf16[1024,1024]{1,0:T(8,128)(2,1)S(1)}, bf16[1024,1024]{1,0:T(8,128)(2,1)}, u32[]{:S(2)}) copy-start(bf16[1024,1024]{1,0:T(8,128)(2,1)} %get-tuple-element.68.q_ref) | copy-start | bytes 6291460
  195.6 13.9 %collective-permute-start.3 = (bf16[256,1024]{1,0:T(8,128)(2,1)}, bf16[256,1024]{1,0:T(8,128)(2,1)S(1)}, u32[]{:S(2)}, u32[]{:S(2)}) collective-permute-start(bf16[256,1024]{1,0:T(8,128)(2,1)} %get-tuple-element.73), channel_id=1, source_target_pairs={{0,3},{1,0},{2,1},{3,2},{4,7},{5,4},{6,5},{7,6},{8,11},{9,8},{10,9... | collective-permute-start | bytes 1572872 | tf_op jit(solution)/shard_map/ppermute | solution.py:644
  196.9 24.5 %collective-permute-start.4 = (bf16[256,1024]{1,0:T(8,128)(2,1)}, bf16[256,1024]{1,0:T(8,128)(2,1)S(1)}, u32[]{:S(2)}, u32[]{:S(2)}) collective-permute-start(bf16[256,1024]{1,0:T(8,128)(2,1)} %get-tuple-element.74), channel_id=1, source_target_pairs={{0,2},{1,3},{2,0},{3,1},{4,6},{5,7},{6,4},{7,5},{8,10},{9,11},{10,... | collective-permute-start | bytes 1572872 | tf_op jit(solution)/shard_map/ppermute | solution.py:644
  197.2 24.2 %collective-permute-start.5 = (bf16[256,1024]{1,0:T(8,128)(2,1)}, bf16[256,1024]{1,0:T(8,128)(2,1)S(1)}, u32[]{:S(2)}, u32[]{:S(2)}) collective-permute-start(bf16[256,1024]{1,0:T(8,128)(2,1)} %get-tuple-element.75), channel_id=1, source_target_pairs={{0,1},{1,2},{2,3},{3,0},{4,5},{5,6},{6,7},{7,4},{8,9},{9,10},{10,1... | collective-permute-start | bytes 1572872 | tf_op jit(solution)/shard_map/ppermute | solution.py:644
  200.6 20.8 %copy-start.13 = (bf16[1024,1024]{1,0:T(8,128)(2,1)S(1)}, bf16[1024,1024]{1,0:T(8,128)(2,1)}, u32[]{:S(2)}) copy-start(bf16[1024,1024]{1,0:T(8,128)(2,1)} %get-tuple-element.63.from_node_ref) | copy-start | bytes 6291460
  228.3 5.7 %copy-start.11 = (bf16[1024,1024]{1,0:T(8,128)(2,1)S(1)}, bf16[1024,1024]{1,0:T(8,128)(2,1)}, u32[]{:S(2)}) copy-start(bf16[1024,1024]{1,0:T(8,128)(2,1)} %get-tuple-element.42.pick_ref) | copy-start | bytes 6291460
  228.3 54.4 %all-to-all-start.3 = ((bf16[32,32,1024]{2,1,0:T(8,128)(2,1)}), bf16[32,32,1024]{2,1,0:T(8,128)(2,1)}, u32[]{:S(2)}, u32[]{:S(2)}) async-start(bf16[32,32,1024]{2,1,0:T(8,128)(2,1)} %bitcast.15), calls=%async_computation.3 | async-start | bytes 4194304 | tf_op jit(solution)/shard_map/all_to_all | solution.py:600
  282.8 5.4 %copy-start.1 = (s32[32,4,2]{0,2,1:T(2,128)S(1)}, s32[32,4,2]{0,2,1:T(2,128)}, u32[]{:S(2)}) copy-start(s32[32,4,2]{0,2,1:T(2,128)} %param.16) | copy-start | bytes 3076
  (15 other events, 26.5 us)

commit v3 on v2

--- a/solution.py
+++ b/solution.py
@@ -25,6 +25,10 @@
 
 def hbm(shape, dtype):
     return pltpu.HBM(shape, jnp.dtype(dtype))
+
+
+def pin(value):
+    return pltpu.with_memory_space_constraint(value, pltpu.HBM)
 
 
 def params(mib):
@@ -70,9 +74,10 @@
     return jnp.where(cond, 1.0, 0.0)
 
 
-def send_kernel(self_ref, loader_ref, rows_ref, out_ref, slot_ref):
+def send_kernel(self_ref, loader_ref, rows_ref, *refs):
+    out_refs, slot_ref = refs[:-1], refs[-1]
     step = pl.program_id(0)
-    chunk = out_ref.shape[0]
+    chunk, piece = out_refs[0].shape
     rows_dev = rows_ref.shape[0]
 
     @pl.when(step == 0)
@@ -81,25 +86,28 @@
         slot_ref[...] = send_slots(nodes, loader_ref.shape[0])
 
     pick = one_hot(slot_ref[...] == iota((chunk, rows_dev), 0) + step * chunk)
-    out_ref[...] = matmul(pick.astype(bf16), rows_ref[...]).astype(bf16)
-
-
-def send_permute(self_id, loader, rows):
+    moved = matmul(pick.astype(bf16), rows_ref[...]).astype(bf16)
+    for at, out_ref in enumerate(out_refs):
+        out_ref[...] = moved[:, at * piece : (at + 1) * piece]
+
+
+def send_permute(self_id, loader, rows, pieces):
     rows_dev, width = rows.shape
     chunk = 256
+    piece = width // pieces
     return pl.pallas_call(
         send_kernel,
-        out_shape=hbm((rows_dev, width), bf16),
+        out_shape=[hbm((rows_dev, piece), bf16)] * pieces,
         grid_spec=pltpu.PrefetchScalarGridSpec(
             num_scalar_prefetch=1,
             grid=(rows_dev // chunk,),
             in_specs=[whole(loader.shape), whole(rows.shape)],
-            out_specs=pl.BlockSpec((chunk, width), lambda i, _: (i, 0)),
+            out_specs=[pl.BlockSpec((chunk, piece), lambda i, _: (i, 0))] * pieces,
             scratch_shapes=[pltpu.VMEM((1, rows_dev), jnp.int32)],
         ),
         compiler_params=params(10),
         name="send_permute",
-    )(self_id, loader, rows)
+    )(self_id, loader, pin(rows))
 
 
 def index_kernel(self_ref, loader_ref, to_node_ref, from_node_ref, to_row_ref, slot_ref, key_ref):
@@ -158,22 +166,29 @@
     )(self_id, loader)
 
 
-def permute_kernel(pick_ref, rows_ref, out_ref):
-    out_ref[...] = matmul(pick_ref[...], rows_ref[...]).astype(bf16)
-
-
-def permute(pick, rows):
-    rows_dev, width = rows.shape
+def permute_kernel(pick_ref, rows_ref, *refs):
+    refs[-1][...] = matmul(pick_ref[...], rows_ref[...]).astype(bf16)
+
+
+def permute(pick, pieces):
+    rows_dev, piece = pieces[0].shape
     chunk = 256
-    return pl.pallas_call(
-        permute_kernel,
-        out_shape=hbm((rows_dev, width), bf16),
-        grid=(rows_dev // chunk,),
-        in_specs=[pl.BlockSpec((chunk, rows_dev), lambda i: (i, 0)), whole(rows.shape)],
-        out_specs=pl.BlockSpec((chunk, width), lambda i: (i, 0)),
-        compiler_params=params(8),
-        name="permute",
-    )(pick, rows)
+    out = []
+    for at, rows in enumerate(pieces):
+        out = [
+            pl.pallas_call(
+                permute_kernel,
+                out_shape=hbm((rows_dev, piece * len(pieces)), bf16),
+                grid=(rows_dev // chunk,),
+                in_specs=[pl.BlockSpec((chunk, rows_dev), lambda i: (i, 0)), whole(rows.shape)]
+                + [pl.BlockSpec(memory_space=pl.ANY)] * len(out),
+                out_specs=pl.BlockSpec((chunk, piece), lambda i, at=at: (i, at)),
+                input_output_aliases={2: 0} if out else {},
+                compiler_params=params(8),
+                name="permute",
+            )(pin(pick), pin(rows), *out)
+        ]
+    return out[0]
 
 
 def outbound_kernel(capacity, block, picks_ref, to_node_ref, rows_ref, *out_refs):
@@ -198,18 +213,21 @@
         ),
         compiler_params=params(12),
         name="outbound",
-    )(picks, to_node, rows)
-
-
-def project_kernel(to_node_ref, rows_ref, wq_ref, wk_ref, wv_ref, q_ref, k_ref, v_ref):
-    owned = matmul(to_node_ref[...], rows_ref[...]).astype(bf16)
+    )(picks, pin(to_node), pin(rows))
+
+
+def project_kernel(to_node_ref, wq_ref, wk_ref, wv_ref, *refs):
+    row_refs, (q_ref, k_ref, v_ref) = refs[:-3], refs[-3:]
+    owned = [matmul(to_node_ref[...], ref[...]).astype(bf16) for ref in row_refs]
+    owned = jnp.concatenate(owned, axis=1)
     q_ref[...] = matmul(owned, wq_ref[...]).astype(bf16)
     k_ref[...] = matmul(owned, wk_ref[...]).astype(bf16)
     v_ref[...] = matmul(owned, wv_ref[...]).astype(bf16)
 
 
 def project(to_node, rows, w_query, w_key, w_value, table_rows):
-    rows_dev, width = rows.shape
+    rows_dev = to_node.shape[0]
+    width = w_query.shape[1]
     chunk = 256
     out_spec = pl.BlockSpec((chunk, width), lambda i: (i, 0))
     table = hbm((table_rows, width), bf16)
@@ -219,46 +237,42 @@
         grid=(rows_dev // chunk,),
         in_specs=[
             pl.BlockSpec((chunk, rows_dev), lambda i: (i, 0)),
-            whole(rows.shape),
             whole(w_query.shape),
             whole(w_key.shape),
             whole(w_value.shape),
-        ],
+        ]
+        + [whole(piece.shape) for piece in rows],
         out_specs=(out_spec, out_spec, out_spec),
         compiler_params=params(20),
         name="project",
-    )(to_node, rows, w_query, w_key, w_value)
-
-
-def remote_kernel(rows_ref, wk_ref, wv_ref, k_in, v_in, k_ref, v_ref):
-    k_ref[...] = matmul(rows_ref[...], wk_ref[...]).astype(bf16)
-    v_ref[...] = matmul(rows_ref[...], wv_ref[...]).astype(bf16)
+    )(pin(to_node), w_query, w_key, w_value, *map(pin, rows))
+
+
+def remote_kernel(wk_ref, wv_ref, k_in, v_in, *refs):
+    row_refs, (k_ref, v_ref) = refs[:-2], refs[-2:]
+    rows = jnp.concatenate([ref[...] for ref in row_refs], axis=1)
+    k_ref[...] = matmul(rows, wk_ref[...]).astype(bf16)
+    v_ref[...] = matmul(rows, wv_ref[...]).astype(bf16)
 
 
 def remote_project(rows, w_key, w_value, k_table, v_table, first_row):
-    chunk, width = rows.shape
+    chunk = rows[0].shape[0]
+    width = w_key.shape[1]
     at = first_row // chunk
     out_spec = pl.BlockSpec((chunk, width), lambda i: (at, 0))
     any_spec = pl.BlockSpec(memory_space=pl.ANY)
+    table = hbm(k_table.shape, bf16)
     return pl.pallas_call(
         remote_kernel,
-        out_shape=(
-            hbm(k_table.shape, bf16),
-            hbm(v_table.shape, bf16),
-        ),
+        out_shape=(table, table),
         grid=(1,),
-        in_specs=[
-            whole(rows.shape),
-            whole(w_key.shape),
-            whole(w_value.shape),
-            any_spec,
-            any_spec,
-        ],
+        in_specs=[whole(w_key.shape), whole(w_value.shape), any_spec, any_spec]
+        + [whole(piece.shape) for piece in rows],
         out_specs=(out_spec, out_spec),
-        input_output_aliases={3: 0, 4: 1},
+        input_output_aliases={2: 0, 3: 1},
         compiler_params=params(12),
         name="remote_project",
-    )(rows, w_key, w_value, k_table, v_table)
+    )(w_key, w_value, k_table, v_table, *rows)
 
 
 def split_dot(left, right):
@@ -272,35 +286,35 @@
     return total
 
 
-def block_starts(entries_ref, block, reads):
-    at = pl.program_id(0) * reads
-    return [pl.multiple_of(entries_ref[at + j] * block, block) for j in range(reads)]
+def entry_specs(block, width, reads):
+    return [
+        pl.BlockSpec((block, width), lambda i, entries, j=j: (entries[i * reads + j], 0))
+        for j in range(reads)
+    ]
+
+
+def entry_args(table, reads):
+    return [pin(table)] * reads
 
 
 def forward_kernel(
     reads,
     entries_ref,
     q_ref,
-    k_ref,
-    v_ref,
     gain_ref,
     from_node_ref,
-    out_ref,
-    mixed_ref,
-    stats_ref,
-    layer_ref,
-    score_ref,
-    prob_ref,
+    *refs,
 ):
+    k_refs, v_refs = refs[:reads], refs[reads : 2 * reads]
+    out_ref, mixed_ref, stats_ref, layer_ref, score_ref, prob_ref = refs[2 * reads :]
     block, width = q_ref.shape
     step = pl.program_id(0)
     keys = reads * block
-    starts = block_starts(entries_ref, block, reads)
     for head in range(HEADS):
         cols = slice(head * HEAD_DIM, (head + 1) * HEAD_DIM)
-        for j, at in enumerate(starts):
+        for j, k_ref in enumerate(k_refs):
             part = slice(j * block, (j + 1) * block)
-            score_ref[head, part, :] = split_dot(k_ref[pl.ds(at, block), cols], q_ref[:, cols])
+            score_ref[head, part, :] = split_dot(k_ref[:, cols], q_ref[:, cols])
     for head in range(HEADS):
         top = fold(score_ref[head, :CHUNK, :], jnp.maximum)
         for at in range(CHUNK, keys, CHUNK):
@@ -319,7 +333,7 @@
         stats_ref[2 * head + 1 : 2 * head + 2, :] = inv
     for head in range(HEADS):
         cols = slice(head * HEAD_DIM, (head + 1) * HEAD_DIM)
-        vals = jnp.concatenate([v_ref[pl.ds(at, block), cols] for at in starts], axis=0)
+        vals = jnp.concatenate([ref[:, cols] for ref in v_refs], axis=0)
         mixed_ref[:, cols] = lax.dot_general(
             prob_ref[head], vals, TN, preferred_element_type=f32
         )
@@ -347,11 +361,10 @@
             grid=(rows_dev // block,),
             in_specs=[
                 pl.BlockSpec((block, width), lambda i, _: (i, 0)),
-                whole(k_table.shape),
-                whole(v_table.shape),
                 whole(gain.shape),
                 whole(from_node.shape),
-            ],
+            ]
+            + entry_specs(block, width, reads) * 2,
             out_specs=(
                 whole((rows_dev, width)),
                 pl.BlockSpec((block, width), lambda i, _: (i, 0)),
@@ -365,7 +378,14 @@
         ),
         compiler_params=params(32),
         name="forward",
-    )(entries, queries, k_table, v_table, gain, from_node)
+    )(
+        entries,
+        pin(queries),
+        gain,
+        from_node,
+        *entry_args(k_table, reads),
+        *entry_args(v_table, reads),
+    )
 
 
 def backward_kernel(
@@ -377,21 +397,12 @@
     mixed_ref,
     stats_ref,
     q_ref,
-    k_ref,
-    v_ref,
-    gq_ref,
-    own_k_ref,
-    own_v_ref,
-    far_k_ref,
-    far_v_ref,
-    sum_k_ref,
-    sum_v_ref,
-    prob_ref,
-    grad_prob_ref,
-    prob_half_ref,
-    grad_score_ref,
-    grad_mix_ref,
+    *refs,
 ):
+    k_refs, v_refs = refs[:reads], refs[reads : 2 * reads]
+    gq_ref, own_k_ref, own_v_ref, far_k_ref, far_v_ref = refs[2 * reads : 2 * reads + 5]
+    sum_k_ref, sum_v_ref, prob_ref, grad_prob_ref = refs[2 * reads + 5 : 2 * reads + 9]
+    prob_half_ref, grad_score_ref, grad_mix_ref = refs[2 * reads + 9 :]
     block, width = q_ref.shape
     step = pl.program_id(0)
     own = own_k_ref.shape[0]
@@ -402,7 +413,8 @@
         sum_k_ref[...] = jnp.zeros_like(sum_k_ref)
         sum_v_ref[...] = jnp.zeros_like(sum_v_ref)
 
-    starts = block_starts(entries_ref, block, reads)
+    entries = [entries_ref[step * reads + j] * block for j in range(reads)]
+    starts = [pl.multiple_of(at, block) for at in entries]
     mixed = mixed_ref[...]
     inv_rms = lax.rsqrt(jnp.mean(mixed * mixed, axis=1, keepdims=True) + 1e-06)
     grad_in = matmul(to_node_ref[...], cot_ref[...]) * gain_ref[...]
@@ -411,11 +423,10 @@
     grad_mix_ref[...] = grad_mix.astype(bf16)
     for head in range(HEADS):
         cols = slice(head * HEAD_DIM, (head + 1) * HEAD_DIM)
-        for j, at in enumerate(starts):
+        for j, (k_ref, v_ref) in enumerate(zip(k_refs, v_refs)):
             part = slice(j * block, (j + 1) * block)
-            rows = pl.ds(at, block)
-            prob_ref[head, part, :] = split_dot(k_ref[rows, cols], q_ref[:, cols])
-            grad_prob_ref[head, part, :] = split_dot(v_ref[rows, cols], grad_mix_ref[:, cols])
+            prob_ref[head, part, :] = split_dot(k_ref[:, cols], q_ref[:, cols])
+            grad_prob_ref[head, part, :] = split_dot(v_ref[:, cols], grad_mix_ref[:, cols])
     for head in range(HEADS):
         top = stats_ref[2 * head : 2 * head + 1, :]
         inv = stats_ref[2 * head + 1 : 2 * head + 2, :]
@@ -433,7 +444,7 @@
             grad_score_ref[head, part, :] = (prob_ref[head, part, :] * centred).astype(bf16)
     for head in range(HEADS):
         cols = slice(head * HEAD_DIM, (head + 1) * HEAD_DIM)
-        key_rows = jnp.concatenate([k_ref[pl.ds(at, block), cols] for at in starts], axis=0)
+        key_rows = jnp.concatenate([ref[:, cols] for ref in k_refs], axis=0)
         gq = lax.dot_general(grad_score_ref[head], key_rows, TN, preferred_element_type=f32)
         gq_ref[:, cols] = gq.astype(bf16)
         for j, at in enumerate(starts):
@@ -457,6 +468,7 @@
     table_rows = k_table.shape[0]
     own = hbm((rows_dev, width), bf16)
     far = hbm((table_rows - rows_dev, width), bf16)
+    grant = min(60, 16 + 12 * table_rows * width // MIB)
     row_spec = pl.BlockSpec((block, width), lambda i, _: (i, 0))
     return pl.pallas_call(
         functools.partial(backward_kernel, reads),
@@ -471,9 +483,8 @@
                 row_spec,
                 pl.BlockSpec((2 * HEADS, block), lambda i, _: (i, 0)),
                 row_spec,
-                whole(k_table.shape),
-                whole(v_table.shape),
-            ],
+            ]
+            + entry_specs(block, width, reads) * 2,
             out_specs=(
                 row_spec,
                 whole(own.shape),
@@ -491,9 +502,19 @@
                 pltpu.VMEM((block, width), bf16),
             ],
         ),
-        compiler_params=params(60),
+        compiler_params=params(grant),
         name="backward",
-    )(entries, to_node, cot_rows, gain, mixed, stats, queries, k_table, v_table)
+    )(
+        entries,
+        pin(to_node),
+        pin(cot_rows),
+        gain,
+        pin(mixed),
+        pin(stats),
+        pin(queries),
+        *entry_args(k_table, reads),
+        *entry_args(v_table, reads),
+    )
 
 
 def far_kernel(k_ref, v_ref, wk_ref, wv_ref, *out_refs):
@@ -505,18 +526,19 @@
         out_ref[...] = total.astype(bf16)
 
 
-def far_project(far_k, far_v, w_key, w_value, shifts):
+def far_project(far_k, far_v, w_key, w_value, shifts, piece, at):
     rows, width = far_k.shape
-    shape = (rows // shifts, width)
+    shape = (rows // shifts, piece)
+    w_spec = pl.BlockSpec((piece, width), lambda i: (at, 0), pipeline_mode=pl.Buffered(1))
     return pl.pallas_call(
         far_kernel,
         out_shape=[hbm(shape, bf16)] * shifts,
         grid=(1,),
-        in_specs=[whole(far_k.shape), whole(far_v.shape), whole(w_key.shape), whole(w_value.shape)],
+        in_specs=[whole(far_k.shape), whole(far_v.shape), w_spec, w_spec],
         out_specs=[whole(shape)] * shifts,
         compiler_params=params(14),
         name="far_project",
-    )(far_k, far_v, w_key, w_value)
+    )(pin(far_k), pin(far_v), w_key, w_value)
 
 
 def own_kernel(q_ref, k_ref, v_ref, wq_ref, wk_ref, wv_ref, out_ref):
@@ -526,19 +548,20 @@
     out_ref[...] = total
 
 
-def own_project(grad_q, own_k, own_v, w_query, w_key, w_value):
+def own_project(grad_q, own_k, own_v, w_query, w_key, w_value, piece, at):
     rows_dev, width = grad_q.shape
     chunk = 256
     spec = pl.BlockSpec((chunk, width), lambda i: (i, 0))
+    w_spec = pl.BlockSpec((piece, width), lambda i: (at, 0), pipeline_mode=pl.Buffered(1))
     return pl.pallas_call(
         own_kernel,
-        out_shape=hbm((rows_dev, width), f32),
+        out_shape=jax.ShapeDtypeStruct((rows_dev, piece), f32),
         grid=(rows_dev // chunk,),
-        in_specs=[spec, spec, spec] + [whole(w_query.shape)] * 3,
-        out_specs=spec,
+        in_specs=[spec, spec, spec, w_spec, w_spec, w_spec],
+        out_specs=pl.BlockSpec((chunk, piece), lambda i: (i, 0)),
         compiler_params=params(16),
         name="own_project",
-    )(grad_q, own_k, own_v, w_query, w_key, w_value)
+    )(pin(grad_q), pin(own_k), pin(own_v), w_query, w_key, w_value)
 
 
 def collect_kernel(capacity, block, picks_ref, own_ref, from_node_ref, *refs):
@@ -595,10 +618,13 @@
     loader = loader.reshape(devices, rows_dev)
     gain = norm_gain.reshape(1, width)
 
+    pieces = 2
+    piece = width // pieces
+
     def exchange(rows):
-        buffer = rows.reshape(devices, per_peer, width)
+        buffer = rows.reshape(devices, per_peer, rows.shape[1])
         out = lax.all_to_all(buffer, ("row", "col"), split_axis=0, concat_axis=0, tiled=True)
-        return out.reshape(rows_dev, width)
+        return out.reshape(rows.shape)
 
     send_row = lax.dynamic_index_in_dim(send_blocks, self_index, 0, keepdims=False)
     peers = (col + 1 + jnp.arange(shifts, dtype=jnp.int32)) % col_count
@@ -611,24 +637,39 @@
         [jnp.arange(block_count, dtype=jnp.int32)[:, None], entries], axis=1
     ).reshape(-1)
 
-    feature_rows = exchange(send_permute(self_id, loader, features))
-    cot_out = send_permute(self_id, loader, cotangent)
+    first, *others = send_permute(self_id, loader, features, pieces)
+    rows = exchange(first)
     to_node, from_node, to_row = index_tables(self_id, loader, rows_dev)
-    feature_rows, cot_out, to_node, from_node, to_row, picks, entries = lax.optimization_barrier(
-        (feature_rows, cot_out, to_node, from_node, to_row, picks, entries)
+    rows, to_node, from_node, to_row, picks, entries, others = lax.optimization_barrier(
+        (rows, to_node, from_node, to_row, picks, entries, others)
     )
-    outgoing = outbound_blocks(picks, to_node, feature_rows, shifts, capacity, block)
-    cot_out, outgoing = lax.optimization_barrier((cot_out, outgoing))
+    def forward_rows(outgoing):
+        moved = []
+        for at in range(shifts):
+            perm = [(c, (c + at + 1) % col_count) for c in range(col_count)]
+            moved.append(lax.ppermute(outgoing[at], "col", perm))
+        return moved
+
+    feature_rows = [rows]
+    outgoing = outbound_blocks(picks, to_node, rows, shifts, capacity, block)
+    arrived = [forward_rows(outgoing)]
+    (cot_out,) = send_permute(self_id, loader, cotangent, 1)
+    for other in others:
+        rows = exchange(other)
+        rows, cot_out, arrived = lax.optimization_barrier((rows, cot_out, arrived))
+        feature_rows.append(rows)
+        outgoing = outbound_blocks(picks, to_node, rows, shifts, capacity, block)
+        cot_out, outgoing = lax.optimization_barrier((cot_out, outgoing))
+        arrived.append(forward_rows(outgoing))
     cot_rows = exchange(cot_out)
 
     queries, k_table, v_table = project(
         to_node, feature_rows, w_query, w_key, w_value, table_rows
     )
     for at in range(shifts):
-        perm = [(c, (c + at + 1) % col_count) for c in range(col_count)]
-        arrived = lax.ppermute(outgoing[at], "col", perm)
-        first = rows_dev + at * capacity * block
-        k_table, v_table = remote_project(arrived, w_key, w_value, k_table, v_table, first)
+        parts = [moved[at] for moved in arrived]
+        start = rows_dev + at * capacity * block
+        k_table, v_table = remote_project(parts, w_key, w_value, k_table, v_table, start)
 
     layer_rows, mixed, stats = forward(
         entries, queries, k_table, v_table, gain, from_node, block, reads
@@ -637,14 +678,24 @@
     grad_q, own_k, own_v, far_k, far_v = backward(
         entries, to_node, cot_rows, gain, mixed, stats, queries, k_table, v_table, block, reads
     )
-    far = far_project(far_k, far_v, w_key, w_value, shifts)
     returned = []
-    for at in range(shifts):
-        perm = [(c, (c - at - 1) % col_count) for c in range(col_count)]
-        returned.append(lax.ppermute(far[at], "col", perm))
-    own = own_project(grad_q, own_k, own_v, w_query, w_key, w_value)
-    grad_back = exchange(collect(picks, own, from_node, returned, capacity, block))
-    return (permute(to_row, layer_back), permute(to_row, grad_back))
+    far_all = [
+        far_project(far_k, far_v, w_key, w_value, shifts, piece, part) for part in range(pieces)
+    ]
+    grad_q, far_all[1:] = lax.optimization_barrier((grad_q, far_all[1:]))
+    for far in far_all:
+        moved = []
+        for at in range(shifts):
+            perm = [(c, (c - at - 1) % col_count) for c in range(col_count)]
+            moved.append(lax.ppermute(far[at], "col", perm))
+        returned.append(moved)
+    grad_back = []
+    for part in range(pieces):
+        own = own_project(grad_q, own_k, own_v, w_query, w_key, w_value, piece, part)
+        grad_back.append(
+            exchange(collect(picks, own, from_node, returned[part], capacity, block))
+        )
+    return (permute(to_row, [layer_back]), permute(to_row, grad_back))
 
 
 def solution(mesh):

time: 289 us -> 271 us (0.938)
  waiting for transfers between devices: 114 us -> 74.4 us
  Pallas kernels: 119 us -> 141 us
  local copies, waits for them, and re-layouts: 24.4 us -> 9.44 us
  starting transfers between devices: 30.8 us -> 43.5 us
    all_to_all x4 -> x6, waiting for transfers between devices: 79.6 us -> 36.8 us  [exchange(): lax.all_to_all(buffer, ('row', 'col'), split_axis=0, concat_axis=0, tiled...]
    unnamed x58 -> x40, local copies, waits for them, and re-layouts: 22.4 us -> 7.43 us
    pallas_call x8 -> x10, Pallas kernels: 33.3 us -> 44.8 us  [the longest x3 15.5 us: permute(): pl.pallas_call(permute_kernel, out_shape=hbm((rows_dev, piece * len(piece...]
    all_to_all x4 -> x6, starting transfers between devices: 25.8 us -> 33.3 us  [exchange(): lax.all_to_all(buffer, ('row', 'col'), split_axis=0, concat_axis=0, tiled...]
    ppermute x6 -> x12, starting transfers between devices: 5 us -> 10.2 us  [the longest x6 6.37 us: forward_rows(): moved.append(lax.ppermute(outgoing[at], 'col', perm))]
    pallas_call x1 -> x2, Pallas kernels: 4.25 us -> 8.96 us  [far_project(): pl.pallas_call(far_kernel, out_shape=[hbm(shape, bf16)] * shifts, grid=(1...]
    ppermute x6 -> x12, waiting for transfers between devices: 34 us -> 37.6 us  [the longest x6 20.2 us: forward_rows(): moved.append(lax.ppermute(outgoing[at], 'col', perm))]
    pallas_call x1 -> x2, Pallas kernels: 4.81 us -> 8.32 us  [outbound_blocks(): pl.pallas_call(functools.partial(outbound_kernel, capacity, block), out_s...]
  transfers between devices with their start and end apart: 10 -> 18, of which waited for: 6 -> 11; matrix products, arithmetic and copies ran while one was open for 0% -> 0% of each run, Pallas kernels for 36% -> 47%
where the time goes in v3:
time: 271 us; the launch traced here: 269 us
  Pallas kernels  141 us (52%)
  waiting for transfers between devices  74.4 us (27%)
  starting transfers between devices  43.5 us (16%)
  local copies, waits for them, and re-layouts  9.44 us (3%)
    all_to_all x6, waiting for transfers between devices, exchange(): lax.all_to_all(buffer, ('row', 'col'), split_axis=0, concat_axis=0, tiled...  36.8 us
    pallas_call x1, Pallas kernels, backward(): pl.pallas_call(functools.partial(backward_kernel, reads), out_shape=(own,...  35 us
    all_to_all x6, starting transfers between devices, exchange(): lax.all_to_all(buffer, ('row', 'col'), split_axis=0, concat_axis=0, tiled...  33.3 us
    ppermute x6, waiting for transfers between devices, forward_rows(): moved.append(lax.ppermute(outgoing[at], 'col', perm))  20.2 us
    pallas_call x1, Pallas kernels, forward(): pl.pallas_call(functools.partial(forward_kernel, reads), out_shape=(hbm((...  20.1 us
    ppermute x6, waiting for transfers between devices, body(): moved.append(lax.ppermute(far[at], 'col', perm))  17.4 us
    pallas_call x3, Pallas kernels, permute(): pl.pallas_call(permute_kernel, out_shape=hbm((rows_dev, piece * len(piece...  15.5 us
    pallas_call x1, Pallas kernels, project(): pl.pallas_call(project_kernel, out_shape=(hbm((rows_dev, width), bf16), t...  12.1 us
  transfers between devices with their start and end apart: 18, of which 11 were waited for; matrix products, arithmetic and copies ran while one was open for 0% of the time, Pallas kernels for 47%

profile of v3, /device:TPU:0, one launch (start us, length us, event | category | flops | bytes accessed | tf_op | source)
XLA Modules:
  0.0 269.4 jit_solution(12486992936425138821)
XLA Ops:
  1.6 5.4 %send_permute.2 = (bf16[1024,512]{1,0:T(8,128)(2,1)}, bf16[1024,512]{1,0:T(8,128)(2,1)}) custom-call(s32[1]{0:T(128)} %bitcast.self_ref, s32[32,1024]{1,0:T(8,128)S(1)} %reshape.105.loader_ref, bf16[1024,1024]{1,0:T(8,128)(2,1)} %rows_ref.2), custom_call_target="tpu_custom_call" | custom-call | tf_op jit(solution)/shard_map/send_permute/pallas_call | solution.py:98
  7.0 7.3 %all-to-all-start = ((bf16[32,32,512]{2,1,0:T(8,128)(2,1)}), bf16[32,32,512]{2,1,0:T(8,128)(2,1)S(1)}, u32[]{:S(2)}, u32[]{:S(2)}) async-start(bf16[32,32,512]{2,1,0:T(8,128)(2,1)} %bitcast.27), calls=%async_computation | async-start | bytes 2097152 | tf_op jit(solution)/shard_map/all_to_all | solution.py:626
  14.3 5.7 %index_tables.1 = (bf16[1024,1024]{1,0:T(8,128)(2,1)}, bf16[1024,1024]{1,0:T(8,128)(2,1)}, bf16[1024,1024]{1,0:T(8,128)(2,1)}) custom-call(s32[1]{0:T(128)} %bitcast.self_ref, s32[32,1024]{1,0:T(8,128)S(1)} %reshape.105.loader_ref), custom_call_target="tpu_custom_call" | custom-call | tf_op jit(solution)/shard_map/index_tables/pallas_call | solution.py:147
  21.2 19.4 %all-to-all-done = bf16[32,32,512]{2,1,0:T(8,128)(2,1)S(1)} async-done(((bf16[32,32,512]{2,1,0:T(8,128)(2,1)}), bf16[32,32,512]{2,1,0:T(8,128)(2,1)S(1)}, u32[]{:S(2)}, u32[]{:S(2)}) %all-to-all-start) | async-done | bytes 1048608 | tf_op jit(solution)/shard_map/all_to_all | solution.py:626
  44.3 4.2 %outbound.2 = (bf16[256,512]{1,0:T(8,128)(2,1)}, bf16[256,512]{1,0:T(8,128)(2,1)}, bf16[256,512]{1,0:T(8,128)(2,1)}) custom-call(s32[6]{0:T(128)S(1)} %reshape.108.picks_ref, bf16[1024,1024]{1,0:T(8,128)(2,1)} %get-tuple-element.63.to_node_ref, bf16[1024,512]{1,0:T(8,128)(2,1)} %bitcast.19), custom_call_target="tpu_custom_call" | custom-call | tf_op jit(solution)/shard_map/outbound/pallas_call | solution.py:205
  51.7 5.6 %send_permute.3 = bf16[1024,1024]{1,0:T(8,128)(2,1)} custom-call(s32[1]{0:T(128)} %bitcast.self_ref, s32[32,1024]{1,0:T(8,128)S(1)} %reshape.105.loader_ref, bf16[1024,1024]{1,0:T(8,128)(2,1)} %rows_ref.3), custom_call_target="tpu_custom_call" | custom-call | tf_op jit(solution)/shard_map/send_permute/pallas_call | solution.py:98
  57.2 5.8 %collective-permute-done.refs_0_ = bf16[256,512]{1,0:T(8,128)(2,1)S(1)} collective-permute-done((bf16[256,512]{1,0:T(8,128)(2,1)}, bf16[256,512]{1,0:T(8,128)(2,1)S(1)}, u32[]{:S(2)}, u32[]{:S(2)}) %collective-permute-start) | collective-permute-done | bytes 262176 | tf_op jit(solution)/shard_map/ppermute | solution.py:650
  63.0 5.6 %collective-permute-done.2.refs_0_ = bf16[256,512]{1,0:T(8,128)(2,1)S(1)} collective-permute-done((bf16[256,512]{1,0:T(8,128)(2,1)}, bf16[256,512]{1,0:T(8,128)(2,1)S(1)}, u32[]{:S(2)}, u32[]{:S(2)}) %collective-permute-start.2) | collective-permute-done | bytes 262176 | tf_op jit(solution)/shard_map/ppermute | solution.py:650
  84.9 12.1 %project.1 = (bf16[1024,1024]{1,0:T(8,128)(2,1)}, bf16[1792,1024]{1,0:T(8,128)(2,1)}, bf16[1792,1024]{1,0:T(8,128)(2,1)}) custom-call(bf16[1024,1024]{1,0:T(8,128)(2,1)} %get-tuple-element.63.to_node_ref, bf16[1024,1024]{1,0:T(8,128)(2,1)S(1)} %copy-done.6, bf16[1024,1024]{1,0:T(8,128)(2,1)S(1)} %copy-done.2, bf16[1024,1024]{1,0:T(8,128)(2,1)S(1)} %copy-done.3, ...), custom_call_target="tpu_custom_call" | custom-call | tf_op jit(solution)/shard_map/project/pallas_call | solution.py:234
  112.1 20.1 %forward.1 = (bf16[1024,1024]{1,0:T(8,128)(2,1)}, f32[1024,1024]{1,0:T(8,128)}, f32[128,128]{1,0:T(8,128)}) custom-call(s32[32]{0:T(128)S(1)} %reshape.109.entries_ref, bf16[1024,1024]{1,0:T(8,128)(2,1)} %get-tuple-element.71.q_ref, f32[1,1024]{1,0:T(1,128)S(1)} %bitcast.17, bf16[1024,1024]{1,0:T(8,128)(2,1)S(1)} %copy-done.9, ...), custom_call_target="tpu_custom_call" | custom-call | tf_op jit(solution)/shard_map/forward/pallas_call | solution.py:352
  132.2 8.9 %all-to-all-start.2 = ((bf16[32,32,1024]{2,1,0:T(8,128)(2,1)}), bf16[32,32,1024]{2,1,0:T(8,128)(2,1)}, u32[]{:S(2)}, u32[]{:S(2)}) async-start(bf16[32,32,1024]{2,1,0:T(8,128)(2,1)} %bitcast.26), calls=%async_computation.2 | async-start | bytes 4194304 | tf_op jit(solution)/shard_map/all_to_all | solution.py:626
  141.1 35.0 %backward.1 = (bf16[1024,1024]{1,0:T(8,128)(2,1)}, bf16[1024,1024]{1,0:T(8,128)(2,1)}, bf16[1024,1024]{1,0:T(8,128)(2,1)}, bf16[768,1024]{1,0:T(8,128)(2,1)}, bf16[768,1024]{1,0:T(8,128)(2,1)}) custom-call(s32[32]{0:T(128)S(1)} %reshape.109.entries_ref, bf16[1024,1024]{1,0:T(8,128)(2,1)} %get-tuple-element.63.to_node_ref, ...), custom_call_target="tpu_custom_call" | custom-call | tf_op jit(solution)/shard_map/backward/pallas_call | solution.py:473
  176.1 4.4 %far_project.3 = (bf16[256,512]{1,0:T(8,128)(2,1)}, bf16[256,512]{1,0:T(8,128)(2,1)}, bf16[256,512]{1,0:T(8,128)(2,1)}) custom-call(bf16[768,1024]{1,0:T(8,128)(2,1)} %get-tuple-element.96.k_ref, bf16[768,1024]{1,0:T(8,128)(2,1)} %get-tuple-element.97.v_ref, bf16[1024,1024]{1,0:T(8,128)(2,1)S(1)} %copy-done.2, bf16[1024,1024]{1,0:T(8,128)(2,1)S(1)} %copy-done.4), custom_call_target="tpu_custom_call" | custom-call | tf_op jit(solution)/shard_map/far_project/pallas_call | solution.py:533
  182.3 4.6 %far_project.2 = (bf16[256,512]{1,0:T(8,128)(2,1)}, bf16[256,512]{1,0:T(8,128)(2,1)}, bf16[256,512]{1,0:T(8,128)(2,1)}) custom-call(bf16[768,1024]{1,0:T(8,128)(2,1)} %get-tuple-element.96.k_ref, bf16[768,1024]{1,0:T(8,128)(2,1)} %get-tuple-element.97.v_ref, bf16[1024,1024]{1,0:T(8,128)(2,1)S(1)} %copy-done.2, bf16[1024,1024]{1,0:T(8,128)(2,1)S(1)} %copy-done.4), custom_call_target="tpu_custom_call" | custom-call | tf_op jit(solution)/shard_map/far_project/pallas_call | solution.py:533
  186.8 6.0 %own_project.3.own_ref = f32[1024,512]{1,0:T(8,128)S(1)} custom-call(bf16[1024,1024]{1,0:T(8,128)(2,1)} %get-tuple-element.101.q_ref, bf16[1024,1024]{1,0:T(8,128)(2,1)} %get-tuple-element.102.k_ref, bf16[1024,1024]{1,0:T(8,128)(2,1)} %get-tuple-element.103.v_ref, bf16[1024,1024]{1,0:T(8,128)(2,1)S(1)} %copy-done.7, bf16[1024,1024]{1,0:T(8,128)(2,1)S(1)} %copy-done.2, ...), custom_call_target="tpu_custom_call" | custom-call | tf_op jit(solution)/shard_map/own_project/pallas_call | solution.py:556
  199.3 5.0 %all-to-all-start.5 = ((bf16[32,32,512]{2,1,0:T(8,128)(2,1)}), bf16[32,32,512]{2,1,0:T(8,128)(2,1)S(1)}, u32[]{:S(2)}, u32[]{:S(2)}) async-start(bf16[32,32,512]{2,1,0:T(8,128)(2,1)} %bitcast.24), calls=%async_computation.5 | async-start | bytes 2097152 | tf_op jit(solution)/shard_map/all_to_all | solution.py:626
  209.7 6.0 %own_project.2.own_ref = f32[1024,512]{1,0:T(8,128)S(1)} custom-call(bf16[1024,1024]{1,0:T(8,128)(2,1)} %get-tuple-element.101.q_ref, bf16[1024,1024]{1,0:T(8,128)(2,1)} %get-tuple-element.102.k_ref, bf16[1024,1024]{1,0:T(8,128)(2,1)} %get-tuple-element.103.v_ref, bf16[1024,1024]{1,0:T(8,128)(2,1)S(1)} %copy-done.8, bf16[1024,1024]{1,0:T(8,128)(2,1)S(1)} %copy-done.2, ...), custom_call_target="tpu_custom_call" | custom-call | tf_op jit(solution)/shard_map/own_project/pallas_call | solution.py:556
  215.7 5.2 %collective-permute-done.6.refs_0_ = bf16[256,512]{1,0:T(8,128)(2,1)S(1)} collective-permute-done((bf16[256,512]{1,0:T(8,128)(2,1)}, bf16[256,512]{1,0:T(8,128)(2,1)S(1)}, u32[]{:S(2)}, u32[]{:S(2)}) %collective-permute-start.6) | collective-permute-done | bytes 262176 | tf_op jit(solution)/shard_map/ppermute | solution.py:690
  220.9 8.8 %collective-permute-done.7.refs_1_ = bf16[256,512]{1,0:T(8,128)(2,1)S(1)} collective-permute-done((bf16[256,512]{1,0:T(8,128)(2,1)}, bf16[256,512]{1,0:T(8,128)(2,1)S(1)}, u32[]{:S(2)}, u32[]{:S(2)}) %collective-permute-start.7) | collective-permute-done | bytes 262176 | tf_op jit(solution)/shard_map/ppermute | solution.py:690
  232.8 4.5 %all-to-all-start.4 = ((bf16[32,32,512]{2,1,0:T(8,128)(2,1)}), bf16[32,32,512]{2,1,0:T(8,128)(2,1)S(1)}, u32[]{:S(2)}, u32[]{:S(2)}) async-start(bf16[32,32,512]{2,1,0:T(8,128)(2,1)} %bitcast.25), calls=%async_computation.4 | async-start | bytes 2097152 | tf_op jit(solution)/shard_map/all_to_all | solution.py:626
  237.4 6.0 %permute.3 = bf16[1024,1024]{1,0:T(8,128)(2,1)} custom-call(bf16[1024,1024]{1,0:T(8,128)(2,1)} %get-tuple-element.61.pick_ref, bf16[1024,1024]{1,0:T(8,128)(2,1)} %bitcast.9.rows_ref), custom_call_target="tpu_custom_call" | custom-call | tf_op jit(solution)/shard_map/permute/pallas_call | solution.py:179
  243.4 4.8 %permute.4.refs_0_ = bf16[1024,1024]{1,0:T(8,128)(2,1)} custom-call(bf16[1024,1024]{1,0:T(8,128)(2,1)} %get-tuple-element.61.pick_ref, bf16[1024,512]{1,0:T(8,128)(2,1)} %bitcast.22), custom_call_target="tpu_custom_call" | custom-call | tf_op jit(solution)/shard_map/permute/pallas_call | solution.py:179
  248.2 15.5 %all-to-all-done.4 = bf16[32,32,512]{2,1,0:T(8,128)(2,1)S(1)} async-done(((bf16[32,32,512]{2,1,0:T(8,128)(2,1)}), bf16[32,32,512]{2,1,0:T(8,128)(2,1)S(1)}, u32[]{:S(2)}, u32[]{:S(2)}) %all-to-all-start.4) | async-done | bytes 1048608 | tf_op jit(solution)/shard_map/all_to_all | solution.py:626
  264.6 4.7 %permute.5 = bf16[1024,1024]{1,0:T(8,128)(2,1)} custom-call(bf16[1024,1024]{1,0:T(8,128)(2,1)} %get-tuple-element.61.pick_ref, bf16[1024,512]{1,0:T(8,128)(2,1)} %bitcast.23, bf16[1024,1024]{1,0:T(8,128)(2,1)} %permute.4.refs_0_), custom_call_target="tpu_custom_call", output_to_operand_aliasing={{}: (2, {})} | custom-call | tf_op jit(solution)/shard_map/permute/pallas_call | solution.py:179
  (85 shorter events, 57.9 us)
Async XLA Ops:
  0.6 19.4 %copy-start = (s32[32,4,2]{0,2,1:T(2,128)S(1)}, s32[32,4,2]{0,2,1:T(2,128)}, u32[]{:S(2)}) copy-start(s32[32,4,2]{0,2,1:T(2,128)} %param.16) | copy-start | bytes 3076
  1.6 19.3 %copy-start.16 = (s32[8,3]{0,1:T(4,128)S(1)}, s32[8,3]{0,1:T(4,128)}, u32[]{:S(2)}) copy-start(s32[8,3]{0,1:T(4,128)} %param.17) | copy-start | bytes 292
  7.0 33.5 %all-to-all-start = ((bf16[32,32,512]{2,1,0:T(8,128)(2,1)}), bf16[32,32,512]{2,1,0:T(8,128)(2,1)S(1)}, u32[]{:S(2)}, u32[]{:S(2)}) async-start(bf16[32,32,512]{2,1,0:T(8,128)(2,1)} %bitcast.27), calls=%async_computation | async-start | bytes 2097152 | tf_op jit(solution)/shard_map/all_to_all | solution.py:626
  40.6 30.0 %all-to-all-start.1 = ((bf16[32,32,512]{2,1,0:T(8,128)(2,1)}), bf16[32,32,512]{2,1,0:T(8,128)(2,1)}, u32[]{:S(2)}, u32[]{:S(2)}) async-start(bf16[32,32,512]{2,1,0:T(8,128)(2,1)} %bitcast.5), calls=%async_computation.1 | async-start | bytes 2097152 | tf_op jit(solution)/shard_map/all_to_all | solution.py:626
  48.5 14.5 %collective-permute-start = (bf16[256,512]{1,0:T(8,128)(2,1)}, bf16[256,512]{1,0:T(8,128)(2,1)S(1)}, u32[]{:S(2)}, u32[]{:S(2)}) collective-permute-start(bf16[256,512]{1,0:T(8,128)(2,1)} %get-tuple-element.67), channel_id=1, source_target_pairs={{0,1},{1,2},{2,3},{3,0},{4,5},{5,6},{6,7},{7,4},{8,9},{9,10},{10,1... | collective-permute-start | bytes 786440 | tf_op jit(solution)/shard_map/ppermute | solution.py:650
  48.7 14.3 %collective-permute-start.1 = (bf16[256,512]{1,0:T(8,128)(2,1)}, bf16[256,512]{1,0:T(8,128)(2,1)S(1)}, u32[]{:S(2)}, u32[]{:S(2)}) collective-permute-start(bf16[256,512]{1,0:T(8,128)(2,1)} %get-tuple-element.68), channel_id=1, source_target_pairs={{0,2},{1,3},{2,0},{3,1},{4,6},{5,7},{6,4},{7,5},{8,10},{9,11},{10,... | collective-permute-start | bytes 786440 | tf_op jit(solution)/shard_map/ppermute | solution.py:650
  50.3 18.3 %collective-permute-start.2 = (bf16[256,512]{1,0:T(8,128)(2,1)}, bf16[256,512]{1,0:T(8,128)(2,1)S(1)}, u32[]{:S(2)}, u32[]{:S(2)}) collective-permute-start(bf16[256,512]{1,0:T(8,128)(2,1)} %get-tuple-element.69), channel_id=1, source_target_pairs={{0,3},{1,0},{2,1},{3,2},{4,7},{5,4},{6,5},{7,6},{8,11},{9,8},{10,9... | collective-permute-start | bytes 786440 | tf_op jit(solution)/shard_map/ppermute | solution.py:650
  74.7 57.5 %all-to-all-start.3 = ((bf16[32,32,1024]{2,1,0:T(8,128)(2,1)}), bf16[32,32,1024]{2,1,0:T(8,128)(2,1)}, u32[]{:S(2)}, u32[]{:S(2)}) async-start(bf16[32,32,1024]{2,1,0:T(8,128)(2,1)} %bitcast.21), calls=%async_computation.3 | async-start | bytes 4194304 | tf_op jit(solution)/shard_map/all_to_all | solution.py:626
  78.5 21.3 %collective-permute-start.3 = (bf16[256,512]{1,0:T(8,128)(2,1)}, bf16[256,512]{1,0:T(8,128)(2,1)S(1)}, u32[]{:S(2)}, u32[]{:S(2)}) collective-permute-start(bf16[256,512]{1,0:T(8,128)(2,1)} %get-tuple-element.80), channel_id=1, source_target_pairs={{0,1},{1,2},{2,3},{3,0},{4,5},{5,6},{6,7},{7,4},{8,9},{9,10},{10,1... | collective-permute-start | bytes 786440 | tf_op jit(solution)/shard_map/ppermute | solution.py:650
  78.7 26.9 %collective-permute-start.4 = (bf16[256,512]{1,0:T(8,128)(2,1)S(1)}, bf16[256,512]{1,0:T(8,128)(2,1)S(1)}, u32[]{:S(2)}, u32[]{:S(2)}) collective-permute-start(bf16[256,512]{1,0:T(8,128)(2,1)S(1)} %copy-done.19), channel_id=1, source_target_pairs={{0,2},{1,3},{2,0},{3,1},{4,6},{5,7},{6,4},{7,5},{8,10},{9,11},{10,... | collective-permute-start | bytes 786440 | tf_op jit(solution)/shard_map/ppermute | solution.py:650
  80.4 29.6 %collective-permute-start.5 = (bf16[256,512]{1,0:T(8,128)(2,1)S(1)}, bf16[256,512]{1,0:T(8,128)(2,1)S(1)}, u32[]{:S(2)}, u32[]{:S(2)}) collective-permute-start(bf16[256,512]{1,0:T(8,128)(2,1)S(1)} %copy-done.18), channel_id=1, source_target_pairs={{0,3},{1,0},{2,1},{3,2},{4,7},{5,4},{6,5},{7,6},{8,11},{9,8},{10,9... | collective-permute-start | bytes 786440 | tf_op jit(solution)/shard_map/ppermute | solution.py:650
  132.2 67.1 %all-to-all-start.2 = ((bf16[32,32,1024]{2,1,0:T(8,128)(2,1)}), bf16[32,32,1024]{2,1,0:T(8,128)(2,1)}, u32[]{:S(2)}, u32[]{:S(2)}) async-start(bf16[32,32,1024]{2,1,0:T(8,128)(2,1)} %bitcast.26), calls=%async_computation.2 | async-start | bytes 4194304 | tf_op jit(solution)/shard_map/all_to_all | solution.py:626
  141.1 35.0 %copy-start.4 = (bf16[1024,1024]{1,0:T(8,128)(2,1)S(1)}, bf16[1024,1024]{1,0:T(8,128)(2,1)}, u32[]{:S(2)}) copy-start(bf16[1024,1024]{1,0:T(8,128)(2,1)} %wv_ref.15) | copy-start | bytes 6291460
  180.5 12.3 %collective-permute-start.9 = (bf16[256,512]{1,0:T(8,128)(2,1)}, bf16[256,512]{1,0:T(8,128)(2,1)S(1)}, u32[]{:S(2)}, u32[]{:S(2)}) collective-permute-start(bf16[256,512]{1,0:T(8,128)(2,1)} %get-tuple-element.107), channel_id=1, source_target_pairs={{0,3},{1,0},{2,1},{3,2},{4,7},{5,4},{6,5},{7,6},{8,11},{9,8},{10,9... | collective-permute-start | bytes 786440 | tf_op jit(solution)/shard_map/ppermute | solution.py:690
  181.8 14.5 %collective-permute-start.10 = (bf16[256,512]{1,0:T(8,128)(2,1)}, bf16[256,512]{1,0:T(8,128)(2,1)S(1)}, u32[]{:S(2)}, u32[]{:S(2)}) collective-permute-start(bf16[256,512]{1,0:T(8,128)(2,1)} %get-tuple-element.108), channel_id=1, source_target_pairs={{0,2},{1,3},{2,0},{3,1},{4,6},{5,7},{6,4},{7,5},{8,10},{9,11},{10,... | collective-permute-start | bytes 786440 | tf_op jit(solution)/shard_map/ppermute | solution.py:690
  182.2 14.1 %collective-permute-start.11 = (bf16[256,512]{1,0:T(8,128)(2,1)}, bf16[256,512]{1,0:T(8,128)(2,1)S(1)}, u32[]{:S(2)}, u32[]{:S(2)}) collective-permute-start(bf16[256,512]{1,0:T(8,128)(2,1)} %get-tuple-element.109), channel_id=1, source_target_pairs={{0,1},{1,2},{2,3},{3,0},{4,5},{5,6},{6,7},{7,4},{8,9},{9,10},{10,1... | collective-permute-start | bytes 786440 | tf_op jit(solution)/shard_map/ppermute | solution.py:690
  186.8 9.5 %copy-start.10 = (bf16[1024,1024]{1,0:T(8,128)(2,1)S(1)}, bf16[1024,1024]{1,0:T(8,128)(2,1)}, u32[]{:S(2)}) copy-start(bf16[1024,1024]{1,0:T(8,128)(2,1)} %get-tuple-element.72.from_node_ref) | copy-start | bytes 6291460
  199.3 33.5 %all-to-all-start.5 = ((bf16[32,32,512]{2,1,0:T(8,128)(2,1)}), bf16[32,32,512]{2,1,0:T(8,128)(2,1)S(1)}, u32[]{:S(2)}, u32[]{:S(2)}) async-start(bf16[32,32,512]{2,1,0:T(8,128)(2,1)} %bitcast.24), calls=%async_computation.5 | async-start | bytes 2097152 | tf_op jit(solution)/shard_map/all_to_all | solution.py:626
  204.4 16.5 %collective-permute-start.6 = (bf16[256,512]{1,0:T(8,128)(2,1)}, bf16[256,512]{1,0:T(8,128)(2,1)S(1)}, u32[]{:S(2)}, u32[]{:S(2)}) collective-permute-start(bf16[256,512]{1,0:T(8,128)(2,1)} %get-tuple-element.104), channel_id=1, source_target_pairs={{0,3},{1,0},{2,1},{3,2},{4,7},{5,4},{6,5},{7,6},{8,11},{9,8},{10,9... | collective-permute-start | bytes 786440 | tf_op jit(solution)/shard_map/ppermute | solution.py:690
  206.0 23.8 %collective-permute-start.7 = (bf16[256,512]{1,0:T(8,128)(2,1)}, bf16[256,512]{1,0:T(8,128)(2,1)S(1)}, u32[]{:S(2)}, u32[]{:S(2)}) collective-permute-start(bf16[256,512]{1,0:T(8,128)(2,1)} %get-tuple-element.105), channel_id=1, source_target_pairs={{0,2},{1,3},{2,0},{3,1},{4,6},{5,7},{6,4},{7,5},{8,10},{9,11},{10,... | collective-permute-start | bytes 786440 | tf_op jit(solution)/shard_map/ppermute | solution.py:690
  206.3 23.4 %collective-permute-start.8 = (bf16[256,512]{1,0:T(8,128)(2,1)S(1)}, bf16[256,512]{1,0:T(8,128)(2,1)S(1)}, u32[]{:S(2)}, u32[]{:S(2)}) collective-permute-start(bf16[256,512]{1,0:T(8,128)(2,1)S(1)} %copy-done.17), channel_id=1, source_target_pairs={{0,1},{1,2},{2,3},{3,0},{4,5},{5,6},{6,7},{7,4},{8,9},{9,10},{10,1... | collective-permute-start | bytes 786440 | tf_op jit(solution)/shard_map/ppermute | solution.py:690
  209.7 20.1 %copy-start.11 = (bf16[1024,1024]{1,0:T(8,128)(2,1)S(1)}, bf16[1024,1024]{1,0:T(8,128)(2,1)}, u32[]{:S(2)}) copy-start(bf16[1024,1024]{1,0:T(8,128)(2,1)} %get-tuple-element.72.from_node_ref) | copy-start | bytes 6291460
  232.8 10.6 %copy-start.14 = (bf16[32,32,512]{2,1,0:T(8,128)(2,1)}, bf16[32,32,512]{2,1,0:T(8,128)(2,1)S(1)}, u32[]{:S(2)}) copy-start(bf16[32,32,512]{2,1,0:T(8,128)(2,1)S(1)} %all-to-all-done.5) | copy-start | bytes 3145732
  232.8 30.8 %all-to-all-start.4 = ((bf16[32,32,512]{2,1,0:T(8,128)(2,1)}), bf16[32,32,512]{2,1,0:T(8,128)(2,1)S(1)}, u32[]{:S(2)}, u32[]{:S(2)}) async-start(bf16[32,32,512]{2,1,0:T(8,128)(2,1)} %bitcast.25), calls=%async_computation.4 | async-start | bytes 2097152 | tf_op jit(solution)/shard_map/all_to_all | solution.py:626
  (14 other events, 49.4 us)

commit v4 on v3

--- a/solution.py
+++ b/solution.py
@@ -16,6 +16,8 @@
 MIB = 1024 * 1024
 SUBLANES = 8
 CHUNK = 64
+UNIT = 256
+LIGHT = pl.CostEstimate(flops=0, transcendentals=0, bytes_accessed=0)
 
 NT = (((1,), (1,)), ((), ()))
 TN = (((0,), (0,)), ((), ()))
@@ -31,8 +33,10 @@
     return pltpu.with_memory_space_constraint(value, pltpu.HBM)
 
 
-def params(mib):
-    return pltpu.CompilerParams(dimension_semantics=("arbitrary",), vmem_limit_bytes=mib * MIB)
+def params(mib, axes=1):
+    return pltpu.CompilerParams(
+        dimension_semantics=("arbitrary",) * axes, vmem_limit_bytes=mib * MIB
+    )
 
 
 def whole(shape):
@@ -74,10 +78,9 @@
     return jnp.where(cond, 1.0, 0.0)
 
 
-def send_kernel(self_ref, loader_ref, rows_ref, *refs):
-    out_refs, slot_ref = refs[:-1], refs[-1]
+def send_kernel(self_ref, loader_ref, rows_ref, out_ref, slot_ref):
     step = pl.program_id(0)
-    chunk, piece = out_refs[0].shape
+    chunk = out_ref.shape[0]
     rows_dev = rows_ref.shape[0]
 
     @pl.when(step == 0)
@@ -86,23 +89,26 @@
         slot_ref[...] = send_slots(nodes, loader_ref.shape[0])
 
     pick = one_hot(slot_ref[...] == iota((chunk, rows_dev), 0) + step * chunk)
-    moved = matmul(pick.astype(bf16), rows_ref[...]).astype(bf16)
-    for at, out_ref in enumerate(out_refs):
-        out_ref[...] = moved[:, at * piece : (at + 1) * piece]
-
-
-def send_permute(self_id, loader, rows, pieces):
+    out_ref[...] = matmul(pick.astype(bf16), rows_ref[...]).astype(bf16)
+
+
+def send_permute(self_id, loader, rows, pieces, at):
     rows_dev, width = rows.shape
     chunk = 256
     piece = width // pieces
     return pl.pallas_call(
         send_kernel,
-        out_shape=[hbm((rows_dev, piece), bf16)] * pieces,
+        out_shape=hbm((rows_dev, piece), bf16),
         grid_spec=pltpu.PrefetchScalarGridSpec(
             num_scalar_prefetch=1,
             grid=(rows_dev // chunk,),
-            in_specs=[whole(loader.shape), whole(rows.shape)],
-            out_specs=[pl.BlockSpec((chunk, piece), lambda i, _: (i, 0))] * pieces,
+            in_specs=[
+                whole(loader.shape),
+                pl.BlockSpec(
+                    (rows_dev, piece), lambda i, _: (0, at), pipeline_mode=pl.Buffered(1)
+                ),
+            ],
+            out_specs=pl.BlockSpec((chunk, piece), lambda i, _: (i, 0)),
             scratch_shapes=[pltpu.VMEM((1, rows_dev), jnp.int32)],
         ),
         compiler_params=params(10),
@@ -167,27 +173,36 @@
 
 
 def permute_kernel(pick_ref, rows_ref, *refs):
-    refs[-1][...] = matmul(pick_ref[...], rows_ref[...]).astype(bf16)
+    out_ref = refs[-1]
+    chunk = out_ref.shape[0]
+    at = pl.multiple_of(pl.program_id(1) * chunk, chunk)
+    out_ref[...] = matmul(pick_ref[pl.ds(at, chunk), :], rows_ref[...]).astype(bf16)
 
 
 def permute(pick, pieces):
-    rows_dev, piece = pieces[0].shape
-    chunk = 256
-    out = []
-    for at, rows in enumerate(pieces):
+    rows_dev = pick.shape[0]
+    width = sum(rows.shape[1] for rows in pieces)
+    chunk = 512
+    out, low = [], 0
+    for rows in pieces:
+        first = low // UNIT
         out = [
             pl.pallas_call(
                 permute_kernel,
-                out_shape=hbm((rows_dev, piece * len(pieces)), bf16),
-                grid=(rows_dev // chunk,),
-                in_specs=[pl.BlockSpec((chunk, rows_dev), lambda i: (i, 0)), whole(rows.shape)]
+                out_shape=hbm((rows_dev, width), bf16),
+                grid=(rows.shape[1] // UNIT, rows_dev // chunk),
+                in_specs=[
+                    whole(pick.shape),
+                    pl.BlockSpec((rows_dev, UNIT), lambda j, i: (0, j)),
+                ]
                 + [pl.BlockSpec(memory_space=pl.ANY)] * len(out),
-                out_specs=pl.BlockSpec((chunk, piece), lambda i, at=at: (i, at)),
+                out_specs=pl.BlockSpec((chunk, UNIT), lambda j, i, first=first: (i, first + j)),
                 input_output_aliases={2: 0} if out else {},
-                compiler_params=params(8),
+                compiler_params=params(10, 2),
                 name="permute",
-            )(pin(pick), pin(rows), *out)
+            )(pick, pin(rows), *out)
         ]
+        low += rows.shape[1]
     return out[0]
 
 
@@ -312,9 +327,8 @@
     keys = reads * block
     for head in range(HEADS):
         cols = slice(head * HEAD_DIM, (head + 1) * HEAD_DIM)
-        for j, k_ref in enumerate(k_refs):
-            part = slice(j * block, (j + 1) * block)
-            score_ref[head, part, :] = split_dot(k_ref[:, cols], q_ref[:, cols])
+        key_rows = jnp.concatenate([ref[:, cols] for ref in k_refs], axis=0)
+        score_ref[head] = split_dot(key_rows, q_ref[:, cols])
     for head in range(HEADS):
         top = fold(score_ref[head, :CHUNK, :], jnp.maximum)
         for at in range(CHUNK, keys, CHUNK):
@@ -390,6 +404,7 @@
 
 def backward_kernel(
     reads,
+    shifts,
     entries_ref,
     to_node_ref,
     cot_ref,
@@ -400,18 +415,26 @@
     *refs,
 ):
     k_refs, v_refs = refs[:reads], refs[reads : 2 * reads]
-    gq_ref, own_k_ref, own_v_ref, far_k_ref, far_v_ref = refs[2 * reads : 2 * reads + 5]
-    sum_k_ref, sum_v_ref, prob_ref, grad_prob_ref = refs[2 * reads + 5 : 2 * reads + 9]
-    prob_half_ref, grad_score_ref, grad_mix_ref = refs[2 * reads + 9 :]
+    wk_hbm, wv_hbm, gq_ref, own_k_hbm, own_v_hbm = refs[2 * reads : 2 * reads + 5]
+    far_refs = refs[2 * reads + 5 : -14]
+    sum_k_ref, sum_v_ref, prob_ref, grad_prob_ref, prob_half_ref = refs[-14:-9]
+    grad_score_ref, grad_mix_ref, own_k_ref, own_v_ref, wk_ref, wv_ref = refs[-9:-3]
+    w_sem, own_k_sem, own_v_sem = refs[-3:]
     block, width = q_ref.shape
     step = pl.program_id(0)
     own = own_k_ref.shape[0]
     keys = reads * block
+    load_wk = pltpu.make_async_copy(wk_hbm, wk_ref, w_sem.at[0])
+    load_wv = pltpu.make_async_copy(wv_hbm, wv_ref, w_sem.at[1])
+    save_k = pltpu.make_async_copy(own_k_ref, own_k_hbm, own_k_sem)
+    save_v = pltpu.make_async_copy(own_v_ref, own_v_hbm, own_v_sem)
 
     @pl.when(step == 0)
     def _():
         sum_k_ref[...] = jnp.zeros_like(sum_k_ref)
         sum_v_ref[...] = jnp.zeros_like(sum_v_ref)
+        load_wk.start()
+        load_wv.start()
 
     entries = [entries_ref[step * reads + j] * block for j in range(reads)]
     starts = [pl.multiple_of(at, block) for at in entries]
@@ -423,10 +446,10 @@
     grad_mix_ref[...] = grad_mix.astype(bf16)
     for head in range(HEADS):
         cols = slice(head * HEAD_DIM, (head + 1) * HEAD_DIM)
-        for j, (k_ref, v_ref) in enumerate(zip(k_refs, v_refs)):
-            part = slice(j * block, (j + 1) * block)
-            prob_ref[head, part, :] = split_dot(k_ref[:, cols], q_ref[:, cols])
-            grad_prob_ref[head, part, :] = split_dot(v_ref[:, cols], grad_mix_ref[:, cols])
+        key_rows = jnp.concatenate([ref[:, cols] for ref in k_refs], axis=0)
+        val_rows = jnp.concatenate([ref[:, cols] for ref in v_refs], axis=0)
+        prob_ref[head] = split_dot(key_rows, q_ref[:, cols])
+        grad_prob_ref[head] = split_dot(val_rows, grad_mix_ref[:, cols])
     for head in range(HEADS):
         top = stats_ref[2 * head : 2 * head + 1, :]
         inv = stats_ref[2 * head + 1 : 2 * head + 2, :]
@@ -447,32 +470,63 @@
         key_rows = jnp.concatenate([ref[:, cols] for ref in k_refs], axis=0)
         gq = lax.dot_general(grad_score_ref[head], key_rows, TN, preferred_element_type=f32)
         gq_ref[:, cols] = gq.astype(bf16)
+        key_term = matmul(grad_score_ref[head], q_ref[:, cols])
+        value_term = matmul(prob_half_ref[head], grad_mix_ref[:, cols])
         for j, at in enumerate(starts):
             part = slice(j * block, (j + 1) * block)
             rows = pl.ds(at, block)
-            sum_k_ref[rows, cols] += matmul(grad_score_ref[head, part, :], q_ref[:, cols])
-            sum_v_ref[rows, cols] += matmul(prob_half_ref[head, part, :], grad_mix_ref[:, cols])
+            sum_k_ref[rows, cols] += key_term[part]
+            sum_v_ref[rows, cols] += value_term[part]
 
     @pl.when(step == pl.num_programs(0) - 1)
     def _():
         own_k_ref[...] = sum_k_ref[:own, :].astype(bf16)
+        save_k.start()
         own_v_ref[...] = sum_v_ref[:own, :].astype(bf16)
-        far_k_ref[...] = sum_k_ref[own:, :].astype(bf16)
-        far_v_ref[...] = sum_v_ref[own:, :].astype(bf16)
+        save_v.start()
+        load_wk.wait()
+        load_wv.wait()
+        low = 0
+        for piece in range(0, len(far_refs), shifts):
+            chunk, wide = far_refs[piece].shape
+            outs = slice(low, low + wide)
+            for at in range(shifts):
+                rows = slice(own + at * chunk, own + (at + 1) * chunk)
+                total = split_dot(sum_k_ref[rows, :].astype(bf16), wk_ref[outs, :])
+                total += split_dot(sum_v_ref[rows, :].astype(bf16), wv_ref[outs, :])
+                far_refs[piece + at][...] = total.astype(bf16)
+            low += wide
+        save_k.wait()
+        save_v.wait()
 
 
 def backward(
-    entries, to_node, cot_rows, gain, mixed, stats, queries, k_table, v_table, block, reads
+    entries,
+    to_node,
+    cot_rows,
+    gain,
+    mixed,
+    stats,
+    queries,
+    k_table,
+    v_table,
+    w_key,
+    w_value,
+    block,
+    reads,
+    shifts,
+    splits,
 ):
     rows_dev, width = queries.shape
     table_rows = k_table.shape[0]
     own = hbm((rows_dev, width), bf16)
-    far = hbm((table_rows - rows_dev, width), bf16)
-    grant = min(60, 16 + 12 * table_rows * width // MIB)
+    far = [((table_rows - rows_dev) // shifts, wide) for wide in splits for _ in range(shifts)]
+    grant = min(60, 24 + 10 * table_rows * width // MIB)
     row_spec = pl.BlockSpec((block, width), lambda i, _: (i, 0))
-    return pl.pallas_call(
-        functools.partial(backward_kernel, reads),
-        out_shape=(own, own, own, far, far),
+    any_spec = pl.BlockSpec(memory_space=pl.ANY)
+    out = pl.pallas_call(
+        functools.partial(backward_kernel, reads, shifts),
+        out_shape=[own, own, own] + [hbm(shape, bf16) for shape in far],
         grid_spec=pltpu.PrefetchScalarGridSpec(
             num_scalar_prefetch=1,
             grid=(rows_dev // block,),
@@ -484,14 +538,9 @@
                 pl.BlockSpec((2 * HEADS, block), lambda i, _: (i, 0)),
                 row_spec,
             ]
-            + entry_specs(block, width, reads) * 2,
-            out_specs=(
-                row_spec,
-                whole(own.shape),
-                whole(own.shape),
-                whole(far.shape),
-                whole(far.shape),
-            ),
+            + entry_specs(block, width, reads) * 2
+            + [any_spec, any_spec],
+            out_specs=[row_spec, any_spec, any_spec] + [whole(shape) for shape in far],
             scratch_shapes=[
                 pltpu.VMEM((table_rows, width), f32),
                 pltpu.VMEM((table_rows, width), f32),
@@ -500,6 +549,13 @@
                 pltpu.VMEM((HEADS, reads * block, block), bf16),
                 pltpu.VMEM((HEADS, reads * block, block), bf16),
                 pltpu.VMEM((block, width), bf16),
+                pltpu.VMEM((rows_dev, width), bf16),
+                pltpu.VMEM((rows_dev, width), bf16),
+                pltpu.VMEM(w_key.shape, bf16),
+                pltpu.VMEM(w_value.shape, bf16),
+                pltpu.SemaphoreType.DMA((2,)),
+                pltpu.SemaphoreType.DMA,
+                pltpu.SemaphoreType.DMA,
             ],
         ),
         compiler_params=params(grant),
@@ -507,59 +563,43 @@
     )(
         entries,
         pin(to_node),
-        pin(cot_rows),
+        cot_rows,
         gain,
         pin(mixed),
         pin(stats),
         pin(queries),
         *entry_args(k_table, reads),
         *entry_args(v_table, reads),
+        pin(w_key),
+        pin(w_value),
     )
-
-
-def far_kernel(k_ref, v_ref, wk_ref, wv_ref, *out_refs):
-    chunk = out_refs[0].shape[0]
-    for at, out_ref in enumerate(out_refs):
-        rows = slice(at * chunk, (at + 1) * chunk)
-        total = lax.dot_general(k_ref[rows, :], wk_ref[...], NT, preferred_element_type=f32)
-        total += lax.dot_general(v_ref[rows, :], wv_ref[...], NT, preferred_element_type=f32)
-        out_ref[...] = total.astype(bf16)
-
-
-def far_project(far_k, far_v, w_key, w_value, shifts, piece, at):
-    rows, width = far_k.shape
-    shape = (rows // shifts, piece)
-    w_spec = pl.BlockSpec((piece, width), lambda i: (at, 0), pipeline_mode=pl.Buffered(1))
-    return pl.pallas_call(
-        far_kernel,
-        out_shape=[hbm(shape, bf16)] * shifts,
-        grid=(1,),
-        in_specs=[whole(far_k.shape), whole(far_v.shape), w_spec, w_spec],
-        out_specs=[whole(shape)] * shifts,
-        compiler_params=params(14),
-        name="far_project",
-    )(pin(far_k), pin(far_v), w_key, w_value)
-
-
-def own_kernel(q_ref, k_ref, v_ref, wq_ref, wk_ref, wv_ref, out_ref):
-    total = lax.dot_general(q_ref[...], wq_ref[...], NT, preferred_element_type=f32)
-    total += lax.dot_general(k_ref[...], wk_ref[...], NT, preferred_element_type=f32)
-    total += lax.dot_general(v_ref[...], wv_ref[...], NT, preferred_element_type=f32)
-    out_ref[...] = total
-
-
-def own_project(grad_q, own_k, own_v, w_query, w_key, w_value, piece, at):
+    pieces = [out[at : at + shifts] for at in range(3, len(out), shifts)]
+    return out[0], out[1], out[2], pieces
+
+
+def own_kernel(q_ref, k_ref, v_ref, wq_ref, wk_ref, wv_ref, *out_refs):
+    total = split_dot(q_ref[...], wq_ref[...])
+    total += split_dot(k_ref[...], wk_ref[...])
+    total += split_dot(v_ref[...], wv_ref[...])
+    low = 0
+    for out_ref in out_refs:
+        wide = out_ref.shape[1]
+        out_ref[...] = total[:, low : low + wide]
+        low += wide
+
+
+def own_project(grad_q, own_k, own_v, w_query, w_key, w_value, splits):
     rows_dev, width = grad_q.shape
     chunk = 256
     spec = pl.BlockSpec((chunk, width), lambda i: (i, 0))
-    w_spec = pl.BlockSpec((piece, width), lambda i: (at, 0), pipeline_mode=pl.Buffered(1))
     return pl.pallas_call(
         own_kernel,
-        out_shape=jax.ShapeDtypeStruct((rows_dev, piece), f32),
+        out_shape=[jax.ShapeDtypeStruct((rows_dev, wide), f32) for wide in splits],
         grid=(rows_dev // chunk,),
-        in_specs=[spec, spec, spec, w_spec, w_spec, w_spec],
-        out_specs=pl.BlockSpec((chunk, piece), lambda i: (i, 0)),
-        compiler_params=params(16),
+        in_specs=[spec, spec, spec] + [whole(w_query.shape)] * 3,
+        out_specs=[pl.BlockSpec((chunk, wide), lambda i: (i, 0)) for wide in splits],
+        compiler_params=params(20),
+        cost_estimate=LIGHT,
         name="own_project",
     )(pin(grad_q), pin(own_k), pin(own_v), w_query, w_key, w_value)
 
@@ -594,6 +634,7 @@
             scratch_shapes=[pltpu.VMEM((rows_dev, width), f32)],
         ),
         compiler_params=params(20),
+        cost_estimate=LIGHT,
         name="collect",
     )(picks, own, from_node, *returned)
 
@@ -618,8 +659,7 @@
     loader = loader.reshape(devices, rows_dev)
     gain = norm_gain.reshape(1, width)
 
-    pieces = 2
-    piece = width // pieces
+    splits = (width // 2, width // 2)
 
     def exchange(rows):
         buffer = rows.reshape(devices, per_peer, rows.shape[1])
@@ -637,8 +677,8 @@
         [jnp.arange(block_count, dtype=jnp.int32)[:, None], entries], axis=1
     ).reshape(-1)
 
-    first, *others = send_permute(self_id, loader, features, pieces)
-    rows = exchange(first)
+    rows = exchange(send_permute(self_id, loader, features, 2, 0))
+    others = [send_permute(self_id, loader, features, 2, 1)]
     to_node, from_node, to_row = index_tables(self_id, loader, rows_dev)
     rows, to_node, from_node, to_row, picks, entries, others = lax.optimization_barrier(
         (rows, to_node, from_node, to_row, picks, entries, others)
@@ -653,7 +693,7 @@
     feature_rows = [rows]
     outgoing = outbound_blocks(picks, to_node, rows, shifts, capacity, block)
     arrived = [forward_rows(outgoing)]
-    (cot_out,) = send_permute(self_id, loader, cotangent, 1)
+    cot_out = send_permute(self_id, loader, cotangent, 1, 0)
     for other in others:
         rows = exchange(other)
         rows, cot_out, arrived = lax.optimization_barrier((rows, cot_out, arrived))
@@ -675,26 +715,35 @@
         entries, queries, k_table, v_table, gain, from_node, block, reads
     )
     layer_back = exchange(layer_rows)
-    grad_q, own_k, own_v, far_k, far_v = backward(
-        entries, to_node, cot_rows, gain, mixed, stats, queries, k_table, v_table, block, reads
+    grad_q, own_k, own_v, far_all = backward(
+        entries,
+        to_node,
+        cot_rows,
+        gain,
+        mixed,
+        stats,
+        queries,
+        k_table,
+        v_table,
+        w_key,
+        w_value,
+        block,
+        reads,
+        shifts,
+        splits,
     )
     returned = []
-    far_all = [
-        far_project(far_k, far_v, w_key, w_value, shifts, piece, part) for part in range(pieces)
-    ]
-    grad_q, far_all[1:] = lax.optimization_barrier((grad_q, far_all[1:]))
     for far in far_all:
         moved = []
         for at in range(shifts):
             perm = [(c, (c - at - 1) % col_count) for c in range(col_count)]
             moved.append(lax.ppermute(far[at], "col", perm))
         returned.append(moved)
-    grad_back = []
-    for part in range(pieces):
-        own = own_project(grad_q, own_k, own_v, w_query, w_key, w_value, piece, part)
-        grad_back.append(
-            exchange(collect(picks, own, from_node, returned[part], capacity, block))
-        )
+    own_parts = own_project(grad_q, own_k, own_v, w_query, w_key, w_value, splits)
+    grad_back = [
+        exchange(collect(picks, own, from_node, moved, capacity, block))
+        for own, moved in zip(own_parts, returned)
+    ]
     return (permute(to_row, [layer_back]), permute(to_row, grad_back))
 
 

time: 271 us -> 265 us (0.978)
  Pallas kernels: 141 us -> 130 us
  waiting for transfers between devices: 74.4 us -> 81.3 us
    ppermute x6, waiting for transfers between devices: 17.4 us -> 29.4 us  [body(): moved.append(lax.ppermute(far[at], 'col', perm))]
    pallas_call x10 -> x8, Pallas kernels: 82.5 us -> 72.6 us  [the longest x1 33.8 us: backward(): pl.pallas_call(functools.partial(backward_kernel, reads, shifts), out_sha...]
    all_to_all x6, waiting for transfers between devices: 36.8 us -> 31.6 us  [exchange(): lax.all_to_all(buffer, ('row', 'col'), split_axis=0, concat_axis=0, tiled...]
  transfers between devices with their start and end apart: 18 -> 18, of which waited for: 11 -> 11; matrix products, arithmetic and copies ran while one was open for 0% -> 0% of each run, Pallas kernels for 47% -> 44%
where the time goes in v4:
time: 265 us; the launch traced here: 264 us
  Pallas kernels  130 us (49%)
  waiting for transfers between devices  81.3 us (31%)
  starting transfers between devices  43.5 us (16%)
  local copies, waits for them, and re-layouts  8.18 us (3%)
    pallas_call x1, Pallas kernels, backward(): pl.pallas_call(functools.partial(backward_kernel, reads, shifts), out_sha...  33.8 us
    all_to_all x6, starting transfers between devices, exchange(): lax.all_to_all(buffer, ('row', 'col'), split_axis=0, concat_axis=0, tiled...  33.3 us
    all_to_all x6, waiting for transfers between devices, exchange(): lax.all_to_all(buffer, ('row', 'col'), split_axis=0, concat_axis=0, tiled...  31.6 us
    ppermute x6, waiting for transfers between devices, body(): moved.append(lax.ppermute(far[at], 'col', perm))  29.4 us
    ppermute x6, waiting for transfers between devices, forward_rows(): moved.append(lax.ppermute(outgoing[at], 'col', perm))  20.3 us
    pallas_call x1, Pallas kernels, forward(): pl.pallas_call(functools.partial(forward_kernel, reads), out_shape=(hbm((...  18.8 us
    pallas_call x3, Pallas kernels, permute(): pl.pallas_call(permute_kernel, out_shape=hbm((rows_dev, width), bf16), gr...  16 us
    pallas_call x3, Pallas kernels, send_permute(): pl.pallas_call(send_kernel, out_shape=hbm((rows_dev, piece), bf16), grid_...  13.9 us
  transfers between devices with their start and end apart: 18, of which 11 were waited for; matrix products, arithmetic and copies ran while one was open for 0% of the time, Pallas kernels for 44%

profile of v4, /device:TPU:0, one launch (start us, length us, event | category | flops | bytes accessed | tf_op | source)
XLA Modules:
  0.0 263.6 jit_solution(666927147170665678)
XLA Ops:
  1.6 4.2 %send_permute.3 = bf16[1024,512]{1,0:T(8,128)(2,1)} custom-call(s32[1]{0:T(128)} %bitcast.self_ref, s32[32,1024]{1,0:T(8,128)S(1)} %reshape.105.loader_ref, bf16[1024,1024]{1,0:T(8,128)(2,1)} %rows_ref.4), custom_call_target="tpu_custom_call" | custom-call | tf_op jit(solution)/shard_map/send_permute/pallas_call | solution.py:99
  5.8 7.3 %all-to-all-start = ((bf16[32,32,512]{2,1,0:T(8,128)(2,1)}), bf16[32,32,512]{2,1,0:T(8,128)(2,1)S(1)}, u32[]{:S(2)}, u32[]{:S(2)}) async-start(bf16[32,32,512]{2,1,0:T(8,128)(2,1)} %bitcast.24), calls=%async_computation | async-start | bytes 2097152 | tf_op jit(solution)/shard_map/all_to_all | solution.py:666
  13.1 5.7 %index_tables.1 = (bf16[1024,1024]{1,0:T(8,128)(2,1)}, bf16[1024,1024]{1,0:T(8,128)(2,1)}, bf16[1024,1024]{1,0:T(8,128)(2,1)}) custom-call(s32[1]{0:T(128)} %bitcast.self_ref, s32[32,1024]{1,0:T(8,128)S(1)} %reshape.105.loader_ref), custom_call_target="tpu_custom_call" | custom-call | tf_op jit(solution)/shard_map/index_tables/pallas_call | solution.py:153
  18.8 4.2 %send_permute.4 = bf16[1024,512]{1,0:T(8,128)(2,1)} custom-call(s32[1]{0:T(128)} %bitcast.self_ref, s32[32,1024]{1,0:T(8,128)S(1)} %reshape.105.loader_ref, bf16[1024,1024]{1,0:T(8,128)(2,1)} %rows_ref.4), custom_call_target="tpu_custom_call" | custom-call | tf_op jit(solution)/shard_map/send_permute/pallas_call | solution.py:99
  24.1 15.2 %all-to-all-done = bf16[32,32,512]{2,1,0:T(8,128)(2,1)S(1)} async-done(((bf16[32,32,512]{2,1,0:T(8,128)(2,1)}), bf16[32,32,512]{2,1,0:T(8,128)(2,1)S(1)}, u32[]{:S(2)}, u32[]{:S(2)}) %all-to-all-start) | async-done | bytes 1048608 | tf_op jit(solution)/shard_map/all_to_all | solution.py:666
  43.1 4.1 %outbound.2 = (bf16[256,512]{1,0:T(8,128)(2,1)}, bf16[256,512]{1,0:T(8,128)(2,1)}, bf16[256,512]{1,0:T(8,128)(2,1)}) custom-call(s32[6]{0:T(128)S(1)} %reshape.108.picks_ref, bf16[1024,1024]{1,0:T(8,128)(2,1)} %get-tuple-element.55.to_node_ref, bf16[1024,512]{1,0:T(8,128)(2,1)} %bitcast.19), custom_call_target="tpu_custom_call" | custom-call | tf_op jit(solution)/shard_map/outbound/pallas_call | solution.py:220
  50.4 5.6 %send_permute.5 = bf16[1024,1024]{1,0:T(8,128)(2,1)} custom-call(s32[1]{0:T(128)} %bitcast.self_ref, s32[32,1024]{1,0:T(8,128)S(1)} %reshape.105.loader_ref, bf16[1024,1024]{1,0:T(8,128)(2,1)} %rows_ref.5), custom_call_target="tpu_custom_call" | custom-call | tf_op jit(solution)/shard_map/send_permute/pallas_call | solution.py:99
  56.0 5.8 %collective-permute-done.refs_0_ = bf16[256,512]{1,0:T(8,128)(2,1)S(1)} collective-permute-done((bf16[256,512]{1,0:T(8,128)(2,1)}, bf16[256,512]{1,0:T(8,128)(2,1)S(1)}, u32[]{:S(2)}, u32[]{:S(2)}) %collective-permute-start) | collective-permute-done | bytes 262176 | tf_op jit(solution)/shard_map/ppermute | solution.py:690
  61.8 5.6 %collective-permute-done.2.refs_0_ = bf16[256,512]{1,0:T(8,128)(2,1)S(1)} collective-permute-done((bf16[256,512]{1,0:T(8,128)(2,1)}, bf16[256,512]{1,0:T(8,128)(2,1)S(1)}, u32[]{:S(2)}, u32[]{:S(2)}) %collective-permute-start.2) | collective-permute-done | bytes 262176 | tf_op jit(solution)/shard_map/ppermute | solution.py:690
  69.3 4.1 %outbound.3 = (bf16[256,512]{1,0:T(8,128)(2,1)}, bf16[256,512]{1,0:T(8,128)(2,1)}, bf16[256,512]{1,0:T(8,128)(2,1)}) custom-call(s32[6]{0:T(128)S(1)} %reshape.108.picks_ref, bf16[1024,1024]{1,0:T(8,128)(2,1)} %get-tuple-element.55.to_node_ref, bf16[1024,512]{1,0:T(8,128)(2,1)} %bitcast.6.refs_1_.rows_ref), custom_call_target="tpu_custom_call" | custom-call | tf_op jit(solution)/shard_map/outbound/pallas_call | solution.py:220
  83.7 12.1 %project.1 = (bf16[1024,1024]{1,0:T(8,128)(2,1)}, bf16[1792,1024]{1,0:T(8,128)(2,1)}, bf16[1792,1024]{1,0:T(8,128)(2,1)}) custom-call(bf16[1024,1024]{1,0:T(8,128)(2,1)} %get-tuple-element.55.to_node_ref, bf16[1024,1024]{1,0:T(8,128)(2,1)S(1)} %copy-done.9, bf16[1024,1024]{1,0:T(8,128)(2,1)S(1)} %copy-done.2, bf16[1024,1024]{1,0:T(8,128)(2,1)S(1)} %copy-done.4, ...), custom_call_target="tpu_custom_call" | custom-call | tf_op jit(solution)/shard_map/project/pallas_call | solution.py:249
  110.8 18.8 %forward.1 = (bf16[1024,1024]{1,0:T(8,128)(2,1)}, f32[1024,1024]{1,0:T(8,128)}, f32[128,128]{1,0:T(8,128)}) custom-call(s32[32]{0:T(128)S(1)} %reshape.109.entries_ref, bf16[1024,1024]{1,0:T(8,128)(2,1)} %get-tuple-element.63.q_ref, f32[1,1024]{1,0:T(1,128)S(1)} %bitcast.17, bf16[1024,1024]{1,0:T(8,128)(2,1)S(1)} %copy-done.6, ...), custom_call_target="tpu_custom_call" | custom-call | tf_op jit(solution)/shard_map/forward/pallas_call | solution.py:366
  129.7 8.9 %all-to-all-start.2 = ((bf16[32,32,1024]{2,1,0:T(8,128)(2,1)}), bf16[32,32,1024]{2,1,0:T(8,128)(2,1)}, u32[]{:S(2)}, u32[]{:S(2)}) async-start(bf16[32,32,1024]{2,1,0:T(8,128)(2,1)} %bitcast.27), calls=%async_computation.2 | async-start | bytes 4194304 | tf_op jit(solution)/shard_map/all_to_all | solution.py:666
  138.6 33.8 %backward.1 = (bf16[1024,1024]{1,0:T(8,128)(2,1)}, bf16[1024,1024]{1,0:T(8,128)(2,1)}, bf16[1024,1024]{1,0:T(8,128)(2,1)}, bf16[256,512]{1,0:T(8,128)(2,1)}, bf1...) custom-call(s32[32]{0:T(128)S(1)} %reshape.109.entries_ref, ...), custom_call_target="tpu_custom_call" | custom-call | tf_op jit(solution)/shard_map/backward/pallas_call | solution.py:527
  174.2 8.9 %own_project.1 = (f32[1024,512]{1,0:T(8,128)S(1)}, f32[1024,512]{1,0:T(8,128)S(1)}) custom-call(bf16[1024,1024]{1,0:T(8,128)(2,1)} %get-tuple-element.87.q_ref, bf16[1024,1024]{1,0:T(8,128)(2,1)} %get-tuple-element.88.k_ref, bf16[1024,1024]{1,0:T(8,128)(2,1)} %get-tuple-element.89.v_ref, bf16[1024,1024]{1,0:T(8,128)(2,1)S(1)} %copy-done.10, ...), custom_call_target="tpu_custom_call" | custom-call | tf_op jit(solution)/shard_map/own_project/pallas_call | solution.py:595
  184.4 6.1 %collective-permute-done.10.refs_1_ = bf16[256,512]{1,0:T(8,128)(2,1)S(1)} collective-permute-done((bf16[256,512]{1,0:T(8,128)(2,1)}, bf16[256,512]{1,0:T(8,128)(2,1)S(1)}, u32[]{:S(2)}, u32[]{:S(2)}) %collective-permute-start.10) | collective-permute-done | bytes 262176 | tf_op jit(solution)/shard_map/ppermute | solution.py:740
  193.5 4.9 %all-to-all-start.5 = ((bf16[32,32,512]{2,1,0:T(8,128)(2,1)}), bf16[32,32,512]{2,1,0:T(8,128)(2,1)S(1)}, u32[]{:S(2)}, u32[]{:S(2)}) async-start(bf16[32,32,512]{2,1,0:T(8,128)(2,1)} %bitcast.25), calls=%async_computation.5 | async-start | bytes 2097152 | tf_op jit(solution)/shard_map/all_to_all | solution.py:666
  200.5 14.4 %collective-permute-done.6.refs_0_ = bf16[256,512]{1,0:T(8,128)(2,1)S(1)} collective-permute-done((bf16[256,512]{1,0:T(8,128)(2,1)}, bf16[256,512]{1,0:T(8,128)(2,1)S(1)}, u32[]{:S(2)}, u32[]{:S(2)}) %collective-permute-start.6) | collective-permute-done | bytes 262176 | tf_op jit(solution)/shard_map/ppermute | solution.py:740
  214.9 8.8 %collective-permute-done.7.refs_1_ = bf16[256,512]{1,0:T(8,128)(2,1)S(1)} collective-permute-done((bf16[256,512]{1,0:T(8,128)(2,1)}, bf16[256,512]{1,0:T(8,128)(2,1)S(1)}, u32[]{:S(2)}, u32[]{:S(2)}) %collective-permute-start.7) | collective-permute-done | bytes 262176 | tf_op jit(solution)/shard_map/ppermute | solution.py:740
  228.3 4.8 %all-to-all-start.4 = ((bf16[32,32,512]{2,1,0:T(8,128)(2,1)}), bf16[32,32,512]{2,1,0:T(8,128)(2,1)}, u32[]{:S(2)}, u32[]{:S(2)}) async-start(bf16[32,32,512]{2,1,0:T(8,128)(2,1)} %bitcast.26), calls=%async_computation.4 | async-start | bytes 2097152 | tf_op jit(solution)/shard_map/all_to_all | solution.py:666
  233.1 7.5 %permute.3 = bf16[1024,1024]{1,0:T(8,128)(2,1)} custom-call(bf16[1024,1024]{1,0:T(8,128)(2,1)S(1)} %copy-done.8, bf16[1024,1024]{1,0:T(8,128)(2,1)} %bitcast.9.rows_ref), custom_call_target="tpu_custom_call" | custom-call | tf_op jit(solution)/shard_map/permute/pallas_call | solution.py:190
  240.6 4.2 %permute.4.refs_0_ = bf16[1024,1024]{1,0:T(8,128)(2,1)} custom-call(bf16[1024,1024]{1,0:T(8,128)(2,1)S(1)} %copy-done.8, bf16[1024,512]{1,0:T(8,128)(2,1)} %bitcast.22), custom_call_target="tpu_custom_call" | custom-call | tf_op jit(solution)/shard_map/permute/pallas_call | solution.py:190
  244.8 14.5 %all-to-all-done.4 = bf16[32,32,512]{2,1,0:T(8,128)(2,1)} async-done(((bf16[32,32,512]{2,1,0:T(8,128)(2,1)}), bf16[32,32,512]{2,1,0:T(8,128)(2,1)}, u32[]{:S(2)}, u32[]{:S(2)}) %all-to-all-start.4) | async-done | bytes 1048608 | tf_op jit(solution)/shard_map/all_to_all | solution.py:666
  259.3 4.3 %permute.5 = bf16[1024,1024]{1,0:T(8,128)(2,1)} custom-call(bf16[1024,1024]{1,0:T(8,128)(2,1)S(1)} %copy-done.8, bf16[1024,512]{1,0:T(8,128)(2,1)} %bitcast.13.rows_ref, bf16[1024,1024]{1,0:T(8,128)(2,1)} %permute.4.refs_0_), custom_call_target="tpu_custom_call", output_to_operand_aliasing={{}: (2, {})} | custom-call | tf_op jit(solution)/shard_map/permute/pallas_call | solution.py:190
  (83 shorter events, 49.0 us)
Async XLA Ops:
  0.6 22.3 %copy-start = (s32[32,4,2]{0,2,1:T(2,128)S(1)}, s32[32,4,2]{0,2,1:T(2,128)}, u32[]{:S(2)}) copy-start(s32[32,4,2]{0,2,1:T(2,128)} %param.16) | copy-start | bytes 3076
  5.8 33.5 %all-to-all-start = ((bf16[32,32,512]{2,1,0:T(8,128)(2,1)}), bf16[32,32,512]{2,1,0:T(8,128)(2,1)S(1)}, u32[]{:S(2)}, u32[]{:S(2)}) async-start(bf16[32,32,512]{2,1,0:T(8,128)(2,1)} %bitcast.24), calls=%async_computation | async-start | bytes 2097152 | tf_op jit(solution)/shard_map/all_to_all | solution.py:666
  39.3 30.0 %all-to-all-start.1 = ((bf16[32,32,512]{2,1,0:T(8,128)(2,1)}), bf16[32,32,512]{2,1,0:T(8,128)(2,1)}, u32[]{:S(2)}, u32[]{:S(2)}) async-start(bf16[32,32,512]{2,1,0:T(8,128)(2,1)} %bitcast.23), calls=%async_computation.1 | async-start | bytes 2097152 | tf_op jit(solution)/shard_map/all_to_all | solution.py:666
  47.2 14.5 %collective-permute-start = (bf16[256,512]{1,0:T(8,128)(2,1)}, bf16[256,512]{1,0:T(8,128)(2,1)S(1)}, u32[]{:S(2)}, u32[]{:S(2)}) collective-permute-start(bf16[256,512]{1,0:T(8,128)(2,1)} %get-tuple-element.59), channel_id=1, source_target_pairs={{0,1},{1,2},{2,3},{3,0},{4,5},{5,6},{6,7},{7,4},{8,9},{9,10},{10,1... | collective-permute-start | bytes 786440 | tf_op jit(solution)/shard_map/ppermute | solution.py:690
  47.4 14.4 %collective-permute-start.1 = (bf16[256,512]{1,0:T(8,128)(2,1)}, bf16[256,512]{1,0:T(8,128)(2,1)S(1)}, u32[]{:S(2)}, u32[]{:S(2)}) collective-permute-start(bf16[256,512]{1,0:T(8,128)(2,1)} %get-tuple-element.60), channel_id=1, source_target_pairs={{0,2},{1,3},{2,0},{3,1},{4,6},{5,7},{6,4},{7,5},{8,10},{9,11},{10,... | collective-permute-start | bytes 786440 | tf_op jit(solution)/shard_map/ppermute | solution.py:690
  49.1 18.3 %collective-permute-start.2 = (bf16[256,512]{1,0:T(8,128)(2,1)}, bf16[256,512]{1,0:T(8,128)(2,1)S(1)}, u32[]{:S(2)}, u32[]{:S(2)}) collective-permute-start(bf16[256,512]{1,0:T(8,128)(2,1)} %get-tuple-element.61), channel_id=1, source_target_pairs={{0,3},{1,0},{2,1},{3,2},{4,7},{5,4},{6,5},{7,6},{8,11},{9,8},{10,9... | collective-permute-start | bytes 786440 | tf_op jit(solution)/shard_map/ppermute | solution.py:690
  73.5 56.2 %all-to-all-start.3 = ((bf16[32,32,1024]{2,1,0:T(8,128)(2,1)}), bf16[32,32,1024]{2,1,0:T(8,128)(2,1)}, u32[]{:S(2)}, u32[]{:S(2)}) async-start(bf16[32,32,1024]{2,1,0:T(8,128)(2,1)} %bitcast.21), calls=%async_computation.3 | async-start | bytes 4194304 | tf_op jit(solution)/shard_map/all_to_all | solution.py:666
  77.3 21.3 %collective-permute-start.3 = (bf16[256,512]{1,0:T(8,128)(2,1)}, bf16[256,512]{1,0:T(8,128)(2,1)S(1)}, u32[]{:S(2)}, u32[]{:S(2)}) collective-permute-start(bf16[256,512]{1,0:T(8,128)(2,1)} %get-tuple-element.72), channel_id=1, source_target_pairs={{0,1},{1,2},{2,3},{3,0},{4,5},{5,6},{6,7},{7,4},{8,9},{9,10},{10,1... | collective-permute-start | bytes 786440 | tf_op jit(solution)/shard_map/ppermute | solution.py:690
  77.5 26.9 %collective-permute-start.4 = (bf16[256,512]{1,0:T(8,128)(2,1)S(1)}, bf16[256,512]{1,0:T(8,128)(2,1)S(1)}, u32[]{:S(2)}, u32[]{:S(2)}) collective-permute-start(bf16[256,512]{1,0:T(8,128)(2,1)S(1)} %copy-done.19), channel_id=1, source_target_pairs={{0,2},{1,3},{2,0},{3,1},{4,6},{5,7},{6,4},{7,5},{8,10},{9,11},{10,... | collective-permute-start | bytes 786440 | tf_op jit(solution)/shard_map/ppermute | solution.py:690
  79.2 29.6 %collective-permute-start.5 = (bf16[256,512]{1,0:T(8,128)(2,1)S(1)}, bf16[256,512]{1,0:T(8,128)(2,1)S(1)}, u32[]{:S(2)}, u32[]{:S(2)}) collective-permute-start(bf16[256,512]{1,0:T(8,128)(2,1)S(1)} %copy-done.18), channel_id=1, source_target_pairs={{0,3},{1,0},{2,1},{3,2},{4,7},{5,4},{6,5},{7,6},{8,11},{9,8},{10,9... | collective-permute-start | bytes 786440 | tf_op jit(solution)/shard_map/ppermute | solution.py:690
  129.7 63.9 %all-to-all-start.2 = ((bf16[32,32,1024]{2,1,0:T(8,128)(2,1)}), bf16[32,32,1024]{2,1,0:T(8,128)(2,1)}, u32[]{:S(2)}, u32[]{:S(2)}) async-start(bf16[32,32,1024]{2,1,0:T(8,128)(2,1)} %bitcast.27), calls=%async_computation.2 | async-start | bytes 4194304 | tf_op jit(solution)/shard_map/all_to_all | solution.py:666
  138.5 35.6 %copy-start.3 = (bf16[1024,1024]{1,0:T(8,128)(2,1)S(1)}, bf16[1024,1024]{1,0:T(8,128)(2,1)}, u32[]{:S(2)}) copy-start(bf16[1024,1024]{1,0:T(8,128)(2,1)} %wk_ref.9) | copy-start | bytes 6291460
  138.6 35.6 %copy-start.5 = (bf16[1024,1024]{1,0:T(8,128)(2,1)S(1)}, bf16[1024,1024]{1,0:T(8,128)(2,1)}, u32[]{:S(2)}) copy-start(bf16[1024,1024]{1,0:T(8,128)(2,1)} %wv_ref.9) | copy-start | bytes 6291460
  138.6 35.6 %copy-start.10 = (bf16[1024,1024]{1,0:T(8,128)(2,1)S(1)}, bf16[1024,1024]{1,0:T(8,128)(2,1)}, u32[]{:S(2)}) copy-start(bf16[1024,1024]{1,0:T(8,128)(2,1)} %wq_ref.3) | copy-start | bytes 6291460
  172.4 12.0 %collective-permute-start.9 = (bf16[256,512]{1,0:T(8,128)(2,1)}, bf16[256,512]{1,0:T(8,128)(2,1)S(1)}, u32[]{:S(2)}, u32[]{:S(2)}) collective-permute-start(bf16[256,512]{1,0:T(8,128)(2,1)} %get-tuple-element.95), channel_id=1, source_target_pairs={{0,3},{1,0},{2,1},{3,2},{4,7},{5,4},{6,5},{7,6},{8,11},{9,8},{10,9... | collective-permute-start | bytes 786440 | tf_op jit(solution)/shard_map/ppermute | solution.py:740
  173.7 16.8 %collective-permute-start.10 = (bf16[256,512]{1,0:T(8,128)(2,1)}, bf16[256,512]{1,0:T(8,128)(2,1)S(1)}, u32[]{:S(2)}, u32[]{:S(2)}) collective-permute-start(bf16[256,512]{1,0:T(8,128)(2,1)} %get-tuple-element.96), channel_id=1, source_target_pairs={{0,2},{1,3},{2,0},{3,1},{4,6},{5,7},{6,4},{7,5},{8,10},{9,11},{10,... | collective-permute-start | bytes 786440 | tf_op jit(solution)/shard_map/ppermute | solution.py:740
  174.1 16.4 %collective-permute-start.11 = (bf16[256,512]{1,0:T(8,128)(2,1)}, bf16[256,512]{1,0:T(8,128)(2,1)S(1)}, u32[]{:S(2)}, u32[]{:S(2)}) collective-permute-start(bf16[256,512]{1,0:T(8,128)(2,1)} %get-tuple-element.97), channel_id=1, source_target_pairs={{0,1},{1,2},{2,3},{3,0},{4,5},{5,6},{6,7},{7,4},{8,9},{9,10},{10,1... | collective-permute-start | bytes 786440 | tf_op jit(solution)/shard_map/ppermute | solution.py:740
  174.2 16.4 %copy-start.7 = (bf16[1024,1024]{1,0:T(8,128)(2,1)S(1)}, bf16[1024,1024]{1,0:T(8,128)(2,1)}, u32[]{:S(2)}) copy-start(bf16[1024,1024]{1,0:T(8,128)(2,1)} %get-tuple-element.64.from_node_ref) | copy-start | bytes 6291460
  193.5 34.8 %all-to-all-start.5 = ((bf16[32,32,512]{2,1,0:T(8,128)(2,1)}), bf16[32,32,512]{2,1,0:T(8,128)(2,1)S(1)}, u32[]{:S(2)}, u32[]{:S(2)}) async-start(bf16[32,32,512]{2,1,0:T(8,128)(2,1)} %bitcast.25), calls=%async_computation.5 | async-start | bytes 2097152 | tf_op jit(solution)/shard_map/all_to_all | solution.py:666
  198.4 16.5 %collective-permute-start.6 = (bf16[256,512]{1,0:T(8,128)(2,1)}, bf16[256,512]{1,0:T(8,128)(2,1)S(1)}, u32[]{:S(2)}, u32[]{:S(2)}) collective-permute-start(bf16[256,512]{1,0:T(8,128)(2,1)} %get-tuple-element.91), channel_id=1, source_target_pairs={{0,3},{1,0},{2,1},{3,2},{4,7},{5,4},{6,5},{7,6},{8,11},{9,8},{10,9... | collective-permute-start | bytes 786440 | tf_op jit(solution)/shard_map/ppermute | solution.py:740
  200.0 23.8 %collective-permute-start.7 = (bf16[256,512]{1,0:T(8,128)(2,1)}, bf16[256,512]{1,0:T(8,128)(2,1)S(1)}, u32[]{:S(2)}, u32[]{:S(2)}) collective-permute-start(bf16[256,512]{1,0:T(8,128)(2,1)} %get-tuple-element.92), channel_id=1, source_target_pairs={{0,2},{1,3},{2,0},{3,1},{4,6},{5,7},{6,4},{7,5},{8,10},{9,11},{10,... | collective-permute-start | bytes 786440 | tf_op jit(solution)/shard_map/ppermute | solution.py:740
  200.4 23.4 %collective-permute-start.8 = (bf16[256,512]{1,0:T(8,128)(2,1)S(1)}, bf16[256,512]{1,0:T(8,128)(2,1)S(1)}, u32[]{:S(2)}, u32[]{:S(2)}) collective-permute-start(bf16[256,512]{1,0:T(8,128)(2,1)S(1)} %copy-done.17), channel_id=1, source_target_pairs={{0,1},{1,2},{2,3},{3,0},{4,5},{5,6},{6,7},{7,4},{8,9},{9,10},{10,1... | collective-permute-start | bytes 786440 | tf_op jit(solution)/shard_map/ppermute | solution.py:740
  228.3 12.2 %copy-start.15 = (bf16[32,32,512]{2,1,0:T(8,128)(2,1)}, bf16[32,32,512]{2,1,0:T(8,128)(2,1)S(1)}, u32[]{:S(2)}) copy-start(bf16[32,32,512]{2,1,0:T(8,128)(2,1)S(1)} %all-to-all-done.5) | copy-start | bytes 3145732
  228.3 31.0 %all-to-all-start.4 = ((bf16[32,32,512]{2,1,0:T(8,128)(2,1)}), bf16[32,32,512]{2,1,0:T(8,128)(2,1)}, u32[]{:S(2)}, u32[]{:S(2)}) async-start(bf16[32,32,512]{2,1,0:T(8,128)(2,1)} %bitcast.26), calls=%async_computation.4 | async-start | bytes 2097152 | tf_op jit(solution)/shard_map/all_to_all | solution.py:666
  (14 other events, 57.5 us)

commit v5 on v4

--- a/solution.py
+++ b/solution.py
@@ -206,29 +206,33 @@
     return out[0]
 
 
-def outbound_kernel(capacity, block, picks_ref, to_node_ref, rows_ref, *out_refs):
-    for at, out_ref in enumerate(out_refs):
-        for slot in range(capacity):
-            start = pl.multiple_of(jnp.maximum(picks_ref[at * capacity + slot], 0) * block, block)
-            picked = matmul(to_node_ref[pl.ds(start, block), :], rows_ref[...])
-            out_ref[slot * block : (slot + 1) * block, :] = picked.astype(bf16)
+def outbound_kernel(picks_ref, rows_ref, *refs):
+    pick_refs, out_refs = refs[: len(refs) // 2], refs[len(refs) // 2 :]
+    for pick_ref, out_ref in zip(pick_refs, out_refs):
+        out_ref[...] = matmul(pick_ref[...], rows_ref[...]).astype(bf16)
 
 
 def outbound_blocks(picks, to_node, rows, shifts, capacity, block):
-    width = rows.shape[1]
-    shape = (capacity * block, width)
+    rows_dev, width = rows.shape
+
+    def pick_spec(shift):
+        def index(slot, picks):
+            return jnp.maximum(picks[shift * capacity + slot], 0), 0
+
+        return pl.BlockSpec((block, rows_dev), index)
+
     return pl.pallas_call(
-        functools.partial(outbound_kernel, capacity, block),
-        out_shape=[hbm(shape, bf16)] * shifts,
+        outbound_kernel,
+        out_shape=[hbm((capacity * block, width), bf16)] * len(shifts),
         grid_spec=pltpu.PrefetchScalarGridSpec(
             num_scalar_prefetch=1,
-            grid=(1,),
-            in_specs=[whole(to_node.shape), whole(rows.shape)],
-            out_specs=[whole(shape)] * shifts,
+            grid=(capacity,),
+            in_specs=[whole(rows.shape)] + [pick_spec(shift) for shift in shifts],
+            out_specs=[pl.BlockSpec((block, width), lambda i, _: (i, 0))] * len(shifts),
         ),
-        compiler_params=params(12),
+        compiler_params=params(16),
         name="outbound",
-    )(picks, pin(to_node), pin(rows))
+    )(picks, pin(rows), *[pin(to_node)] * len(shifts))
 
 
 def project_kernel(to_node_ref, wq_ref, wk_ref, wv_ref, *refs):
@@ -321,7 +325,8 @@
     *refs,
 ):
     k_refs, v_refs = refs[:reads], refs[reads : 2 * reads]
-    out_ref, mixed_ref, stats_ref, layer_ref, score_ref, prob_ref = refs[2 * reads :]
+    out_hbm, mixed_ref, stats_ref, layer_ref, score_ref, prob_ref = refs[2 * reads : -2]
+    out_ref, out_sem = refs[-2:]
     block, width = q_ref.shape
     step = pl.program_id(0)
     keys = reads * block
@@ -358,7 +363,19 @@
 
     @pl.when(step == pl.num_programs(0) - 1)
     def _():
-        out_ref[...] = matmul(from_node_ref[...], layer_ref[...]).astype(bf16)
+        chunk = 2 * block
+        saves = []
+        for at in range(0, out_ref.shape[0], chunk):
+            part = slice(at, at + chunk)
+            out_ref[part, :] = matmul(from_node_ref[part, :], layer_ref[...]).astype(bf16)
+            saves.append(
+                pltpu.make_async_copy(
+                    out_ref.at[part, :], out_hbm.at[part, :], out_sem.at[at // chunk]
+                )
+            )
+            saves[-1].start()
+        for save in saves:
+            save.wait()
 
 
 def forward(entries, queries, k_table, v_table, gain, from_node, block, reads):
@@ -380,7 +397,7 @@
             ]
             + entry_specs(block, width, reads) * 2,
             out_specs=(
-                whole((rows_dev, width)),
+                pl.BlockSpec(memory_space=pl.ANY),
                 pl.BlockSpec((block, width), lambda i, _: (i, 0)),
                 pl.BlockSpec((2 * HEADS, block), lambda i, _: (i, 0)),
             ),
@@ -388,6 +405,8 @@
                 pltpu.VMEM((rows_dev, width), bf16),
                 pltpu.VMEM((HEADS, reads * block, block), f32),
                 pltpu.VMEM((HEADS, reads * block, block), bf16),
+                pltpu.VMEM((rows_dev, width), bf16),
+                pltpu.SemaphoreType.DMA((rows_dev // (2 * block),)),
             ],
         ),
         compiler_params=params(32),
@@ -683,24 +702,22 @@
     rows, to_node, from_node, to_row, picks, entries, others = lax.optimization_barrier(
         (rows, to_node, from_node, to_row, picks, entries, others)
     )
-    def forward_rows(outgoing):
-        moved = []
-        for at in range(shifts):
-            perm = [(c, (c + at + 1) % col_count) for c in range(col_count)]
-            moved.append(lax.ppermute(outgoing[at], "col", perm))
-        return moved
-
+    def forward_rows(outgoing, at):
+        perm = [(c, (c + at + 1) % col_count) for c in range(col_count)]
+        return lax.ppermute(outgoing, "col", perm)
+
+    every = list(range(shifts))
     feature_rows = [rows]
-    outgoing = outbound_blocks(picks, to_node, rows, shifts, capacity, block)
-    arrived = [forward_rows(outgoing)]
+    outgoing = outbound_blocks(picks, to_node, rows, every, capacity, block)
+    arrived = [[forward_rows(outgoing[at], at) for at in every]]
     cot_out = send_permute(self_id, loader, cotangent, 1, 0)
     for other in others:
         rows = exchange(other)
         rows, cot_out, arrived = lax.optimization_barrier((rows, cot_out, arrived))
         feature_rows.append(rows)
-        outgoing = outbound_blocks(picks, to_node, rows, shifts, capacity, block)
+        outgoing = outbound_blocks(picks, to_node, rows, every, capacity, block)
         cot_out, outgoing = lax.optimization_barrier((cot_out, outgoing))
-        arrived.append(forward_rows(outgoing))
+        arrived.append([forward_rows(outgoing[at], at) for at in every])
     cot_rows = exchange(cot_out)
 
     queries, k_table, v_table = project(

time: 265 us -> 265 us (level)
  no operation moved by 1% of the time
where the time goes in v5:
time: 265 us; the launch traced here: 264 us
  Pallas kernels  129 us (49%)
  waiting for transfers between devices  81.4 us (31%)
  starting transfers between devices  43.8 us (17%)
  local copies, waits for them, and re-layouts  8.18 us (3%)
    pallas_call x1, Pallas kernels, backward(): pl.pallas_call(functools.partial(backward_kernel, reads, shifts), out_sha...  33.8 us
    all_to_all x6, starting transfers between devices, exchange(): lax.all_to_all(buffer, ('row', 'col'), split_axis=0, concat_axis=0, tiled...  33.4 us
    all_to_all x6, waiting for transfers between devices, exchange(): lax.all_to_all(buffer, ('row', 'col'), split_axis=0, concat_axis=0, tiled...  31.6 us
    ppermute x6, waiting for transfers between devices, body(): moved.append(lax.ppermute(far[at], 'col', perm))  29.3 us
    ppermute x6, waiting for transfers between devices, forward_rows(): return lax.ppermute(outgoing, 'col', perm)  20.4 us
    pallas_call x1, Pallas kernels, forward(): pl.pallas_call(functools.partial(forward_kernel, reads), out_shape=(hbm((...  19 us
    pallas_call x3, Pallas kernels, permute(): pl.pallas_call(permute_kernel, out_shape=hbm((rows_dev, width), bf16), gr...  15.9 us
    pallas_call x3, Pallas kernels, send_permute(): pl.pallas_call(send_kernel, out_shape=hbm((rows_dev, piece), bf16), grid_...  13.9 us
  transfers between devices with their start and end apart: 18, of which 11 were waited for; matrix products, arithmetic and copies ran while one was open for 0% of the time, Pallas kernels for 44%

profile of v5, /device:TPU:0, one launch (start us, length us, event | category | flops | bytes accessed | tf_op | source)
XLA Modules:
  0.0 263.6 jit_solution(5826105707569024396)
XLA Ops:
  1.6 4.2 %send_permute.3 = bf16[1024,512]{1,0:T(8,128)(2,1)} custom-call(s32[1]{0:T(128)} %bitcast.self_ref, s32[32,1024]{1,0:T(8,128)S(1)} %reshape.105.loader_ref, bf16[1024,1024]{1,0:T(8,128)(2,1)} %rows_ref.4), custom_call_target="tpu_custom_call" | custom-call | tf_op jit(solution)/shard_map/send_permute/pallas_call | solution.py:99
  5.8 7.3 %all-to-all-start = ((bf16[32,32,512]{2,1,0:T(8,128)(2,1)}), bf16[32,32,512]{2,1,0:T(8,128)(2,1)S(1)}, u32[]{:S(2)}, u32[]{:S(2)}) async-start(bf16[32,32,512]{2,1,0:T(8,128)(2,1)} %bitcast.24), calls=%async_computation | async-start | bytes 2097152 | tf_op jit(solution)/shard_map/all_to_all | solution.py:685
  13.1 5.7 %index_tables.1 = (bf16[1024,1024]{1,0:T(8,128)(2,1)}, bf16[1024,1024]{1,0:T(8,128)(2,1)}, bf16[1024,1024]{1,0:T(8,128)(2,1)}) custom-call(s32[1]{0:T(128)} %bitcast.self_ref, s32[32,1024]{1,0:T(8,128)S(1)} %reshape.105.loader_ref), custom_call_target="tpu_custom_call" | custom-call | tf_op jit(solution)/shard_map/index_tables/pallas_call | solution.py:153
  18.8 4.2 %send_permute.4 = bf16[1024,512]{1,0:T(8,128)(2,1)} custom-call(s32[1]{0:T(128)} %bitcast.self_ref, s32[32,1024]{1,0:T(8,128)S(1)} %reshape.105.loader_ref, bf16[1024,1024]{1,0:T(8,128)(2,1)} %rows_ref.4), custom_call_target="tpu_custom_call" | custom-call | tf_op jit(solution)/shard_map/send_permute/pallas_call | solution.py:99
  24.1 15.2 %all-to-all-done = bf16[32,32,512]{2,1,0:T(8,128)(2,1)S(1)} async-done(((bf16[32,32,512]{2,1,0:T(8,128)(2,1)}), bf16[32,32,512]{2,1,0:T(8,128)(2,1)S(1)}, u32[]{:S(2)}, u32[]{:S(2)}) %all-to-all-start) | async-done | bytes 1048608 | tf_op jit(solution)/shard_map/all_to_all | solution.py:685
  43.1 3.9 %outbound.2 = (bf16[256,512]{1,0:T(8,128)(2,1)}, bf16[256,512]{1,0:T(8,128)(2,1)}, bf16[256,512]{1,0:T(8,128)(2,1)}) custom-call(s32[6]{0:T(128)S(1)} %reshape.108.picks_ref, bf16[1024,512]{1,0:T(8,128)(2,1)} %bitcast.19, bf16[1024,1024]{1,0:T(8,128)(2,1)} %get-tuple-element.55.refs_0_.refs_1_.refs_2_.to_node_ref, ...), custom_call_target="tpu_custom_call" | custom-call | tf_op jit(solution)/shard_map/outbound/pallas_call | solution.py:224
  50.3 5.6 %send_permute.5 = bf16[1024,1024]{1,0:T(8,128)(2,1)} custom-call(s32[1]{0:T(128)} %bitcast.self_ref, s32[32,1024]{1,0:T(8,128)S(1)} %reshape.105.loader_ref, bf16[1024,1024]{1,0:T(8,128)(2,1)} %rows_ref.5), custom_call_target="tpu_custom_call" | custom-call | tf_op jit(solution)/shard_map/send_permute/pallas_call | solution.py:99
  55.8 5.9 %collective-permute-done.refs_0_ = bf16[256,512]{1,0:T(8,128)(2,1)S(1)} collective-permute-done((bf16[256,512]{1,0:T(8,128)(2,1)}, bf16[256,512]{1,0:T(8,128)(2,1)S(1)}, u32[]{:S(2)}, u32[]{:S(2)}) %collective-permute-start) | collective-permute-done | bytes 262176 | tf_op jit(solution)/shard_map/ppermute | solution.py:707
  61.8 5.6 %collective-permute-done.2.refs_0_ = bf16[256,512]{1,0:T(8,128)(2,1)S(1)} collective-permute-done((bf16[256,512]{1,0:T(8,128)(2,1)}, bf16[256,512]{1,0:T(8,128)(2,1)S(1)}, u32[]{:S(2)}, u32[]{:S(2)}) %collective-permute-start.2) | collective-permute-done | bytes 262176 | tf_op jit(solution)/shard_map/ppermute | solution.py:707
  69.3 3.9 %outbound.3 = (bf16[256,512]{1,0:T(8,128)(2,1)}, bf16[256,512]{1,0:T(8,128)(2,1)}, bf16[256,512]{1,0:T(8,128)(2,1)}) custom-call(s32[6]{0:T(128)S(1)} %reshape.108.picks_ref, bf16[1024,512]{1,0:T(8,128)(2,1)} %bitcast.6.refs_1_.rows_ref, bf16[1024,1024]{1,0:T(8,128)(2,1)} %get-tuple-element.55.refs_0_.refs_1_.refs_2_.to_node_ref, ...), custom_call_target="tpu_custom_call" | custom-call | tf_op jit(solution)/shard_map/outbound/pallas_call | solution.py:224
  83.5 12.1 %project.1 = (bf16[1024,1024]{1,0:T(8,128)(2,1)}, bf16[1792,1024]{1,0:T(8,128)(2,1)}, bf16[1792,1024]{1,0:T(8,128)(2,1)}) custom-call(bf16[1024,1024]{1,0:T(8,128)(2,1)} %get-tuple-element.55.refs_0_.refs_1_.refs_2_.to_node_ref, bf16[1024,1024]{1,0:T(8,128)(2,1)S(1)} %copy-done.9, bf16[1024,1024]{1,0:T(8,128)(2,1)S(1)} %copy-done.2, ...), custom_call_target="tpu_custom_call" | custom-call | tf_op jit(solution)/shard_map/project/pallas_call | solution.py:253
  110.7 19.0 %forward.1 = (bf16[1024,1024]{1,0:T(8,128)(2,1)}, f32[1024,1024]{1,0:T(8,128)}, f32[128,128]{1,0:T(8,128)}) custom-call(s32[32]{0:T(128)S(1)} %reshape.109.entries_ref, bf16[1024,1024]{1,0:T(8,128)(2,1)} %get-tuple-element.63.q_ref, f32[1,1024]{1,0:T(1,128)S(1)} %bitcast.17, bf16[1024,1024]{1,0:T(8,128)(2,1)S(1)} %copy-done.6, ...), custom_call_target="tpu_custom_call" | custom-call | tf_op jit(solution)/shard_map/forward/pallas_call | solution.py:383
  129.7 8.9 %all-to-all-start.2 = ((bf16[32,32,1024]{2,1,0:T(8,128)(2,1)}), bf16[32,32,1024]{2,1,0:T(8,128)(2,1)}, u32[]{:S(2)}, u32[]{:S(2)}) async-start(bf16[32,32,1024]{2,1,0:T(8,128)(2,1)} %bitcast.27), calls=%async_computation.2 | async-start | bytes 4194304 | tf_op jit(solution)/shard_map/all_to_all | solution.py:685
  138.6 33.8 %backward.1 = (bf16[1024,1024]{1,0:T(8,128)(2,1)}, bf16[1024,1024]{1,0:T(8,128)(2,1)}, bf16[1024,1024]{1,0:T(8,128)(2,1)}, bf16[256,512]{1,0:T(8,128)(2,1)}, bf1...) custom-call(s32[32]{0:T(128)S(1)} %reshape.109.entries_ref, ...), custom_call_target="tpu_custom_call" | custom-call | tf_op jit(solution)/shard_map/backward/pallas_call | solution.py:546
  174.3 8.9 %own_project.1 = (f32[1024,512]{1,0:T(8,128)S(1)}, f32[1024,512]{1,0:T(8,128)S(1)}) custom-call(bf16[1024,1024]{1,0:T(8,128)(2,1)} %get-tuple-element.87.q_ref, bf16[1024,1024]{1,0:T(8,128)(2,1)} %get-tuple-element.88.k_ref, bf16[1024,1024]{1,0:T(8,128)(2,1)} %get-tuple-element.89.v_ref, bf16[1024,1024]{1,0:T(8,128)(2,1)S(1)} %copy-done.10, ...), custom_call_target="tpu_custom_call" | custom-call | tf_op jit(solution)/shard_map/own_project/pallas_call | solution.py:614
  184.5 6.1 %collective-permute-done.10.refs_1_ = bf16[256,512]{1,0:T(8,128)(2,1)S(1)} collective-permute-done((bf16[256,512]{1,0:T(8,128)(2,1)}, bf16[256,512]{1,0:T(8,128)(2,1)S(1)}, u32[]{:S(2)}, u32[]{:S(2)}) %collective-permute-start.10) | collective-permute-done | bytes 262176 | tf_op jit(solution)/shard_map/ppermute | solution.py:757
  193.6 4.9 %all-to-all-start.5 = ((bf16[32,32,512]{2,1,0:T(8,128)(2,1)}), bf16[32,32,512]{2,1,0:T(8,128)(2,1)S(1)}, u32[]{:S(2)}, u32[]{:S(2)}) async-start(bf16[32,32,512]{2,1,0:T(8,128)(2,1)} %bitcast.25), calls=%async_computation.5 | async-start | bytes 2097152 | tf_op jit(solution)/shard_map/all_to_all | solution.py:685
  200.5 14.4 %collective-permute-done.6.refs_0_ = bf16[256,512]{1,0:T(8,128)(2,1)S(1)} collective-permute-done((bf16[256,512]{1,0:T(8,128)(2,1)}, bf16[256,512]{1,0:T(8,128)(2,1)S(1)}, u32[]{:S(2)}, u32[]{:S(2)}) %collective-permute-start.6) | collective-permute-done | bytes 262176 | tf_op jit(solution)/shard_map/ppermute | solution.py:757
  215.0 8.8 %collective-permute-done.7.refs_1_ = bf16[256,512]{1,0:T(8,128)(2,1)S(1)} collective-permute-done((bf16[256,512]{1,0:T(8,128)(2,1)}, bf16[256,512]{1,0:T(8,128)(2,1)S(1)}, u32[]{:S(2)}, u32[]{:S(2)}) %collective-permute-start.7) | collective-permute-done | bytes 262176 | tf_op jit(solution)/shard_map/ppermute | solution.py:757
  228.4 4.7 %all-to-all-start.4 = ((bf16[32,32,512]{2,1,0:T(8,128)(2,1)}), bf16[32,32,512]{2,1,0:T(8,128)(2,1)}, u32[]{:S(2)}, u32[]{:S(2)}) async-start(bf16[32,32,512]{2,1,0:T(8,128)(2,1)} %bitcast.26), calls=%async_computation.4 | async-start | bytes 2097152 | tf_op jit(solution)/shard_map/all_to_all | solution.py:685
  233.1 7.4 %permute.3 = bf16[1024,1024]{1,0:T(8,128)(2,1)} custom-call(bf16[1024,1024]{1,0:T(8,128)(2,1)S(1)} %copy-done.8, bf16[1024,1024]{1,0:T(8,128)(2,1)} %bitcast.9.rows_ref), custom_call_target="tpu_custom_call" | custom-call | tf_op jit(solution)/shard_map/permute/pallas_call | solution.py:190
  240.6 4.2 %permute.4.refs_0_ = bf16[1024,1024]{1,0:T(8,128)(2,1)} custom-call(bf16[1024,1024]{1,0:T(8,128)(2,1)S(1)} %copy-done.8, bf16[1024,512]{1,0:T(8,128)(2,1)} %bitcast.22), custom_call_target="tpu_custom_call" | custom-call | tf_op jit(solution)/shard_map/permute/pallas_call | solution.py:190
  244.8 14.5 %all-to-all-done.4 = bf16[32,32,512]{2,1,0:T(8,128)(2,1)} async-done(((bf16[32,32,512]{2,1,0:T(8,128)(2,1)}), bf16[32,32,512]{2,1,0:T(8,128)(2,1)}, u32[]{:S(2)}, u32[]{:S(2)}) %all-to-all-start.4) | async-done | bytes 1048608 | tf_op jit(solution)/shard_map/all_to_all | solution.py:685
  259.3 4.3 %permute.5 = bf16[1024,1024]{1,0:T(8,128)(2,1)} custom-call(bf16[1024,1024]{1,0:T(8,128)(2,1)S(1)} %copy-done.8, bf16[1024,512]{1,0:T(8,128)(2,1)} %bitcast.13.rows_ref, bf16[1024,1024]{1,0:T(8,128)(2,1)} %permute.4.refs_0_), custom_call_target="tpu_custom_call", output_to_operand_aliasing={{}: (2, {})} | custom-call | tf_op jit(solution)/shard_map/permute/pallas_call | solution.py:190
  (83 shorter events, 49.2 us)
Async XLA Ops:
  0.6 22.3 %copy-start = (s32[32,4,2]{0,2,1:T(2,128)S(1)}, s32[32,4,2]{0,2,1:T(2,128)}, u32[]{:S(2)}) copy-start(s32[32,4,2]{0,2,1:T(2,128)} %param.16) | copy-start | bytes 3076
  5.8 33.5 %all-to-all-start = ((bf16[32,32,512]{2,1,0:T(8,128)(2,1)}), bf16[32,32,512]{2,1,0:T(8,128)(2,1)S(1)}, u32[]{:S(2)}, u32[]{:S(2)}) async-start(bf16[32,32,512]{2,1,0:T(8,128)(2,1)} %bitcast.24), calls=%async_computation | async-start | bytes 2097152 | tf_op jit(solution)/shard_map/all_to_all | solution.py:685
  39.3 30.0 %all-to-all-start.1 = ((bf16[32,32,512]{2,1,0:T(8,128)(2,1)}), bf16[32,32,512]{2,1,0:T(8,128)(2,1)}, u32[]{:S(2)}, u32[]{:S(2)}) async-start(bf16[32,32,512]{2,1,0:T(8,128)(2,1)} %bitcast.23), calls=%async_computation.1 | async-start | bytes 2097152 | tf_op jit(solution)/shard_map/all_to_all | solution.py:685
  47.0 14.8 %collective-permute-start = (bf16[256,512]{1,0:T(8,128)(2,1)}, bf16[256,512]{1,0:T(8,128)(2,1)S(1)}, u32[]{:S(2)}, u32[]{:S(2)}) collective-permute-start(bf16[256,512]{1,0:T(8,128)(2,1)} %get-tuple-element.59), channel_id=1, source_target_pairs={{0,1},{1,2},{2,3},{3,0},{4,5},{5,6},{6,7},{7,4},{8,9},{9,10},{10,1... | collective-permute-start | bytes 786440 | tf_op jit(solution)/shard_map/ppermute | solution.py:707
  47.2 14.6 %collective-permute-start.1 = (bf16[256,512]{1,0:T(8,128)(2,1)}, bf16[256,512]{1,0:T(8,128)(2,1)S(1)}, u32[]{:S(2)}, u32[]{:S(2)}) collective-permute-start(bf16[256,512]{1,0:T(8,128)(2,1)} %get-tuple-element.60), channel_id=1, source_target_pairs={{0,2},{1,3},{2,0},{3,1},{4,6},{5,7},{6,4},{7,5},{8,10},{9,11},{10,... | collective-permute-start | bytes 786440 | tf_op jit(solution)/shard_map/ppermute | solution.py:707
  48.9 18.4 %collective-permute-start.2 = (bf16[256,512]{1,0:T(8,128)(2,1)}, bf16[256,512]{1,0:T(8,128)(2,1)S(1)}, u32[]{:S(2)}, u32[]{:S(2)}) collective-permute-start(bf16[256,512]{1,0:T(8,128)(2,1)} %get-tuple-element.61), channel_id=1, source_target_pairs={{0,3},{1,0},{2,1},{3,2},{4,7},{5,4},{6,5},{7,6},{8,11},{9,8},{10,9... | collective-permute-start | bytes 786440 | tf_op jit(solution)/shard_map/ppermute | solution.py:707
  73.2 56.4 %all-to-all-start.3 = ((bf16[32,32,1024]{2,1,0:T(8,128)(2,1)}), bf16[32,32,1024]{2,1,0:T(8,128)(2,1)}, u32[]{:S(2)}, u32[]{:S(2)}) async-start(bf16[32,32,1024]{2,1,0:T(8,128)(2,1)} %bitcast.21), calls=%async_computation.3 | async-start | bytes 4194304 | tf_op jit(solution)/shard_map/all_to_all | solution.py:685
  77.1 21.3 %collective-permute-start.3 = (bf16[256,512]{1,0:T(8,128)(2,1)}, bf16[256,512]{1,0:T(8,128)(2,1)S(1)}, u32[]{:S(2)}, u32[]{:S(2)}) collective-permute-start(bf16[256,512]{1,0:T(8,128)(2,1)} %get-tuple-element.72), channel_id=1, source_target_pairs={{0,1},{1,2},{2,3},{3,0},{4,5},{5,6},{6,7},{7,4},{8,9},{9,10},{10,1... | collective-permute-start | bytes 786440 | tf_op jit(solution)/shard_map/ppermute | solution.py:707
  77.4 26.9 %collective-permute-start.4 = (bf16[256,512]{1,0:T(8,128)(2,1)S(1)}, bf16[256,512]{1,0:T(8,128)(2,1)S(1)}, u32[]{:S(2)}, u32[]{:S(2)}) collective-permute-start(bf16[256,512]{1,0:T(8,128)(2,1)S(1)} %copy-done.19), channel_id=1, source_target_pairs={{0,2},{1,3},{2,0},{3,1},{4,6},{5,7},{6,4},{7,5},{8,10},{9,11},{10,... | collective-permute-start | bytes 786440 | tf_op jit(solution)/shard_map/ppermute | solution.py:707
  79.0 29.6 %collective-permute-start.5 = (bf16[256,512]{1,0:T(8,128)(2,1)S(1)}, bf16[256,512]{1,0:T(8,128)(2,1)S(1)}, u32[]{:S(2)}, u32[]{:S(2)}) collective-permute-start(bf16[256,512]{1,0:T(8,128)(2,1)S(1)} %copy-done.18), channel_id=1, source_target_pairs={{0,3},{1,0},{2,1},{3,2},{4,7},{5,4},{6,5},{7,6},{8,11},{9,8},{10,9... | collective-permute-start | bytes 786440 | tf_op jit(solution)/shard_map/ppermute | solution.py:707
  129.7 63.9 %all-to-all-start.2 = ((bf16[32,32,1024]{2,1,0:T(8,128)(2,1)}), bf16[32,32,1024]{2,1,0:T(8,128)(2,1)}, u32[]{:S(2)}, u32[]{:S(2)}) async-start(bf16[32,32,1024]{2,1,0:T(8,128)(2,1)} %bitcast.27), calls=%async_computation.2 | async-start | bytes 4194304 | tf_op jit(solution)/shard_map/all_to_all | solution.py:685
  138.6 35.7 %copy-start.3 = (bf16[1024,1024]{1,0:T(8,128)(2,1)S(1)}, bf16[1024,1024]{1,0:T(8,128)(2,1)}, u32[]{:S(2)}) copy-start(bf16[1024,1024]{1,0:T(8,128)(2,1)} %wk_ref.9) | copy-start | bytes 6291460
  138.6 35.7 %copy-start.5 = (bf16[1024,1024]{1,0:T(8,128)(2,1)S(1)}, bf16[1024,1024]{1,0:T(8,128)(2,1)}, u32[]{:S(2)}) copy-start(bf16[1024,1024]{1,0:T(8,128)(2,1)} %wv_ref.9) | copy-start | bytes 6291460
  138.6 35.7 %copy-start.10 = (bf16[1024,1024]{1,0:T(8,128)(2,1)S(1)}, bf16[1024,1024]{1,0:T(8,128)(2,1)}, u32[]{:S(2)}) copy-start(bf16[1024,1024]{1,0:T(8,128)(2,1)} %wq_ref.3) | copy-start | bytes 6291460
  172.5 12.1 %collective-permute-start.9 = (bf16[256,512]{1,0:T(8,128)(2,1)}, bf16[256,512]{1,0:T(8,128)(2,1)S(1)}, u32[]{:S(2)}, u32[]{:S(2)}) collective-permute-start(bf16[256,512]{1,0:T(8,128)(2,1)} %get-tuple-element.95), channel_id=1, source_target_pairs={{0,3},{1,0},{2,1},{3,2},{4,7},{5,4},{6,5},{7,6},{8,11},{9,8},{10,9... | collective-permute-start | bytes 786440 | tf_op jit(solution)/shard_map/ppermute | solution.py:757
  173.8 16.8 %collective-permute-start.10 = (bf16[256,512]{1,0:T(8,128)(2,1)}, bf16[256,512]{1,0:T(8,128)(2,1)S(1)}, u32[]{:S(2)}, u32[]{:S(2)}) collective-permute-start(bf16[256,512]{1,0:T(8,128)(2,1)} %get-tuple-element.96), channel_id=1, source_target_pairs={{0,2},{1,3},{2,0},{3,1},{4,6},{5,7},{6,4},{7,5},{8,10},{9,11},{10,... | collective-permute-start | bytes 786440 | tf_op jit(solution)/shard_map/ppermute | solution.py:757
  174.1 16.5 %collective-permute-start.11 = (bf16[256,512]{1,0:T(8,128)(2,1)}, bf16[256,512]{1,0:T(8,128)(2,1)S(1)}, u32[]{:S(2)}, u32[]{:S(2)}) collective-permute-start(bf16[256,512]{1,0:T(8,128)(2,1)} %get-tuple-element.97), channel_id=1, source_target_pairs={{0,1},{1,2},{2,3},{3,0},{4,5},{5,6},{6,7},{7,4},{8,9},{9,10},{10,1... | collective-permute-start | bytes 786440 | tf_op jit(solution)/shard_map/ppermute | solution.py:757
  174.3 16.3 %copy-start.7 = (bf16[1024,1024]{1,0:T(8,128)(2,1)S(1)}, bf16[1024,1024]{1,0:T(8,128)(2,1)}, u32[]{:S(2)}) copy-start(bf16[1024,1024]{1,0:T(8,128)(2,1)} %get-tuple-element.64.from_node_ref) | copy-start | bytes 6291460
  193.6 34.8 %all-to-all-start.5 = ((bf16[32,32,512]{2,1,0:T(8,128)(2,1)}), bf16[32,32,512]{2,1,0:T(8,128)(2,1)S(1)}, u32[]{:S(2)}, u32[]{:S(2)}) async-start(bf16[32,32,512]{2,1,0:T(8,128)(2,1)} %bitcast.25), calls=%async_computation.5 | async-start | bytes 2097152 | tf_op jit(solution)/shard_map/all_to_all | solution.py:685
  198.5 16.5 %collective-permute-start.6 = (bf16[256,512]{1,0:T(8,128)(2,1)}, bf16[256,512]{1,0:T(8,128)(2,1)S(1)}, u32[]{:S(2)}, u32[]{:S(2)}) collective-permute-start(bf16[256,512]{1,0:T(8,128)(2,1)} %get-tuple-element.91), channel_id=1, source_target_pairs={{0,3},{1,0},{2,1},{3,2},{4,7},{5,4},{6,5},{7,6},{8,11},{9,8},{10,9... | collective-permute-start | bytes 786440 | tf_op jit(solution)/shard_map/ppermute | solution.py:757
  200.0 23.8 %collective-permute-start.7 = (bf16[256,512]{1,0:T(8,128)(2,1)}, bf16[256,512]{1,0:T(8,128)(2,1)S(1)}, u32[]{:S(2)}, u32[]{:S(2)}) collective-permute-start(bf16[256,512]{1,0:T(8,128)(2,1)} %get-tuple-element.92), channel_id=1, source_target_pairs={{0,2},{1,3},{2,0},{3,1},{4,6},{5,7},{6,4},{7,5},{8,10},{9,11},{10,... | collective-permute-start | bytes 786440 | tf_op jit(solution)/shard_map/ppermute | solution.py:757
  200.4 23.4 %collective-permute-start.8 = (bf16[256,512]{1,0:T(8,128)(2,1)S(1)}, bf16[256,512]{1,0:T(8,128)(2,1)S(1)}, u32[]{:S(2)}, u32[]{:S(2)}) collective-permute-start(bf16[256,512]{1,0:T(8,128)(2,1)S(1)} %copy-done.17), channel_id=1, source_target_pairs={{0,1},{1,2},{2,3},{3,0},{4,5},{5,6},{6,7},{7,4},{8,9},{9,10},{10,1... | collective-permute-start | bytes 786440 | tf_op jit(solution)/shard_map/ppermute | solution.py:757
  228.4 12.2 %copy-start.15 = (bf16[32,32,512]{2,1,0:T(8,128)(2,1)}, bf16[32,32,512]{2,1,0:T(8,128)(2,1)S(1)}, u32[]{:S(2)}) copy-start(bf16[32,32,512]{2,1,0:T(8,128)(2,1)S(1)} %all-to-all-done.5) | copy-start | bytes 3145732
  228.4 30.9 %all-to-all-start.4 = ((bf16[32,32,512]{2,1,0:T(8,128)(2,1)}), bf16[32,32,512]{2,1,0:T(8,128)(2,1)}, u32[]{:S(2)}, u32[]{:S(2)}) async-start(bf16[32,32,512]{2,1,0:T(8,128)(2,1)} %bitcast.26), calls=%async_computation.4 | async-start | bytes 2097152 | tf_op jit(solution)/shard_map/all_to_all | solution.py:685
  (14 other events, 57.7 us)

commit v6 on v5

--- a/solution.py
+++ b/solution.py
@@ -596,28 +596,25 @@
     return out[0], out[1], out[2], pieces
 
 
-def own_kernel(q_ref, k_ref, v_ref, wq_ref, wk_ref, wv_ref, *out_refs):
+def own_kernel(q_ref, k_ref, v_ref, wq_ref, wk_ref, wv_ref, out_ref):
     total = split_dot(q_ref[...], wq_ref[...])
     total += split_dot(k_ref[...], wk_ref[...])
     total += split_dot(v_ref[...], wv_ref[...])
-    low = 0
-    for out_ref in out_refs:
-        wide = out_ref.shape[1]
-        out_ref[...] = total[:, low : low + wide]
-        low += wide
-
-
-def own_project(grad_q, own_k, own_v, w_query, w_key, w_value, splits):
+    out_ref[...] = total
+
+
+def own_project(grad_q, own_k, own_v, w_query, w_key, w_value, wide, at):
     rows_dev, width = grad_q.shape
     chunk = 256
     spec = pl.BlockSpec((chunk, width), lambda i: (i, 0))
+    w_spec = pl.BlockSpec((wide, width), lambda i: (at, 0), pipeline_mode=pl.Buffered(1))
     return pl.pallas_call(
         own_kernel,
-        out_shape=[jax.ShapeDtypeStruct((rows_dev, wide), f32) for wide in splits],
+        out_shape=pltpu.VMEM((rows_dev, wide), jnp.dtype(f32)),
         grid=(rows_dev // chunk,),
-        in_specs=[spec, spec, spec] + [whole(w_query.shape)] * 3,
-        out_specs=[pl.BlockSpec((chunk, wide), lambda i: (i, 0)) for wide in splits],
-        compiler_params=params(20),
+        in_specs=[spec, spec, spec, w_spec, w_spec, w_spec],
+        out_specs=pl.BlockSpec((chunk, wide), lambda i: (i, 0)),
+        compiler_params=params(16),
         cost_estimate=LIGHT,
         name="own_project",
     )(pin(grad_q), pin(own_k), pin(own_v), w_query, w_key, w_value)
@@ -652,7 +649,7 @@
             out_specs=whole((rows_dev, width)),
             scratch_shapes=[pltpu.VMEM((rows_dev, width), f32)],
         ),
-        compiler_params=params(20),
+        compiler_params=params(14),
         cost_estimate=LIGHT,
         name="collect",
     )(picks, own, from_node, *returned)
@@ -723,7 +720,7 @@
     queries, k_table, v_table = project(
         to_node, feature_rows, w_query, w_key, w_value, table_rows
     )
-    for at in range(shifts):
+    for at in sorted(every, key=lambda at: min(at + 1, shifts - at)):
         parts = [moved[at] for moved in arrived]
         start = rows_dev + at * capacity * block
         k_table, v_table = remote_project(parts, w_key, w_value, k_table, v_table, start)
@@ -756,11 +753,10 @@
             perm = [(c, (c - at - 1) % col_count) for c in range(col_count)]
             moved.append(lax.ppermute(far[at], "col", perm))
         returned.append(moved)
-    own_parts = own_project(grad_q, own_k, own_v, w_query, w_key, w_value, splits)
-    grad_back = [
-        exchange(collect(picks, own, from_node, moved, capacity, block))
-        for own, moved in zip(own_parts, returned)
-    ]
+    grad_back = []
+    for at, (wide, moved) in enumerate(zip(splits, returned)):
+        own = own_project(grad_q, own_k, own_v, w_query, w_key, w_value, wide, at)
+        grad_back.append(exchange(collect(picks, own, from_node, moved, capacity, block)))
     return (permute(to_row, [layer_back]), permute(to_row, grad_back))
 
 

time: 265 us -> 262 us (0.989)
  Pallas kernels: 129 us -> 133 us
  waiting for transfers between devices: 81.4 us -> 77.6 us
  starting transfers between devices: 43.8 us -> 40.5 us
    ppermute x6, waiting for transfers between devices: 29.3 us -> 24.3 us  [body(): moved.append(lax.ppermute(far[at], 'col', perm))]
    all_to_all x6, starting transfers between devices: 33.4 us -> 30.1 us  [exchange(): lax.all_to_all(buffer, ('row', 'col'), split_axis=0, concat_axis=0, tiled...]
    pallas_call x1 -> x2, Pallas kernels: 8.9 us -> 12.1 us  [own_project(): pl.pallas_call(own_kernel, out_shape=pltpu.VMEM((rows_dev, wide), jnp.dty...]
    unnamed x40 -> x42, local copies, waits for them, and re-layouts: 6.17 us -> 6.45 us
  transfers between devices with their start and end apart: 18 -> 18, of which waited for: 11 -> 12; matrix products, arithmetic and copies ran while one was open for 0% -> 0% of each run, Pallas kernels for 44% -> 46%
where the time goes in v6:
time: 262 us; the launch traced here: 260 us
  Pallas kernels  133 us (51%)
  waiting for transfers between devices  77.6 us (30%)
  starting transfers between devices  40.5 us (15%)
  local copies, waits for them, and re-layouts  8.46 us (3%)
    pallas_call x1, Pallas kernels, backward(): pl.pallas_call(functools.partial(backward_kernel, reads, shifts), out_sha...  33.8 us
    all_to_all x6, waiting for transfers between devices, exchange(): lax.all_to_all(buffer, ('row', 'col'), split_axis=0, concat_axis=0, tiled...  31.6 us
    all_to_all x6, starting transfers between devices, exchange(): lax.all_to_all(buffer, ('row', 'col'), split_axis=0, concat_axis=0, tiled...  30.1 us
    ppermute x6, waiting for transfers between devices, body(): moved.append(lax.ppermute(far[at], 'col', perm))  24.3 us
    ppermute x6, waiting for transfers between devices, forward_rows(): return lax.ppermute(outgoing, 'col', perm)  21.7 us
    pallas_call x1, Pallas kernels, forward(): pl.pallas_call(functools.partial(forward_kernel, reads), out_shape=(hbm((...  18.9 us
    pallas_call x3, Pallas kernels, permute(): pl.pallas_call(permute_kernel, out_shape=hbm((rows_dev, width), bf16), gr...  16 us
    pallas_call x3, Pallas kernels, send_permute(): pl.pallas_call(send_kernel, out_shape=hbm((rows_dev, piece), bf16), grid_...  13.9 us
  transfers between devices with their start and end apart: 18, of which 12 were waited for; matrix products, arithmetic and copies ran while one was open for 0% of the time, Pallas kernels for 46%

profile of v6, /device:TPU:0, one launch (start us, length us, event | category | flops | bytes accessed | tf_op | source)
XLA Modules:
  0.0 260.3 jit_solution(687623873924405621)
XLA Ops:
  1.6 4.2 %send_permute.3 = bf16[1024,512]{1,0:T(8,128)(2,1)} custom-call(s32[1]{0:T(128)} %bitcast.self_ref, s32[32,1024]{1,0:T(8,128)S(1)} %reshape.105.loader_ref, bf16[1024,1024]{1,0:T(8,128)(2,1)} %rows_ref.4), custom_call_target="tpu_custom_call" | custom-call | tf_op jit(solution)/shard_map/send_permute/pallas_call | solution.py:99
  5.8 7.3 %all-to-all-start = ((bf16[32,32,512]{2,1,0:T(8,128)(2,1)}), bf16[32,32,512]{2,1,0:T(8,128)(2,1)S(1)}, u32[]{:S(2)}, u32[]{:S(2)}) async-start(bf16[32,32,512]{2,1,0:T(8,128)(2,1)} %bitcast.24), calls=%async_computation | async-start | bytes 2097152 | tf_op jit(solution)/shard_map/all_to_all | solution.py:682
  13.1 5.7 %index_tables.1 = (bf16[1024,1024]{1,0:T(8,128)(2,1)}, bf16[1024,1024]{1,0:T(8,128)(2,1)}, bf16[1024,1024]{1,0:T(8,128)(2,1)}) custom-call(s32[1]{0:T(128)} %bitcast.self_ref, s32[32,1024]{1,0:T(8,128)S(1)} %reshape.105.loader_ref), custom_call_target="tpu_custom_call" | custom-call | tf_op jit(solution)/shard_map/index_tables/pallas_call | solution.py:153
  18.8 4.2 %send_permute.4 = bf16[1024,512]{1,0:T(8,128)(2,1)} custom-call(s32[1]{0:T(128)} %bitcast.self_ref, s32[32,1024]{1,0:T(8,128)S(1)} %reshape.105.loader_ref, bf16[1024,1024]{1,0:T(8,128)(2,1)} %rows_ref.4), custom_call_target="tpu_custom_call" | custom-call | tf_op jit(solution)/shard_map/send_permute/pallas_call | solution.py:99
  24.1 15.2 %all-to-all-done = bf16[32,32,512]{2,1,0:T(8,128)(2,1)S(1)} async-done(((bf16[32,32,512]{2,1,0:T(8,128)(2,1)}), bf16[32,32,512]{2,1,0:T(8,128)(2,1)S(1)}, u32[]{:S(2)}, u32[]{:S(2)}) %all-to-all-start) | async-done | bytes 1048608 | tf_op jit(solution)/shard_map/all_to_all | solution.py:682
  50.2 5.6 %send_permute.5 = bf16[1024,1024]{1,0:T(8,128)(2,1)} custom-call(s32[1]{0:T(128)} %bitcast.self_ref, s32[32,1024]{1,0:T(8,128)S(1)} %reshape.105.loader_ref, bf16[1024,1024]{1,0:T(8,128)(2,1)} %rows_ref.5), custom_call_target="tpu_custom_call" | custom-call | tf_op jit(solution)/shard_map/send_permute/pallas_call | solution.py:99
  55.7 6.0 %collective-permute-done.refs_0_ = bf16[256,512]{1,0:T(8,128)(2,1)S(1)} collective-permute-done((bf16[256,512]{1,0:T(8,128)(2,1)}, bf16[256,512]{1,0:T(8,128)(2,1)S(1)}, u32[]{:S(2)}, u32[]{:S(2)}) %collective-permute-start) | collective-permute-done | bytes 262176 | tf_op jit(solution)/shard_map/ppermute | solution.py:704
  61.8 5.6 %collective-permute-done.2.refs_0_ = bf16[256,512]{1,0:T(8,128)(2,1)S(1)} collective-permute-done((bf16[256,512]{1,0:T(8,128)(2,1)}, bf16[256,512]{1,0:T(8,128)(2,1)S(1)}, u32[]{:S(2)}, u32[]{:S(2)}) %collective-permute-start.2) | collective-permute-done | bytes 262176 | tf_op jit(solution)/shard_map/ppermute | solution.py:704
  83.8 12.1 %project.1 = (bf16[1024,1024]{1,0:T(8,128)(2,1)}, bf16[1792,1024]{1,0:T(8,128)(2,1)}, bf16[1792,1024]{1,0:T(8,128)(2,1)}) custom-call(bf16[1024,1024]{1,0:T(8,128)(2,1)} %get-tuple-element.53.refs_0_.refs_1_.refs_2_.to_node_ref, bf16[1024,1024]{1,0:T(8,128)(2,1)S(1)} %copy-done.7, bf16[1024,1024]{1,0:T(8,128)(2,1)S(1)} %copy-done.2, ...), custom_call_target="tpu_custom_call" | custom-call | tf_op jit(solution)/shard_map/project/pallas_call | solution.py:253
  103.3 6.8 %collective-permute-done.5.refs_1_ = bf16[256,512]{1,0:T(8,128)(2,1)S(1)} collective-permute-done((bf16[256,512]{1,0:T(8,128)(2,1)S(1)}, bf16[256,512]{1,0:T(8,128)(2,1)S(1)}, u32[]{:S(2)}, u32[]{:S(2)}) %collective-permute-start.5) | collective-permute-done | bytes 262176 | tf_op jit(solution)/shard_map/ppermute | solution.py:704
  112.1 18.9 %forward.1 = (bf16[1024,1024]{1,0:T(8,128)(2,1)}, f32[1024,1024]{1,0:T(8,128)}, f32[128,128]{1,0:T(8,128)}) custom-call(s32[32]{0:T(128)S(1)} %reshape.109.entries_ref, bf16[1024,1024]{1,0:T(8,128)(2,1)} %get-tuple-element.61.q_ref, f32[1,1024]{1,0:T(1,128)S(1)} %bitcast.17, bf16[1024,1024]{1,0:T(8,128)(2,1)S(1)} %copy-done.10, ...), custom_call_target="tpu_custom_call" | custom-call | tf_op jit(solution)/shard_map/forward/pallas_call | solution.py:383
  131.1 5.7 %all-to-all-start.2 = ((bf16[32,32,1024]{2,1,0:T(8,128)(2,1)}), bf16[32,32,1024]{2,1,0:T(8,128)(2,1)}, u32[]{:S(2)}, u32[]{:S(2)}) async-start(bf16[32,32,1024]{2,1,0:T(8,128)(2,1)} %bitcast.27), calls=%async_computation.2 | async-start | bytes 4194304 | tf_op jit(solution)/shard_map/all_to_all | solution.py:682
  136.8 33.8 %backward.1 = (bf16[1024,1024]{1,0:T(8,128)(2,1)}, bf16[1024,1024]{1,0:T(8,128)(2,1)}, bf16[1024,1024]{1,0:T(8,128)(2,1)}, bf16[256,512]{1,0:T(8,128)(2,1)}, bf1...) custom-call(s32[32]{0:T(128)S(1)} %reshape.109.entries_ref, ...), custom_call_target="tpu_custom_call" | custom-call | tf_op jit(solution)/shard_map/backward/pallas_call | solution.py:546
  172.4 6.0 %own_project.3.own_ref = f32[1024,512]{1,0:T(8,128)S(1)} custom-call(bf16[1024,1024]{1,0:T(8,128)(2,1)} %get-tuple-element.85.q_ref, bf16[1024,1024]{1,0:T(8,128)(2,1)} %get-tuple-element.86.k_ref, bf16[1024,1024]{1,0:T(8,128)(2,1)} %get-tuple-element.87.v_ref, bf16[1024,1024]{1,0:T(8,128)(2,1)S(1)} %copy-done.8, bf16[1024,1024]{1,0:T(8,128)(2,1)S(1)} %copy-done.3, ...), custom_call_target="tpu_custom_call" | custom-call | tf_op jit(solution)/shard_map/own_project/pallas_call | solution.py:611
  181.8 7.0 %collective-permute-done.10.refs_1_ = bf16[256,512]{1,0:T(8,128)(2,1)S(1)} collective-permute-done((bf16[256,512]{1,0:T(8,128)(2,1)}, bf16[256,512]{1,0:T(8,128)(2,1)S(1)}, u32[]{:S(2)}, u32[]{:S(2)}) %collective-permute-start.10) | collective-permute-done | bytes 262176 | tf_op jit(solution)/shard_map/ppermute | solution.py:754
  191.8 4.9 %all-to-all-start.5 = ((bf16[32,32,512]{2,1,0:T(8,128)(2,1)}), bf16[32,32,512]{2,1,0:T(8,128)(2,1)S(1)}, u32[]{:S(2)}, u32[]{:S(2)}) async-start(bf16[32,32,512]{2,1,0:T(8,128)(2,1)} %bitcast.25), calls=%async_computation.5 | async-start | bytes 2097152 | tf_op jit(solution)/shard_map/all_to_all | solution.py:682
  202.0 6.0 %own_project.2.own_ref = f32[1024,512]{1,0:T(8,128)S(1)} custom-call(bf16[1024,1024]{1,0:T(8,128)(2,1)} %get-tuple-element.85.q_ref, bf16[1024,1024]{1,0:T(8,128)(2,1)} %get-tuple-element.86.k_ref, bf16[1024,1024]{1,0:T(8,128)(2,1)} %get-tuple-element.87.v_ref, bf16[1024,1024]{1,0:T(8,128)(2,1)S(1)} %copy-done.9, bf16[1024,1024]{1,0:T(8,128)(2,1)S(1)} %copy-done.3, ...), custom_call_target="tpu_custom_call" | custom-call | tf_op jit(solution)/shard_map/own_project/pallas_call | solution.py:611
  208.0 5.2 %collective-permute-done.6.refs_0_ = bf16[256,512]{1,0:T(8,128)(2,1)S(1)} collective-permute-done((bf16[256,512]{1,0:T(8,128)(2,1)}, bf16[256,512]{1,0:T(8,128)(2,1)S(1)}, u32[]{:S(2)}, u32[]{:S(2)}) %collective-permute-start.6) | collective-permute-done | bytes 262176 | tf_op jit(solution)/shard_map/ppermute | solution.py:754
  213.2 8.8 %collective-permute-done.7.refs_1_ = bf16[256,512]{1,0:T(8,128)(2,1)S(1)} collective-permute-done((bf16[256,512]{1,0:T(8,128)(2,1)}, bf16[256,512]{1,0:T(8,128)(2,1)S(1)}, u32[]{:S(2)}, u32[]{:S(2)}) %collective-permute-start.7) | collective-permute-done | bytes 262176 | tf_op jit(solution)/shard_map/ppermute | solution.py:754
  225.1 4.7 %all-to-all-start.4 = ((bf16[32,32,512]{2,1,0:T(8,128)(2,1)}), bf16[32,32,512]{2,1,0:T(8,128)(2,1)}, u32[]{:S(2)}, u32[]{:S(2)}) async-start(bf16[32,32,512]{2,1,0:T(8,128)(2,1)} %bitcast.26), calls=%async_computation.4 | async-start | bytes 2097152 | tf_op jit(solution)/shard_map/all_to_all | solution.py:682
  229.8 7.4 %permute.3 = bf16[1024,1024]{1,0:T(8,128)(2,1)} custom-call(bf16[1024,1024]{1,0:T(8,128)(2,1)S(1)} %copy-done.13, bf16[1024,1024]{1,0:T(8,128)(2,1)} %bitcast.9.rows_ref), custom_call_target="tpu_custom_call" | custom-call | tf_op jit(solution)/shard_map/permute/pallas_call | solution.py:190
  237.2 4.3 %permute.4.refs_0_ = bf16[1024,1024]{1,0:T(8,128)(2,1)} custom-call(bf16[1024,1024]{1,0:T(8,128)(2,1)S(1)} %copy-done.13, bf16[1024,512]{1,0:T(8,128)(2,1)} %bitcast.22), custom_call_target="tpu_custom_call" | custom-call | tf_op jit(solution)/shard_map/permute/pallas_call | solution.py:190
  241.5 14.5 %all-to-all-done.4 = bf16[32,32,512]{2,1,0:T(8,128)(2,1)} async-done(((bf16[32,32,512]{2,1,0:T(8,128)(2,1)}), bf16[32,32,512]{2,1,0:T(8,128)(2,1)}, u32[]{:S(2)}, u32[]{:S(2)}) %all-to-all-start.4) | async-done | bytes 1048608 | tf_op jit(solution)/shard_map/all_to_all | solution.py:682
  256.0 4.3 %permute.5 = bf16[1024,1024]{1,0:T(8,128)(2,1)} custom-call(bf16[1024,1024]{1,0:T(8,128)(2,1)S(1)} %copy-done.13, bf16[1024,512]{1,0:T(8,128)(2,1)} %bitcast.13.rows_ref, bf16[1024,1024]{1,0:T(8,128)(2,1)} %permute.4.refs_0_), custom_call_target="tpu_custom_call", output_to_operand_aliasing={{}: (2, {})} | custom-call | tf_op jit(solution)/shard_map/permute/pallas_call | solution.py:190
  (86 shorter events, 55.3 us)
Async XLA Ops:
  0.6 22.3 %copy-start = (s32[32,4,2]{0,2,1:T(2,128)S(1)}, s32[32,4,2]{0,2,1:T(2,128)}, u32[]{:S(2)}) copy-start(s32[32,4,2]{0,2,1:T(2,128)} %param.16) | copy-start | bytes 3076
  5.8 33.5 %all-to-all-start = ((bf16[32,32,512]{2,1,0:T(8,128)(2,1)}), bf16[32,32,512]{2,1,0:T(8,128)(2,1)S(1)}, u32[]{:S(2)}, u32[]{:S(2)}) async-start(bf16[32,32,512]{2,1,0:T(8,128)(2,1)} %bitcast.24), calls=%async_computation | async-start | bytes 2097152 | tf_op jit(solution)/shard_map/all_to_all | solution.py:682
  39.3 30.0 %all-to-all-start.1 = ((bf16[32,32,512]{2,1,0:T(8,128)(2,1)}), bf16[32,32,512]{2,1,0:T(8,128)(2,1)}, u32[]{:S(2)}, u32[]{:S(2)}) async-start(bf16[32,32,512]{2,1,0:T(8,128)(2,1)} %bitcast.23), calls=%async_computation.1 | async-start | bytes 2097152 | tf_op jit(solution)/shard_map/all_to_all | solution.py:682
  47.1 14.7 %collective-permute-start = (bf16[256,512]{1,0:T(8,128)(2,1)}, bf16[256,512]{1,0:T(8,128)(2,1)S(1)}, u32[]{:S(2)}, u32[]{:S(2)}) collective-permute-start(bf16[256,512]{1,0:T(8,128)(2,1)} %get-tuple-element.57), channel_id=1, source_target_pairs={{0,1},{1,2},{2,3},{3,0},{4,5},{5,6},{6,7},{7,4},{8,9},{9,10},{10,1... | collective-permute-start | bytes 786440 | tf_op jit(solution)/shard_map/ppermute | solution.py:704
  47.3 14.5 %collective-permute-start.1 = (bf16[256,512]{1,0:T(8,128)(2,1)}, bf16[256,512]{1,0:T(8,128)(2,1)S(1)}, u32[]{:S(2)}, u32[]{:S(2)}) collective-permute-start(bf16[256,512]{1,0:T(8,128)(2,1)} %get-tuple-element.58), channel_id=1, source_target_pairs={{0,2},{1,3},{2,0},{3,1},{4,6},{5,7},{6,4},{7,5},{8,10},{9,11},{10,... | collective-permute-start | bytes 786440 | tf_op jit(solution)/shard_map/ppermute | solution.py:704
  48.9 18.5 %collective-permute-start.2 = (bf16[256,512]{1,0:T(8,128)(2,1)}, bf16[256,512]{1,0:T(8,128)(2,1)S(1)}, u32[]{:S(2)}, u32[]{:S(2)}) collective-permute-start(bf16[256,512]{1,0:T(8,128)(2,1)} %get-tuple-element.59), channel_id=1, source_target_pairs={{0,3},{1,0},{2,1},{3,2},{4,7},{5,4},{6,5},{7,6},{8,11},{9,8},{10,9... | collective-permute-start | bytes 786440 | tf_op jit(solution)/shard_map/ppermute | solution.py:704
  73.3 57.8 %all-to-all-start.3 = ((bf16[32,32,1024]{2,1,0:T(8,128)(2,1)}), bf16[32,32,1024]{2,1,0:T(8,128)(2,1)}, u32[]{:S(2)}, u32[]{:S(2)}) async-start(bf16[32,32,1024]{2,1,0:T(8,128)(2,1)} %bitcast.21), calls=%async_computation.3 | async-start | bytes 4194304 | tf_op jit(solution)/shard_map/all_to_all | solution.py:682
  77.1 21.3 %collective-permute-start.3 = (bf16[256,512]{1,0:T(8,128)(2,1)}, bf16[256,512]{1,0:T(8,128)(2,1)S(1)}, u32[]{:S(2)}, u32[]{:S(2)}) collective-permute-start(bf16[256,512]{1,0:T(8,128)(2,1)} %get-tuple-element.70), channel_id=1, source_target_pairs={{0,1},{1,2},{2,3},{3,0},{4,5},{5,6},{6,7},{7,4},{8,9},{9,10},{10,1... | collective-permute-start | bytes 786440 | tf_op jit(solution)/shard_map/ppermute | solution.py:704
  77.4 23.8 %collective-permute-start.4 = (bf16[256,512]{1,0:T(8,128)(2,1)S(1)}, bf16[256,512]{1,0:T(8,128)(2,1)S(1)}, u32[]{:S(2)}, u32[]{:S(2)}) collective-permute-start(bf16[256,512]{1,0:T(8,128)(2,1)S(1)} %copy-done.20), channel_id=1, source_target_pairs={{0,3},{1,0},{2,1},{3,2},{4,7},{5,4},{6,5},{7,6},{8,11},{9,8},{10,9... | collective-permute-start | bytes 786440 | tf_op jit(solution)/shard_map/ppermute | solution.py:704
  78.9 31.1 %collective-permute-start.5 = (bf16[256,512]{1,0:T(8,128)(2,1)S(1)}, bf16[256,512]{1,0:T(8,128)(2,1)S(1)}, u32[]{:S(2)}, u32[]{:S(2)}) collective-permute-start(bf16[256,512]{1,0:T(8,128)(2,1)S(1)} %copy-done.19), channel_id=1, source_target_pairs={{0,2},{1,3},{2,0},{3,1},{4,6},{5,7},{6,4},{7,5},{8,10},{9,11},{10,... | collective-permute-start | bytes 786440 | tf_op jit(solution)/shard_map/ppermute | solution.py:704
  131.1 60.7 %all-to-all-start.2 = ((bf16[32,32,1024]{2,1,0:T(8,128)(2,1)}), bf16[32,32,1024]{2,1,0:T(8,128)(2,1)}, u32[]{:S(2)}, u32[]{:S(2)}) async-start(bf16[32,32,1024]{2,1,0:T(8,128)(2,1)} %bitcast.27), calls=%async_computation.2 | async-start | bytes 4194304 | tf_op jit(solution)/shard_map/all_to_all | solution.py:682
  136.8 35.6 %copy-start.3 = (bf16[1024,1024]{1,0:T(8,128)(2,1)S(1)}, bf16[1024,1024]{1,0:T(8,128)(2,1)}, u32[]{:S(2)}) copy-start(bf16[1024,1024]{1,0:T(8,128)(2,1)} %wk_ref.11) | copy-start | bytes 6291460
  136.8 35.6 %copy-start.5 = (bf16[1024,1024]{1,0:T(8,128)(2,1)S(1)}, bf16[1024,1024]{1,0:T(8,128)(2,1)}, u32[]{:S(2)}) copy-start(bf16[1024,1024]{1,0:T(8,128)(2,1)} %wv_ref.11) | copy-start | bytes 6291460
  136.8 35.6 %copy-start.8 = (bf16[1024,1024]{1,0:T(8,128)(2,1)S(1)}, bf16[1024,1024]{1,0:T(8,128)(2,1)}, u32[]{:S(2)}) copy-start(bf16[1024,1024]{1,0:T(8,128)(2,1)} %wq_ref.5) | copy-start | bytes 6291460
  170.7 11.1 %collective-permute-start.9 = (bf16[256,512]{1,0:T(8,128)(2,1)}, bf16[256,512]{1,0:T(8,128)(2,1)S(1)}, u32[]{:S(2)}, u32[]{:S(2)}) collective-permute-start(bf16[256,512]{1,0:T(8,128)(2,1)} %get-tuple-element.91), channel_id=1, source_target_pairs={{0,3},{1,0},{2,1},{3,2},{4,7},{5,4},{6,5},{7,6},{8,11},{9,8},{10,9... | collective-permute-start | bytes 786440 | tf_op jit(solution)/shard_map/ppermute | solution.py:754
  172.0 16.8 %collective-permute-start.10 = (bf16[256,512]{1,0:T(8,128)(2,1)}, bf16[256,512]{1,0:T(8,128)(2,1)S(1)}, u32[]{:S(2)}, u32[]{:S(2)}) collective-permute-start(bf16[256,512]{1,0:T(8,128)(2,1)} %get-tuple-element.92), channel_id=1, source_target_pairs={{0,2},{1,3},{2,0},{3,1},{4,6},{5,7},{6,4},{7,5},{8,10},{9,11},{10,... | collective-permute-start | bytes 786440 | tf_op jit(solution)/shard_map/ppermute | solution.py:754
  172.3 16.4 %collective-permute-start.11 = (bf16[256,512]{1,0:T(8,128)(2,1)}, bf16[256,512]{1,0:T(8,128)(2,1)S(1)}, u32[]{:S(2)}, u32[]{:S(2)}) collective-permute-start(bf16[256,512]{1,0:T(8,128)(2,1)} %get-tuple-element.93), channel_id=1, source_target_pairs={{0,1},{1,2},{2,3},{3,0},{4,5},{5,6},{6,7},{7,4},{8,9},{9,10},{10,1... | collective-permute-start | bytes 786440 | tf_op jit(solution)/shard_map/ppermute | solution.py:754
  172.4 16.4 %copy-start.11 = (bf16[1024,1024]{1,0:T(8,128)(2,1)S(1)}, bf16[1024,1024]{1,0:T(8,128)(2,1)}, u32[]{:S(2)}) copy-start(bf16[1024,1024]{1,0:T(8,128)(2,1)} %get-tuple-element.62.from_node_ref) | copy-start | bytes 6291460
  191.8 33.3 %all-to-all-start.5 = ((bf16[32,32,512]{2,1,0:T(8,128)(2,1)}), bf16[32,32,512]{2,1,0:T(8,128)(2,1)S(1)}, u32[]{:S(2)}, u32[]{:S(2)}) async-start(bf16[32,32,512]{2,1,0:T(8,128)(2,1)} %bitcast.25), calls=%async_computation.5 | async-start | bytes 2097152 | tf_op jit(solution)/shard_map/all_to_all | solution.py:682
  196.7 16.5 %collective-permute-start.6 = (bf16[256,512]{1,0:T(8,128)(2,1)}, bf16[256,512]{1,0:T(8,128)(2,1)S(1)}, u32[]{:S(2)}, u32[]{:S(2)}) collective-permute-start(bf16[256,512]{1,0:T(8,128)(2,1)} %get-tuple-element.88), channel_id=1, source_target_pairs={{0,3},{1,0},{2,1},{3,2},{4,7},{5,4},{6,5},{7,6},{8,11},{9,8},{10,9... | collective-permute-start | bytes 786440 | tf_op jit(solution)/shard_map/ppermute | solution.py:754
  198.3 23.8 %collective-permute-start.7 = (bf16[256,512]{1,0:T(8,128)(2,1)}, bf16[256,512]{1,0:T(8,128)(2,1)S(1)}, u32[]{:S(2)}, u32[]{:S(2)}) collective-permute-start(bf16[256,512]{1,0:T(8,128)(2,1)} %get-tuple-element.89), channel_id=1, source_target_pairs={{0,2},{1,3},{2,0},{3,1},{4,6},{5,7},{6,4},{7,5},{8,10},{9,11},{10,... | collective-permute-start | bytes 786440 | tf_op jit(solution)/shard_map/ppermute | solution.py:754
  198.6 23.4 %collective-permute-start.8 = (bf16[256,512]{1,0:T(8,128)(2,1)S(1)}, bf16[256,512]{1,0:T(8,128)(2,1)S(1)}, u32[]{:S(2)}, u32[]{:S(2)}) collective-permute-start(bf16[256,512]{1,0:T(8,128)(2,1)S(1)} %copy-done.18), channel_id=1, source_target_pairs={{0,1},{1,2},{2,3},{3,0},{4,5},{5,6},{6,7},{7,4},{8,9},{9,10},{10,1... | collective-permute-start | bytes 786440 | tf_op jit(solution)/shard_map/ppermute | solution.py:754
  202.0 20.1 %copy-start.12 = (bf16[1024,1024]{1,0:T(8,128)(2,1)S(1)}, bf16[1024,1024]{1,0:T(8,128)(2,1)}, u32[]{:S(2)}) copy-start(bf16[1024,1024]{1,0:T(8,128)(2,1)} %get-tuple-element.62.from_node_ref) | copy-start | bytes 6291460
  225.1 30.9 %all-to-all-start.4 = ((bf16[32,32,512]{2,1,0:T(8,128)(2,1)}), bf16[32,32,512]{2,1,0:T(8,128)(2,1)}, u32[]{:S(2)}, u32[]{:S(2)}) async-start(bf16[32,32,512]{2,1,0:T(8,128)(2,1)} %bitcast.26), calls=%async_computation.4 | async-start | bytes 2097152 | tf_op jit(solution)/shard_map/all_to_all | solution.py:682
  (15 other events, 70.1 us)

commit v7 on v6

--- a/solution.py
+++ b/solution.py
@@ -16,7 +16,7 @@
 MIB = 1024 * 1024
 SUBLANES = 8
 CHUNK = 64
-UNIT = 256
+UNIT = 512
 LIGHT = pl.CostEstimate(flops=0, transcendentals=0, bytes_accessed=0)
 
 NT = (((1,), (1,)), ((), ()))
@@ -182,7 +182,7 @@
 def permute(pick, pieces):
     rows_dev = pick.shape[0]
     width = sum(rows.shape[1] for rows in pieces)
-    chunk = 512
+    chunk = 256
     out, low = [], 0
     for rows in pieces:
         first = low // UNIT
@@ -713,7 +713,6 @@
         rows, cot_out, arrived = lax.optimization_barrier((rows, cot_out, arrived))
         feature_rows.append(rows)
         outgoing = outbound_blocks(picks, to_node, rows, every, capacity, block)
-        cot_out, outgoing = lax.optimization_barrier((cot_out, outgoing))
         arrived.append([forward_rows(outgoing[at], at) for at in every])
     cot_rows = exchange(cot_out)
 

time: 262 us -> 257 us (0.981)
  local copies, waits for them, and re-layouts: 8.46 us -> 5.28 us
    unnamed x42 -> x38, local copies, waits for them, and re-layouts: 6.45 us -> 3.27 us
  transfers between devices with their start and end apart: 18 -> 18, of which waited for: 12 -> 11; matrix products, arithmetic and copies ran while one was open for 0% -> 0% of each run, Pallas kernels for 46% -> 48%
where the time goes in v7:
time: 257 us; the launch traced here: 256 us
  Pallas kernels  132 us (51%)
  waiting for transfers between devices  77.9 us (30%)
  starting transfers between devices  40 us (16%)
  local copies, waits for them, and re-layouts  5.28 us (2%)
    pallas_call x1, Pallas kernels, backward(): pl.pallas_call(functools.partial(backward_kernel, reads, shifts), out_sha...  33.7 us
    all_to_all x6, waiting for transfers between devices, exchange(): lax.all_to_all(buffer, ('row', 'col'), split_axis=0, concat_axis=0, tiled...  32.5 us
    all_to_all x6, starting transfers between devices, exchange(): lax.all_to_all(buffer, ('row', 'col'), split_axis=0, concat_axis=0, tiled...  29.3 us
    ppermute x6, waiting for transfers between devices, body(): moved.append(lax.ppermute(far[at], 'col', perm))  24.2 us
    ppermute x6, waiting for transfers between devices, forward_rows(): return lax.ppermute(outgoing, 'col', perm)  21.1 us
    pallas_call x1, Pallas kernels, forward(): pl.pallas_call(functools.partial(forward_kernel, reads), out_shape=(hbm((...  19 us
    pallas_call x3, Pallas kernels, permute(): pl.pallas_call(permute_kernel, out_shape=hbm((rows_dev, width), bf16), gr...  14.8 us
    pallas_call x3, Pallas kernels, send_permute(): pl.pallas_call(send_kernel, out_shape=hbm((rows_dev, piece), bf16), grid_...  13.9 us
  transfers between devices with their start and end apart: 18, of which 11 were waited for; matrix products, arithmetic and copies ran while one was open for 0% of the time, Pallas kernels for 48%

profile of v7, /device:TPU:0, one launch (start us, length us, event | category | flops | bytes accessed | tf_op | source)
XLA Modules:
  0.0 255.7 jit_solution(9309515891446120862)
XLA Ops:
  1.6 4.2 %send_permute.3 = bf16[1024,512]{1,0:T(8,128)(2,1)} custom-call(s32[1]{0:T(128)} %bitcast.self_ref, s32[32,1024]{1,0:T(8,128)S(1)} %reshape.105.loader_ref, bf16[1024,1024]{1,0:T(8,128)(2,1)} %rows_ref.4), custom_call_target="tpu_custom_call" | custom-call | tf_op jit(solution)/shard_map/send_permute/pallas_call | solution.py:99
  5.8 7.3 %all-to-all-start = ((bf16[32,32,512]{2,1,0:T(8,128)(2,1)}), bf16[32,32,512]{2,1,0:T(8,128)(2,1)S(1)}, u32[]{:S(2)}, u32[]{:S(2)}) async-start(bf16[32,32,512]{2,1,0:T(8,128)(2,1)} %bitcast.24), calls=%async_computation | async-start | bytes 2097152 | tf_op jit(solution)/shard_map/all_to_all | solution.py:682
  13.1 5.7 %index_tables.1 = (bf16[1024,1024]{1,0:T(8,128)(2,1)}, bf16[1024,1024]{1,0:T(8,128)(2,1)}, bf16[1024,1024]{1,0:T(8,128)(2,1)}) custom-call(s32[1]{0:T(128)} %bitcast.self_ref, s32[32,1024]{1,0:T(8,128)S(1)} %reshape.105.loader_ref), custom_call_target="tpu_custom_call" | custom-call | tf_op jit(solution)/shard_map/index_tables/pallas_call | solution.py:153
  18.8 4.2 %send_permute.4 = bf16[1024,512]{1,0:T(8,128)(2,1)} custom-call(s32[1]{0:T(128)} %bitcast.self_ref, s32[32,1024]{1,0:T(8,128)S(1)} %reshape.105.loader_ref, bf16[1024,1024]{1,0:T(8,128)(2,1)} %rows_ref.4), custom_call_target="tpu_custom_call" | custom-call | tf_op jit(solution)/shard_map/send_permute/pallas_call | solution.py:99
  24.1 15.2 %all-to-all-done = bf16[32,32,512]{2,1,0:T(8,128)(2,1)S(1)} async-done(((bf16[32,32,512]{2,1,0:T(8,128)(2,1)}), bf16[32,32,512]{2,1,0:T(8,128)(2,1)S(1)}, u32[]{:S(2)}, u32[]{:S(2)}) %all-to-all-start) | async-done | bytes 1048608 | tf_op jit(solution)/shard_map/all_to_all | solution.py:682
  50.3 5.6 %send_permute.5 = bf16[1024,1024]{1,0:T(8,128)(2,1)} custom-call(s32[1]{0:T(128)} %bitcast.self_ref, s32[32,1024]{1,0:T(8,128)S(1)} %reshape.105.loader_ref, bf16[1024,1024]{1,0:T(8,128)(2,1)} %rows_ref.5), custom_call_target="tpu_custom_call" | custom-call | tf_op jit(solution)/shard_map/send_permute/pallas_call | solution.py:99
  55.8 5.9 %collective-permute-done.refs_0_ = bf16[256,512]{1,0:T(8,128)(2,1)S(1)} collective-permute-done((bf16[256,512]{1,0:T(8,128)(2,1)}, bf16[256,512]{1,0:T(8,128)(2,1)S(1)}, u32[]{:S(2)}, u32[]{:S(2)}) %collective-permute-start) | collective-permute-done | bytes 262176 | tf_op jit(solution)/shard_map/ppermute | solution.py:704
  61.8 5.6 %collective-permute-done.2.refs_0_ = bf16[256,512]{1,0:T(8,128)(2,1)S(1)} collective-permute-done((bf16[256,512]{1,0:T(8,128)(2,1)}, bf16[256,512]{1,0:T(8,128)(2,1)S(1)}, u32[]{:S(2)}, u32[]{:S(2)}) %collective-permute-start.2) | collective-permute-done | bytes 262176 | tf_op jit(solution)/shard_map/ppermute | solution.py:704
  73.1 4.2 %outbound.3 = (bf16[256,512]{1,0:T(8,128)(2,1)}, bf16[256,512]{1,0:T(8,128)(2,1)}, bf16[256,512]{1,0:T(8,128)(2,1)}) custom-call(s32[6]{0:T(128)S(1)} %reshape.108.picks_ref, bf16[1024,512]{1,0:T(8,128)(2,1)} %bitcast.6.refs_1_.rows_ref, bf16[1024,1024]{1,0:T(8,128)(2,1)} %get-tuple-element.49.refs_0_.refs_1_.refs_2_.to_node_ref, ...), custom_call_target="tpu_custom_call" | custom-call | tf_op jit(solution)/shard_map/outbound/pallas_call | solution.py:224
  80.9 12.1 %project.1 = (bf16[1024,1024]{1,0:T(8,128)(2,1)}, bf16[1792,1024]{1,0:T(8,128)(2,1)}, bf16[1792,1024]{1,0:T(8,128)(2,1)}) custom-call(bf16[1024,1024]{1,0:T(8,128)(2,1)} %get-tuple-element.49.refs_0_.refs_1_.refs_2_.to_node_ref, bf16[1024,1024]{1,0:T(8,128)(2,1)S(1)} %copy-done.7, bf16[1024,1024]{1,0:T(8,128)(2,1)S(1)} %copy-done.2, ...), custom_call_target="tpu_custom_call" | custom-call | tf_op jit(solution)/shard_map/project/pallas_call | solution.py:253
  92.9 7.2 %collective-permute-done.3.refs_1_ = bf16[256,512]{1,0:T(8,128)(2,1)S(1)} collective-permute-done((bf16[256,512]{1,0:T(8,128)(2,1)}, bf16[256,512]{1,0:T(8,128)(2,1)S(1)}, u32[]{:S(2)}, u32[]{:S(2)}) %collective-permute-start.3) | collective-permute-done | bytes 262176 | tf_op jit(solution)/shard_map/ppermute | solution.py:704
  108.7 19.0 %forward.1 = (bf16[1024,1024]{1,0:T(8,128)(2,1)}, f32[1024,1024]{1,0:T(8,128)}, f32[128,128]{1,0:T(8,128)}) custom-call(s32[32]{0:T(128)S(1)} %reshape.109.entries_ref, bf16[1024,1024]{1,0:T(8,128)(2,1)} %get-tuple-element.57.q_ref, f32[1,1024]{1,0:T(1,128)S(1)} %bitcast.17, bf16[1024,1024]{1,0:T(8,128)(2,1)S(1)} %copy-done.10, ...), custom_call_target="tpu_custom_call" | custom-call | tf_op jit(solution)/shard_map/forward/pallas_call | solution.py:383
  127.7 5.0 %all-to-all-start.2 = ((bf16[32,32,1024]{2,1,0:T(8,128)(2,1)}), bf16[32,32,1024]{2,1,0:T(8,128)(2,1)}, u32[]{:S(2)}, u32[]{:S(2)}) async-start(bf16[32,32,1024]{2,1,0:T(8,128)(2,1)} %bitcast.27), calls=%async_computation.2 | async-start | bytes 4194304 | tf_op jit(solution)/shard_map/all_to_all | solution.py:682
  132.8 33.7 %backward.1 = (bf16[1024,1024]{1,0:T(8,128)(2,1)}, bf16[1024,1024]{1,0:T(8,128)(2,1)}, bf16[1024,1024]{1,0:T(8,128)(2,1)}, bf16[256,512]{1,0:T(8,128)(2,1)}, bf1...) custom-call(s32[32]{0:T(128)S(1)} %reshape.109.entries_ref, ...), custom_call_target="tpu_custom_call" | custom-call | tf_op jit(solution)/shard_map/backward/pallas_call | solution.py:546
  168.4 6.0 %own_project.3.own_ref = f32[1024,512]{1,0:T(8,128)S(1)} custom-call(bf16[1024,1024]{1,0:T(8,128)(2,1)} %get-tuple-element.77.q_ref, bf16[1024,1024]{1,0:T(8,128)(2,1)} %get-tuple-element.78.k_ref, bf16[1024,1024]{1,0:T(8,128)(2,1)} %get-tuple-element.79.v_ref, bf16[1024,1024]{1,0:T(8,128)(2,1)S(1)} %copy-done.8, bf16[1024,1024]{1,0:T(8,128)(2,1)S(1)} %copy-done.3, ...), custom_call_target="tpu_custom_call" | custom-call | tf_op jit(solution)/shard_map/own_project/pallas_call | solution.py:611
  177.6 7.0 %collective-permute-done.10.refs_1_ = bf16[256,512]{1,0:T(8,128)(2,1)S(1)} collective-permute-done((bf16[256,512]{1,0:T(8,128)(2,1)}, bf16[256,512]{1,0:T(8,128)(2,1)S(1)}, u32[]{:S(2)}, u32[]{:S(2)}) %collective-permute-start.10) | collective-permute-done | bytes 262176 | tf_op jit(solution)/shard_map/ppermute | solution.py:753
  187.7 4.8 %all-to-all-start.5 = ((bf16[32,32,512]{2,1,0:T(8,128)(2,1)}), bf16[32,32,512]{2,1,0:T(8,128)(2,1)S(1)}, u32[]{:S(2)}, u32[]{:S(2)}) async-start(bf16[32,32,512]{2,1,0:T(8,128)(2,1)} %bitcast.25), calls=%async_computation.5 | async-start | bytes 2097152 | tf_op jit(solution)/shard_map/all_to_all | solution.py:682
  197.8 6.0 %own_project.2.own_ref = f32[1024,512]{1,0:T(8,128)S(1)} custom-call(bf16[1024,1024]{1,0:T(8,128)(2,1)} %get-tuple-element.77.q_ref, bf16[1024,1024]{1,0:T(8,128)(2,1)} %get-tuple-element.78.k_ref, bf16[1024,1024]{1,0:T(8,128)(2,1)} %get-tuple-element.79.v_ref, bf16[1024,1024]{1,0:T(8,128)(2,1)S(1)} %copy-done.9, bf16[1024,1024]{1,0:T(8,128)(2,1)S(1)} %copy-done.3, ...), custom_call_target="tpu_custom_call" | custom-call | tf_op jit(solution)/shard_map/own_project/pallas_call | solution.py:611
  203.8 5.2 %collective-permute-done.6.refs_0_ = bf16[256,512]{1,0:T(8,128)(2,1)S(1)} collective-permute-done((bf16[256,512]{1,0:T(8,128)(2,1)}, bf16[256,512]{1,0:T(8,128)(2,1)S(1)}, u32[]{:S(2)}, u32[]{:S(2)}) %collective-permute-start.6) | collective-permute-done | bytes 262176 | tf_op jit(solution)/shard_map/ppermute | solution.py:753
  209.0 8.8 %collective-permute-done.7.refs_1_ = bf16[256,512]{1,0:T(8,128)(2,1)S(1)} collective-permute-done((bf16[256,512]{1,0:T(8,128)(2,1)}, bf16[256,512]{1,0:T(8,128)(2,1)S(1)}, u32[]{:S(2)}, u32[]{:S(2)}) %collective-permute-start.7) | collective-permute-done | bytes 262176 | tf_op jit(solution)/shard_map/ppermute | solution.py:753
  220.9 4.7 %all-to-all-start.4 = ((bf16[32,32,512]{2,1,0:T(8,128)(2,1)}), bf16[32,32,512]{2,1,0:T(8,128)(2,1)}, u32[]{:S(2)}, u32[]{:S(2)}) async-start(bf16[32,32,512]{2,1,0:T(8,128)(2,1)} %bitcast.26), calls=%async_computation.4 | async-start | bytes 2097152 | tf_op jit(solution)/shard_map/all_to_all | solution.py:682
  225.5 6.9 %permute.3 = bf16[1024,1024]{1,0:T(8,128)(2,1)} custom-call(bf16[1024,1024]{1,0:T(8,128)(2,1)S(1)} %copy-done.13, bf16[1024,1024]{1,0:T(8,128)(2,1)} %bitcast.9.rows_ref), custom_call_target="tpu_custom_call" | custom-call | tf_op jit(solution)/shard_map/permute/pallas_call | solution.py:190
  236.4 15.4 %all-to-all-done.4 = bf16[32,32,512]{2,1,0:T(8,128)(2,1)} async-done(((bf16[32,32,512]{2,1,0:T(8,128)(2,1)}), bf16[32,32,512]{2,1,0:T(8,128)(2,1)}, u32[]{:S(2)}, u32[]{:S(2)}) %all-to-all-start.4) | async-done | bytes 1048608 | tf_op jit(solution)/shard_map/all_to_all | solution.py:682
  251.7 4.0 %permute.5 = bf16[1024,1024]{1,0:T(8,128)(2,1)} custom-call(bf16[1024,1024]{1,0:T(8,128)(2,1)S(1)} %copy-done.13, bf16[1024,512]{1,0:T(8,128)(2,1)} %bitcast.13.rows_ref, bf16[1024,1024]{1,0:T(8,128)(2,1)} %permute.4.refs_0_), custom_call_target="tpu_custom_call", output_to_operand_aliasing={{}: (2, {})} | custom-call | tf_op jit(solution)/shard_map/permute/pallas_call | solution.py:190
  (82 shorter events, 51.2 us)
Async XLA Ops:
  0.6 22.3 %copy-start = (s32[32,4,2]{0,2,1:T(2,128)S(1)}, s32[32,4,2]{0,2,1:T(2,128)}, u32[]{:S(2)}) copy-start(s32[32,4,2]{0,2,1:T(2,128)} %param.16) | copy-start | bytes 3076
  5.8 33.5 %all-to-all-start = ((bf16[32,32,512]{2,1,0:T(8,128)(2,1)}), bf16[32,32,512]{2,1,0:T(8,128)(2,1)S(1)}, u32[]{:S(2)}, u32[]{:S(2)}) async-start(bf16[32,32,512]{2,1,0:T(8,128)(2,1)} %bitcast.24), calls=%async_computation | async-start | bytes 2097152 | tf_op jit(solution)/shard_map/all_to_all | solution.py:682
  39.3 30.0 %all-to-all-start.1 = ((bf16[32,32,512]{2,1,0:T(8,128)(2,1)}), bf16[32,32,512]{2,1,0:T(8,128)(2,1)}, u32[]{:S(2)}, u32[]{:S(2)}) async-start(bf16[32,32,512]{2,1,0:T(8,128)(2,1)} %bitcast.23), calls=%async_computation.1 | async-start | bytes 2097152 | tf_op jit(solution)/shard_map/all_to_all | solution.py:682
  47.0 14.7 %collective-permute-start = (bf16[256,512]{1,0:T(8,128)(2,1)}, bf16[256,512]{1,0:T(8,128)(2,1)S(1)}, u32[]{:S(2)}, u32[]{:S(2)}) collective-permute-start(bf16[256,512]{1,0:T(8,128)(2,1)} %get-tuple-element.53), channel_id=1, source_target_pairs={{0,1},{1,2},{2,3},{3,0},{4,5},{5,6},{6,7},{7,4},{8,9},{9,10},{10,1... | collective-permute-start | bytes 786440 | tf_op jit(solution)/shard_map/ppermute | solution.py:704
  47.3 14.5 %collective-permute-start.1 = (bf16[256,512]{1,0:T(8,128)(2,1)}, bf16[256,512]{1,0:T(8,128)(2,1)S(1)}, u32[]{:S(2)}, u32[]{:S(2)}) collective-permute-start(bf16[256,512]{1,0:T(8,128)(2,1)} %get-tuple-element.54), channel_id=1, source_target_pairs={{0,2},{1,3},{2,0},{3,1},{4,6},{5,7},{6,4},{7,5},{8,10},{9,11},{10,... | collective-permute-start | bytes 786440 | tf_op jit(solution)/shard_map/ppermute | solution.py:704
  48.9 18.5 %collective-permute-start.2 = (bf16[256,512]{1,0:T(8,128)(2,1)}, bf16[256,512]{1,0:T(8,128)(2,1)S(1)}, u32[]{:S(2)}, u32[]{:S(2)}) collective-permute-start(bf16[256,512]{1,0:T(8,128)(2,1)} %get-tuple-element.55), channel_id=1, source_target_pairs={{0,3},{1,0},{2,1},{3,2},{4,7},{5,4},{6,5},{7,6},{8,11},{9,8},{10,9... | collective-permute-start | bytes 786440 | tf_op jit(solution)/shard_map/ppermute | solution.py:704
  69.3 58.4 %all-to-all-start.3 = ((bf16[32,32,1024]{2,1,0:T(8,128)(2,1)}), bf16[32,32,1024]{2,1,0:T(8,128)(2,1)}, u32[]{:S(2)}, u32[]{:S(2)}) async-start(bf16[32,32,1024]{2,1,0:T(8,128)(2,1)} %bitcast.21), calls=%async_computation.3 | async-start | bytes 4194304 | tf_op jit(solution)/shard_map/all_to_all | solution.py:682
  77.3 22.9 %collective-permute-start.3 = (bf16[256,512]{1,0:T(8,128)(2,1)}, bf16[256,512]{1,0:T(8,128)(2,1)S(1)}, u32[]{:S(2)}, u32[]{:S(2)}) collective-permute-start(bf16[256,512]{1,0:T(8,128)(2,1)} %get-tuple-element.62), channel_id=1, source_target_pairs={{0,1},{1,2},{2,3},{3,0},{4,5},{5,6},{6,7},{7,4},{8,9},{9,10},{10,1... | collective-permute-start | bytes 786440 | tf_op jit(solution)/shard_map/ppermute | solution.py:704
  77.6 24.6 %collective-permute-start.4 = (bf16[256,512]{1,0:T(8,128)(2,1)}, bf16[256,512]{1,0:T(8,128)(2,1)S(1)}, u32[]{:S(2)}, u32[]{:S(2)}) collective-permute-start(bf16[256,512]{1,0:T(8,128)(2,1)} %get-tuple-element.66), channel_id=1, source_target_pairs={{0,3},{1,0},{2,1},{3,2},{4,7},{5,4},{6,5},{7,6},{8,11},{9,8},{10,9... | collective-permute-start | bytes 786440 | tf_op jit(solution)/shard_map/ppermute | solution.py:704
  79.1 27.6 %collective-permute-start.5 = (bf16[256,512]{1,0:T(8,128)(2,1)}, bf16[256,512]{1,0:T(8,128)(2,1)S(1)}, u32[]{:S(2)}, u32[]{:S(2)}) collective-permute-start(bf16[256,512]{1,0:T(8,128)(2,1)} %get-tuple-element.70), channel_id=1, source_target_pairs={{0,2},{1,3},{2,0},{3,1},{4,6},{5,7},{6,4},{7,5},{8,10},{9,11},{10,... | collective-permute-start | bytes 786440 | tf_op jit(solution)/shard_map/ppermute | solution.py:704
  127.7 60.0 %all-to-all-start.2 = ((bf16[32,32,1024]{2,1,0:T(8,128)(2,1)}), bf16[32,32,1024]{2,1,0:T(8,128)(2,1)}, u32[]{:S(2)}, u32[]{:S(2)}) async-start(bf16[32,32,1024]{2,1,0:T(8,128)(2,1)} %bitcast.27), calls=%async_computation.2 | async-start | bytes 4194304 | tf_op jit(solution)/shard_map/all_to_all | solution.py:682
  132.7 35.6 %copy-start.3 = (bf16[1024,1024]{1,0:T(8,128)(2,1)S(1)}, bf16[1024,1024]{1,0:T(8,128)(2,1)}, u32[]{:S(2)}) copy-start(bf16[1024,1024]{1,0:T(8,128)(2,1)} %wk_ref.11) | copy-start | bytes 6291460
  132.7 35.6 %copy-start.5 = (bf16[1024,1024]{1,0:T(8,128)(2,1)S(1)}, bf16[1024,1024]{1,0:T(8,128)(2,1)}, u32[]{:S(2)}) copy-start(bf16[1024,1024]{1,0:T(8,128)(2,1)} %wv_ref.11) | copy-start | bytes 6291460
  132.7 35.6 %copy-start.8 = (bf16[1024,1024]{1,0:T(8,128)(2,1)S(1)}, bf16[1024,1024]{1,0:T(8,128)(2,1)}, u32[]{:S(2)}) copy-start(bf16[1024,1024]{1,0:T(8,128)(2,1)} %wq_ref.5) | copy-start | bytes 6291460
  166.5 11.1 %collective-permute-start.9 = (bf16[256,512]{1,0:T(8,128)(2,1)}, bf16[256,512]{1,0:T(8,128)(2,1)S(1)}, u32[]{:S(2)}, u32[]{:S(2)}) collective-permute-start(bf16[256,512]{1,0:T(8,128)(2,1)} %get-tuple-element.83), channel_id=1, source_target_pairs={{0,3},{1,0},{2,1},{3,2},{4,7},{5,4},{6,5},{7,6},{8,11},{9,8},{10,9... | collective-permute-start | bytes 786440 | tf_op jit(solution)/shard_map/ppermute | solution.py:753
  167.8 16.8 %collective-permute-start.10 = (bf16[256,512]{1,0:T(8,128)(2,1)}, bf16[256,512]{1,0:T(8,128)(2,1)S(1)}, u32[]{:S(2)}, u32[]{:S(2)}) collective-permute-start(bf16[256,512]{1,0:T(8,128)(2,1)} %get-tuple-element.84), channel_id=1, source_target_pairs={{0,2},{1,3},{2,0},{3,1},{4,6},{5,7},{6,4},{7,5},{8,10},{9,11},{10,... | collective-permute-start | bytes 786440 | tf_op jit(solution)/shard_map/ppermute | solution.py:753
  168.2 16.4 %collective-permute-start.11 = (bf16[256,512]{1,0:T(8,128)(2,1)}, bf16[256,512]{1,0:T(8,128)(2,1)S(1)}, u32[]{:S(2)}, u32[]{:S(2)}) collective-permute-start(bf16[256,512]{1,0:T(8,128)(2,1)} %get-tuple-element.85), channel_id=1, source_target_pairs={{0,1},{1,2},{2,3},{3,0},{4,5},{5,6},{6,7},{7,4},{8,9},{9,10},{10,1... | collective-permute-start | bytes 786440 | tf_op jit(solution)/shard_map/ppermute | solution.py:753
  168.4 16.3 %copy-start.11 = (bf16[1024,1024]{1,0:T(8,128)(2,1)S(1)}, bf16[1024,1024]{1,0:T(8,128)(2,1)}, u32[]{:S(2)}) copy-start(bf16[1024,1024]{1,0:T(8,128)(2,1)} %get-tuple-element.58.from_node_ref) | copy-start | bytes 6291460
  187.7 33.2 %all-to-all-start.5 = ((bf16[32,32,512]{2,1,0:T(8,128)(2,1)}), bf16[32,32,512]{2,1,0:T(8,128)(2,1)S(1)}, u32[]{:S(2)}, u32[]{:S(2)}) async-start(bf16[32,32,512]{2,1,0:T(8,128)(2,1)} %bitcast.25), calls=%async_computation.5 | async-start | bytes 2097152 | tf_op jit(solution)/shard_map/all_to_all | solution.py:682
  192.5 16.5 %collective-permute-start.6 = (bf16[256,512]{1,0:T(8,128)(2,1)}, bf16[256,512]{1,0:T(8,128)(2,1)S(1)}, u32[]{:S(2)}, u32[]{:S(2)}) collective-permute-start(bf16[256,512]{1,0:T(8,128)(2,1)} %get-tuple-element.80), channel_id=1, source_target_pairs={{0,3},{1,0},{2,1},{3,2},{4,7},{5,4},{6,5},{7,6},{8,11},{9,8},{10,9... | collective-permute-start | bytes 786440 | tf_op jit(solution)/shard_map/ppermute | solution.py:753
  194.1 23.8 %collective-permute-start.7 = (bf16[256,512]{1,0:T(8,128)(2,1)}, bf16[256,512]{1,0:T(8,128)(2,1)S(1)}, u32[]{:S(2)}, u32[]{:S(2)}) collective-permute-start(bf16[256,512]{1,0:T(8,128)(2,1)} %get-tuple-element.81), channel_id=1, source_target_pairs={{0,2},{1,3},{2,0},{3,1},{4,6},{5,7},{6,4},{7,5},{8,10},{9,11},{10,... | collective-permute-start | bytes 786440 | tf_op jit(solution)/shard_map/ppermute | solution.py:753
  194.4 23.4 %collective-permute-start.8 = (bf16[256,512]{1,0:T(8,128)(2,1)S(1)}, bf16[256,512]{1,0:T(8,128)(2,1)S(1)}, u32[]{:S(2)}, u32[]{:S(2)}) collective-permute-start(bf16[256,512]{1,0:T(8,128)(2,1)S(1)} %copy-done.18), channel_id=1, source_target_pairs={{0,1},{1,2},{2,3},{3,0},{4,5},{5,6},{6,7},{7,4},{8,9},{9,10},{10,1... | collective-permute-start | bytes 786440 | tf_op jit(solution)/shard_map/ppermute | solution.py:753
  197.8 20.1 %copy-start.12 = (bf16[1024,1024]{1,0:T(8,128)(2,1)S(1)}, bf16[1024,1024]{1,0:T(8,128)(2,1)}, u32[]{:S(2)}) copy-start(bf16[1024,1024]{1,0:T(8,128)(2,1)} %get-tuple-element.58.from_node_ref) | copy-start | bytes 6291460
  220.9 30.9 %all-to-all-start.4 = ((bf16[32,32,512]{2,1,0:T(8,128)(2,1)}), bf16[32,32,512]{2,1,0:T(8,128)(2,1)}, u32[]{:S(2)}, u32[]{:S(2)}) async-start(bf16[32,32,512]{2,1,0:T(8,128)(2,1)} %bitcast.26), calls=%async_computation.4 | async-start | bytes 2097152 | tf_op jit(solution)/shard_map/all_to_all | solution.py:682
  (13 other events, 72.1 us)

commit v8 on v7

--- a/solution.py
+++ b/solution.py
@@ -450,13 +450,13 @@
 
     @pl.when(step == 0)
     def _():
-        sum_k_ref[...] = jnp.zeros_like(sum_k_ref)
-        sum_v_ref[...] = jnp.zeros_like(sum_v_ref)
         load_wk.start()
         load_wv.start()
 
     entries = [entries_ref[step * reads + j] * block for j in range(reads)]
     starts = [pl.multiple_of(at, block) for at in entries]
+    flags = (pl.num_programs(0) + step) * reads
+    fresh = [entries_ref[flags + j] > 0 for j in range(reads)]
     mixed = mixed_ref[...]
     inv_rms = lax.rsqrt(jnp.mean(mixed * mixed, axis=1, keepdims=True) + 1e-06)
     grad_in = matmul(to_node_ref[...], cot_ref[...]) * gain_ref[...]
@@ -494,8 +494,10 @@
         for j, at in enumerate(starts):
             part = slice(j * block, (j + 1) * block)
             rows = pl.ds(at, block)
-            sum_k_ref[rows, cols] += key_term[part]
-            sum_v_ref[rows, cols] += value_term[part]
+            key_sum = jnp.where(fresh[j], 0.0, sum_k_ref[rows, cols])
+            value_sum = jnp.where(fresh[j], 0.0, sum_v_ref[rows, cols])
+            sum_k_ref[rows, cols] = key_sum + key_term[part]
+            sum_v_ref[rows, cols] = value_sum + value_term[part]
 
     @pl.when(step == pl.num_programs(0) - 1)
     def _():
@@ -621,7 +623,7 @@
 
 
 def collect_kernel(capacity, block, picks_ref, own_ref, from_node_ref, *refs):
-    returned, (out_ref, total_ref) = refs[:-2], refs[-2:]
+    returned, (out_hbm, total_ref, out_ref, out_sem) = refs[:-4], refs[-4:]
     total_ref[...] = own_ref[...]
     for at, ref in enumerate(returned):
         for slot in range(capacity):
@@ -633,7 +635,20 @@
                 part = ref[slot * block : (slot + 1) * block, :]
                 total_ref[rows, :] += part.astype(f32)
 
-    out_ref[...] = matmul(from_node_ref[...], total_ref[...].astype(bf16)).astype(bf16)
+    total = total_ref[...].astype(bf16)
+    chunk = 2 * block
+    saves = []
+    for at in range(0, out_ref.shape[0], chunk):
+        part = slice(at, at + chunk)
+        out_ref[part, :] = matmul(from_node_ref[part, :], total).astype(bf16)
+        saves.append(
+            pltpu.make_async_copy(
+                out_ref.at[part, :], out_hbm.at[part, :], out_sem.at[at // chunk]
+            )
+        )
+        saves[-1].start()
+    for save in saves:
+        save.wait()
 
 
 def collect(picks, own, from_node, returned, capacity, block):
@@ -646,8 +661,12 @@
             grid=(1,),
             in_specs=[whole(own.shape), whole(from_node.shape)]
             + [whole(part.shape) for part in returned],
-            out_specs=whole((rows_dev, width)),
-            scratch_shapes=[pltpu.VMEM((rows_dev, width), f32)],
+            out_specs=pl.BlockSpec(memory_space=pl.ANY),
+            scratch_shapes=[
+                pltpu.VMEM((rows_dev, width), f32),
+                pltpu.VMEM((rows_dev, width), bf16),
+                pltpu.SemaphoreType.DMA((rows_dev // (2 * block),)),
+            ],
         ),
         compiler_params=params(14),
         cost_estimate=LIGHT,
@@ -692,6 +711,10 @@
     entries = jnp.concatenate(
         [jnp.arange(block_count, dtype=jnp.int32)[:, None], entries], axis=1
     ).reshape(-1)
+    order = jnp.arange(entries.shape[0], dtype=jnp.int32)
+    earlier = (entries[:, None] == entries[None, :]) & (order[None, :] < order[:, None])
+    first_use = 1 - jnp.max(earlier.astype(jnp.int32), axis=1)
+    entries = jnp.concatenate([entries, first_use])
 
     rows = exchange(send_permute(self_id, loader, features, 2, 0))
     others = [send_permute(self_id, loader, features, 2, 1)]

time: 257 us -> 256 us (level)
  transfers between devices with their start and end apart: 18 -> 18, of which waited for: 11 -> 11; matrix products, arithmetic and copies ran while one was open for 0% -> 1% of each run, Pallas kernels for 48% -> 48%
where the time goes in v8:
time: 256 us; the launch traced here: 254 us
  Pallas kernels  131 us (51%)
  waiting for transfers between devices  77.5 us (30%)
  starting transfers between devices  39.9 us (16%)
  local copies, waits for them, and re-layouts  5.29 us (2%)
    pallas_call x1, Pallas kernels, backward(): pl.pallas_call(functools.partial(backward_kernel, reads, shifts), out_sha...  32.6 us
    all_to_all x6, waiting for transfers between devices, exchange(): lax.all_to_all(buffer, ('row', 'col'), split_axis=0, concat_axis=0, tiled...  32.1 us
    all_to_all x6, starting transfers between devices, exchange(): lax.all_to_all(buffer, ('row', 'col'), split_axis=0, concat_axis=0, tiled...  29.5 us
    ppermute x6, waiting for transfers between devices, body(): moved.append(lax.ppermute(far[at], 'col', perm))  24.3 us
    ppermute x6, waiting for transfers between devices, forward_rows(): return lax.ppermute(outgoing, 'col', perm)  21.1 us
    pallas_call x1, Pallas kernels, forward(): pl.pallas_call(functools.partial(forward_kernel, reads), out_shape=(hbm((...  19 us
    pallas_call x3, Pallas kernels, permute(): pl.pallas_call(permute_kernel, out_shape=hbm((rows_dev, width), bf16), gr...  14.9 us
    pallas_call x3, Pallas kernels, send_permute(): pl.pallas_call(send_kernel, out_shape=hbm((rows_dev, piece), bf16), grid_...  14 us
  transfers between devices with their start and end apart: 18, of which 11 were waited for; matrix products, arithmetic and copies ran while one was open for 1% of the time, Pallas kernels for 48%

profile of v8, /device:TPU:0, one launch (start us, length us, event | category | flops | bytes accessed | tf_op | source)
XLA Modules:
  0.0 254.5 jit_solution(15580152451328913462)
XLA Ops:
  1.6 4.2 %send_permute.3 = bf16[1024,512]{1,0:T(8,128)(2,1)} custom-call(s32[1]{0:T(128)} %bitcast.self_ref, s32[32,1024]{1,0:T(8,128)S(1)} %reshape.107.loader_ref, bf16[1024,1024]{1,0:T(8,128)(2,1)} %rows_ref.4), custom_call_target="tpu_custom_call" | custom-call | tf_op jit(solution)/shard_map/send_permute/pallas_call | solution.py:99
  5.8 7.3 %all-to-all-start = ((bf16[32,32,512]{2,1,0:T(8,128)(2,1)}), bf16[32,32,512]{2,1,0:T(8,128)(2,1)S(1)}, u32[]{:S(2)}, u32[]{:S(2)}) async-start(bf16[32,32,512]{2,1,0:T(8,128)(2,1)} %bitcast.24), calls=%async_computation | async-start | bytes 2097152 | tf_op jit(solution)/shard_map/all_to_all | solution.py:701
  13.1 5.7 %index_tables.1 = (bf16[1024,1024]{1,0:T(8,128)(2,1)}, bf16[1024,1024]{1,0:T(8,128)(2,1)}, bf16[1024,1024]{1,0:T(8,128)(2,1)}) custom-call(s32[1]{0:T(128)} %bitcast.self_ref, s32[32,1024]{1,0:T(8,128)S(1)} %reshape.107.loader_ref), custom_call_target="tpu_custom_call" | custom-call | tf_op jit(solution)/shard_map/index_tables/pallas_call | solution.py:153
  18.8 4.2 %send_permute.4 = bf16[1024,512]{1,0:T(8,128)(2,1)} custom-call(s32[1]{0:T(128)} %bitcast.self_ref, s32[32,1024]{1,0:T(8,128)S(1)} %reshape.107.loader_ref, bf16[1024,1024]{1,0:T(8,128)(2,1)} %rows_ref.4), custom_call_target="tpu_custom_call" | custom-call | tf_op jit(solution)/shard_map/send_permute/pallas_call | solution.py:99
  24.4 14.9 %all-to-all-done = bf16[32,32,512]{2,1,0:T(8,128)(2,1)S(1)} async-done(((bf16[32,32,512]{2,1,0:T(8,128)(2,1)}), bf16[32,32,512]{2,1,0:T(8,128)(2,1)S(1)}, u32[]{:S(2)}, u32[]{:S(2)}) %all-to-all-start) | async-done | bytes 1048608 | tf_op jit(solution)/shard_map/all_to_all | solution.py:701
  43.1 4.0 %outbound.2 = (bf16[256,512]{1,0:T(8,128)(2,1)}, bf16[256,512]{1,0:T(8,128)(2,1)}, bf16[256,512]{1,0:T(8,128)(2,1)}) custom-call(s32[6]{0:T(128)S(1)} %reshape.110.picks_ref, bf16[1024,512]{1,0:T(8,128)(2,1)} %bitcast.19, bf16[1024,1024]{1,0:T(8,128)(2,1)} %get-tuple-element.49.refs_0_.refs_1_.refs_2_.to_node_ref, ...), custom_call_target="tpu_custom_call" | custom-call | tf_op jit(solution)/shard_map/outbound/pallas_call | solution.py:224
  50.3 5.6 %send_permute.5 = bf16[1024,1024]{1,0:T(8,128)(2,1)} custom-call(s32[1]{0:T(128)} %bitcast.self_ref, s32[32,1024]{1,0:T(8,128)S(1)} %reshape.107.loader_ref, bf16[1024,1024]{1,0:T(8,128)(2,1)} %rows_ref.5), custom_call_target="tpu_custom_call" | custom-call | tf_op jit(solution)/shard_map/send_permute/pallas_call | solution.py:99
  55.8 6.0 %collective-permute-done.refs_0_ = bf16[256,512]{1,0:T(8,128)(2,1)S(1)} collective-permute-done((bf16[256,512]{1,0:T(8,128)(2,1)}, bf16[256,512]{1,0:T(8,128)(2,1)S(1)}, u32[]{:S(2)}, u32[]{:S(2)}) %collective-permute-start) | collective-permute-done | bytes 262176 | tf_op jit(solution)/shard_map/ppermute | solution.py:727
  61.8 5.6 %collective-permute-done.2.refs_0_ = bf16[256,512]{1,0:T(8,128)(2,1)S(1)} collective-permute-done((bf16[256,512]{1,0:T(8,128)(2,1)}, bf16[256,512]{1,0:T(8,128)(2,1)S(1)}, u32[]{:S(2)}, u32[]{:S(2)}) %collective-permute-start.2) | collective-permute-done | bytes 262176 | tf_op jit(solution)/shard_map/ppermute | solution.py:727
  73.1 4.3 %outbound.3 = (bf16[256,512]{1,0:T(8,128)(2,1)}, bf16[256,512]{1,0:T(8,128)(2,1)}, bf16[256,512]{1,0:T(8,128)(2,1)}) custom-call(s32[6]{0:T(128)S(1)} %reshape.110.picks_ref, bf16[1024,512]{1,0:T(8,128)(2,1)} %bitcast.6.refs_1_.rows_ref, bf16[1024,1024]{1,0:T(8,128)(2,1)} %get-tuple-element.49.refs_0_.refs_1_.refs_2_.to_node_ref, ...), custom_call_target="tpu_custom_call" | custom-call | tf_op jit(solution)/shard_map/outbound/pallas_call | solution.py:224
  80.9 12.1 %project.1 = (bf16[1024,1024]{1,0:T(8,128)(2,1)}, bf16[1792,1024]{1,0:T(8,128)(2,1)}, bf16[1792,1024]{1,0:T(8,128)(2,1)}) custom-call(bf16[1024,1024]{1,0:T(8,128)(2,1)} %get-tuple-element.49.refs_0_.refs_1_.refs_2_.to_node_ref, bf16[1024,1024]{1,0:T(8,128)(2,1)S(1)} %copy-done.7, bf16[1024,1024]{1,0:T(8,128)(2,1)S(1)} %copy-done.2, ...), custom_call_target="tpu_custom_call" | custom-call | tf_op jit(solution)/shard_map/project/pallas_call | solution.py:253
  93.0 7.3 %collective-permute-done.3.refs_1_ = bf16[256,512]{1,0:T(8,128)(2,1)S(1)} collective-permute-done((bf16[256,512]{1,0:T(8,128)(2,1)}, bf16[256,512]{1,0:T(8,128)(2,1)S(1)}, u32[]{:S(2)}, u32[]{:S(2)}) %collective-permute-start.3) | collective-permute-done | bytes 262176 | tf_op jit(solution)/shard_map/ppermute | solution.py:727
  108.8 19.0 %forward.1 = (bf16[1024,1024]{1,0:T(8,128)(2,1)}, f32[1024,1024]{1,0:T(8,128)}, f32[128,128]{1,0:T(8,128)}) custom-call(s32[64]{0:T(128)S(1)} %pad_add_fusion.1.entries_ref, bf16[1024,1024]{1,0:T(8,128)(2,1)} %get-tuple-element.57.q_ref, f32[1,1024]{1,0:T(1,128)S(1)} %bitcast.17, bf16[1024,1024]{1,0:T(8,128)(2,1)S(1)} %copy-done.10, ...), custom_call_target="tpu_custom_call" | custom-call | tf_op jit(solution)/shard_map/forward/pallas_call | solution.py:383
  127.8 5.0 %all-to-all-start.2 = ((bf16[32,32,1024]{2,1,0:T(8,128)(2,1)}), bf16[32,32,1024]{2,1,0:T(8,128)(2,1)}, u32[]{:S(2)}, u32[]{:S(2)}) async-start(bf16[32,32,1024]{2,1,0:T(8,128)(2,1)} %bitcast.27), calls=%async_computation.2 | async-start | bytes 4194304 | tf_op jit(solution)/shard_map/all_to_all | solution.py:701
  132.9 32.6 %backward.1 = (bf16[1024,1024]{1,0:T(8,128)(2,1)}, bf16[1024,1024]{1,0:T(8,128)(2,1)}, bf16[1024,1024]{1,0:T(8,128)(2,1)}, bf16[256,512]{1,0:T(8,128)(2,1)}, bf1...) custom-call(s32[64]{0:T(128)S(1)} %pad_add_fusion.1.entries_ref, ...), custom_call_target="tpu_custom_call" | custom-call | tf_op jit(solution)/shard_map/backward/pallas_call | solution.py:548
  167.2 6.0 %own_project.3.own_ref = f32[1024,512]{1,0:T(8,128)S(1)} custom-call(bf16[1024,1024]{1,0:T(8,128)(2,1)} %get-tuple-element.77.q_ref, bf16[1024,1024]{1,0:T(8,128)(2,1)} %get-tuple-element.78.k_ref, bf16[1024,1024]{1,0:T(8,128)(2,1)} %get-tuple-element.79.v_ref, bf16[1024,1024]{1,0:T(8,128)(2,1)S(1)} %copy-done.8, bf16[1024,1024]{1,0:T(8,128)(2,1)S(1)} %copy-done.3, ...), custom_call_target="tpu_custom_call" | custom-call | tf_op jit(solution)/shard_map/own_project/pallas_call | solution.py:613
  176.3 7.3 %collective-permute-done.10.refs_1_ = bf16[256,512]{1,0:T(8,128)(2,1)S(1)} collective-permute-done((bf16[256,512]{1,0:T(8,128)(2,1)}, bf16[256,512]{1,0:T(8,128)(2,1)S(1)}, u32[]{:S(2)}, u32[]{:S(2)}) %collective-permute-start.10) | collective-permute-done | bytes 262176 | tf_op jit(solution)/shard_map/ppermute | solution.py:776
  186.4 4.9 %all-to-all-start.5 = ((bf16[32,32,512]{2,1,0:T(8,128)(2,1)}), bf16[32,32,512]{2,1,0:T(8,128)(2,1)S(1)}, u32[]{:S(2)}, u32[]{:S(2)}) async-start(bf16[32,32,512]{2,1,0:T(8,128)(2,1)} %bitcast.25), calls=%async_computation.5 | async-start | bytes 2097152 | tf_op jit(solution)/shard_map/all_to_all | solution.py:701
  196.6 6.0 %own_project.2.own_ref = f32[1024,512]{1,0:T(8,128)S(1)} custom-call(bf16[1024,1024]{1,0:T(8,128)(2,1)} %get-tuple-element.77.q_ref, bf16[1024,1024]{1,0:T(8,128)(2,1)} %get-tuple-element.78.k_ref, bf16[1024,1024]{1,0:T(8,128)(2,1)} %get-tuple-element.79.v_ref, bf16[1024,1024]{1,0:T(8,128)(2,1)S(1)} %copy-done.9, bf16[1024,1024]{1,0:T(8,128)(2,1)S(1)} %copy-done.3, ...), custom_call_target="tpu_custom_call" | custom-call | tf_op jit(solution)/shard_map/own_project/pallas_call | solution.py:613
  202.6 5.2 %collective-permute-done.6.refs_0_ = bf16[256,512]{1,0:T(8,128)(2,1)S(1)} collective-permute-done((bf16[256,512]{1,0:T(8,128)(2,1)}, bf16[256,512]{1,0:T(8,128)(2,1)S(1)}, u32[]{:S(2)}, u32[]{:S(2)}) %collective-permute-start.6) | collective-permute-done | bytes 262176 | tf_op jit(solution)/shard_map/ppermute | solution.py:776
  207.8 8.8 %collective-permute-done.7.refs_1_ = bf16[256,512]{1,0:T(8,128)(2,1)S(1)} collective-permute-done((bf16[256,512]{1,0:T(8,128)(2,1)}, bf16[256,512]{1,0:T(8,128)(2,1)S(1)}, u32[]{:S(2)}, u32[]{:S(2)}) %collective-permute-start.7) | collective-permute-done | bytes 262176 | tf_op jit(solution)/shard_map/ppermute | solution.py:776
  219.5 4.7 %all-to-all-start.4 = ((bf16[32,32,512]{2,1,0:T(8,128)(2,1)}), bf16[32,32,512]{2,1,0:T(8,128)(2,1)}, u32[]{:S(2)}, u32[]{:S(2)}) async-start(bf16[32,32,512]{2,1,0:T(8,128)(2,1)} %bitcast.26), calls=%async_computation.4 | async-start | bytes 2097152 | tf_op jit(solution)/shard_map/all_to_all | solution.py:701
  224.3 6.9 %permute.3 = bf16[1024,1024]{1,0:T(8,128)(2,1)} custom-call(bf16[1024,1024]{1,0:T(8,128)(2,1)S(1)} %copy-done.13, bf16[1024,1024]{1,0:T(8,128)(2,1)} %bitcast.9.rows_ref), custom_call_target="tpu_custom_call" | custom-call | tf_op jit(solution)/shard_map/permute/pallas_call | solution.py:190
  235.2 15.3 %all-to-all-done.4 = bf16[32,32,512]{2,1,0:T(8,128)(2,1)} async-done(((bf16[32,32,512]{2,1,0:T(8,128)(2,1)}), bf16[32,32,512]{2,1,0:T(8,128)(2,1)}, u32[]{:S(2)}, u32[]{:S(2)}) %all-to-all-start.4) | async-done | bytes 1048608 | tf_op jit(solution)/shard_map/all_to_all | solution.py:701
  (85 shorter events, 50.7 us)
Async XLA Ops:
  0.6 22.4 %copy-start = (s32[32,4,2]{0,2,1:T(2,128)S(1)}, s32[32,4,2]{0,2,1:T(2,128)}, u32[]{:S(2)}) copy-start(s32[32,4,2]{0,2,1:T(2,128)} %param.16) | copy-start | bytes 3076
  5.8 33.5 %all-to-all-start = ((bf16[32,32,512]{2,1,0:T(8,128)(2,1)}), bf16[32,32,512]{2,1,0:T(8,128)(2,1)S(1)}, u32[]{:S(2)}, u32[]{:S(2)}) async-start(bf16[32,32,512]{2,1,0:T(8,128)(2,1)} %bitcast.24), calls=%async_computation | async-start | bytes 2097152 | tf_op jit(solution)/shard_map/all_to_all | solution.py:701
  39.3 30.0 %all-to-all-start.1 = ((bf16[32,32,512]{2,1,0:T(8,128)(2,1)}), bf16[32,32,512]{2,1,0:T(8,128)(2,1)}, u32[]{:S(2)}, u32[]{:S(2)}) async-start(bf16[32,32,512]{2,1,0:T(8,128)(2,1)} %bitcast.23), calls=%async_computation.1 | async-start | bytes 2097152 | tf_op jit(solution)/shard_map/all_to_all | solution.py:701
  47.1 14.7 %collective-permute-start = (bf16[256,512]{1,0:T(8,128)(2,1)}, bf16[256,512]{1,0:T(8,128)(2,1)S(1)}, u32[]{:S(2)}, u32[]{:S(2)}) collective-permute-start(bf16[256,512]{1,0:T(8,128)(2,1)} %get-tuple-element.53), channel_id=1, source_target_pairs={{0,1},{1,2},{2,3},{3,0},{4,5},{5,6},{6,7},{7,4},{8,9},{9,10},{10,1... | collective-permute-start | bytes 786440 | tf_op jit(solution)/shard_map/ppermute | solution.py:727
  47.3 14.5 %collective-permute-start.1 = (bf16[256,512]{1,0:T(8,128)(2,1)}, bf16[256,512]{1,0:T(8,128)(2,1)S(1)}, u32[]{:S(2)}, u32[]{:S(2)}) collective-permute-start(bf16[256,512]{1,0:T(8,128)(2,1)} %get-tuple-element.54), channel_id=1, source_target_pairs={{0,2},{1,3},{2,0},{3,1},{4,6},{5,7},{6,4},{7,5},{8,10},{9,11},{10,... | collective-permute-start | bytes 786440 | tf_op jit(solution)/shard_map/ppermute | solution.py:727
  48.9 18.5 %collective-permute-start.2 = (bf16[256,512]{1,0:T(8,128)(2,1)}, bf16[256,512]{1,0:T(8,128)(2,1)S(1)}, u32[]{:S(2)}, u32[]{:S(2)}) collective-permute-start(bf16[256,512]{1,0:T(8,128)(2,1)} %get-tuple-element.55), channel_id=1, source_target_pairs={{0,3},{1,0},{2,1},{3,2},{4,7},{5,4},{6,5},{7,6},{8,11},{9,8},{10,9... | collective-permute-start | bytes 786440 | tf_op jit(solution)/shard_map/ppermute | solution.py:727
  69.3 58.5 %all-to-all-start.3 = ((bf16[32,32,1024]{2,1,0:T(8,128)(2,1)}), bf16[32,32,1024]{2,1,0:T(8,128)(2,1)}, u32[]{:S(2)}, u32[]{:S(2)}) async-start(bf16[32,32,1024]{2,1,0:T(8,128)(2,1)} %bitcast.21), calls=%async_computation.3 | async-start | bytes 4194304 | tf_op jit(solution)/shard_map/all_to_all | solution.py:701
  77.4 22.8 %collective-permute-start.3 = (bf16[256,512]{1,0:T(8,128)(2,1)}, bf16[256,512]{1,0:T(8,128)(2,1)S(1)}, u32[]{:S(2)}, u32[]{:S(2)}) collective-permute-start(bf16[256,512]{1,0:T(8,128)(2,1)} %get-tuple-element.62), channel_id=1, source_target_pairs={{0,1},{1,2},{2,3},{3,0},{4,5},{5,6},{6,7},{7,4},{8,9},{9,10},{10,1... | collective-permute-start | bytes 786440 | tf_op jit(solution)/shard_map/ppermute | solution.py:727
  77.6 24.7 %collective-permute-start.4 = (bf16[256,512]{1,0:T(8,128)(2,1)}, bf16[256,512]{1,0:T(8,128)(2,1)S(1)}, u32[]{:S(2)}, u32[]{:S(2)}) collective-permute-start(bf16[256,512]{1,0:T(8,128)(2,1)} %get-tuple-element.66), channel_id=1, source_target_pairs={{0,3},{1,0},{2,1},{3,2},{4,7},{5,4},{6,5},{7,6},{8,11},{9,8},{10,9... | collective-permute-start | bytes 786440 | tf_op jit(solution)/shard_map/ppermute | solution.py:727
  79.2 27.5 %collective-permute-start.5 = (bf16[256,512]{1,0:T(8,128)(2,1)}, bf16[256,512]{1,0:T(8,128)(2,1)S(1)}, u32[]{:S(2)}, u32[]{:S(2)}) collective-permute-start(bf16[256,512]{1,0:T(8,128)(2,1)} %get-tuple-element.70), channel_id=1, source_target_pairs={{0,2},{1,3},{2,0},{3,1},{4,6},{5,7},{6,4},{7,5},{8,10},{9,11},{10,... | collective-permute-start | bytes 786440 | tf_op jit(solution)/shard_map/ppermute | solution.py:727
  127.8 58.6 %all-to-all-start.2 = ((bf16[32,32,1024]{2,1,0:T(8,128)(2,1)}), bf16[32,32,1024]{2,1,0:T(8,128)(2,1)}, u32[]{:S(2)}, u32[]{:S(2)}) async-start(bf16[32,32,1024]{2,1,0:T(8,128)(2,1)} %bitcast.27), calls=%async_computation.2 | async-start | bytes 4194304 | tf_op jit(solution)/shard_map/all_to_all | solution.py:701
  132.8 34.4 %copy-start.3 = (bf16[1024,1024]{1,0:T(8,128)(2,1)S(1)}, bf16[1024,1024]{1,0:T(8,128)(2,1)}, u32[]{:S(2)}) copy-start(bf16[1024,1024]{1,0:T(8,128)(2,1)} %wk_ref.11) | copy-start | bytes 6291460
  132.8 34.3 %copy-start.5 = (bf16[1024,1024]{1,0:T(8,128)(2,1)S(1)}, bf16[1024,1024]{1,0:T(8,128)(2,1)}, u32[]{:S(2)}) copy-start(bf16[1024,1024]{1,0:T(8,128)(2,1)} %wv_ref.11) | copy-start | bytes 6291460
  132.8 34.3 %copy-start.8 = (bf16[1024,1024]{1,0:T(8,128)(2,1)S(1)}, bf16[1024,1024]{1,0:T(8,128)(2,1)}, u32[]{:S(2)}) copy-start(bf16[1024,1024]{1,0:T(8,128)(2,1)} %wq_ref.5) | copy-start | bytes 6291460
  165.4 10.8 %collective-permute-start.9 = (bf16[256,512]{1,0:T(8,128)(2,1)}, bf16[256,512]{1,0:T(8,128)(2,1)S(1)}, u32[]{:S(2)}, u32[]{:S(2)}) collective-permute-start(bf16[256,512]{1,0:T(8,128)(2,1)} %get-tuple-element.83), channel_id=1, source_target_pairs={{0,3},{1,0},{2,1},{3,2},{4,7},{5,4},{6,5},{7,6},{8,11},{9,8},{10,9... | collective-permute-start | bytes 786440 | tf_op jit(solution)/shard_map/ppermute | solution.py:776
  166.8 16.7 %collective-permute-start.10 = (bf16[256,512]{1,0:T(8,128)(2,1)}, bf16[256,512]{1,0:T(8,128)(2,1)S(1)}, u32[]{:S(2)}, u32[]{:S(2)}) collective-permute-start(bf16[256,512]{1,0:T(8,128)(2,1)} %get-tuple-element.84), channel_id=1, source_target_pairs={{0,2},{1,3},{2,0},{3,1},{4,6},{5,7},{6,4},{7,5},{8,10},{9,11},{10,... | collective-permute-start | bytes 786440 | tf_op jit(solution)/shard_map/ppermute | solution.py:776
  167.2 16.4 %collective-permute-start.11 = (bf16[256,512]{1,0:T(8,128)(2,1)}, bf16[256,512]{1,0:T(8,128)(2,1)S(1)}, u32[]{:S(2)}, u32[]{:S(2)}) collective-permute-start(bf16[256,512]{1,0:T(8,128)(2,1)} %get-tuple-element.85), channel_id=1, source_target_pairs={{0,1},{1,2},{2,3},{3,0},{4,5},{5,6},{6,7},{7,4},{8,9},{9,10},{10,1... | collective-permute-start | bytes 786440 | tf_op jit(solution)/shard_map/ppermute | solution.py:776
  167.2 16.4 %copy-start.11 = (bf16[1024,1024]{1,0:T(8,128)(2,1)S(1)}, bf16[1024,1024]{1,0:T(8,128)(2,1)}, u32[]{:S(2)}) copy-start(bf16[1024,1024]{1,0:T(8,128)(2,1)} %get-tuple-element.58.from_node_ref) | copy-start | bytes 6291460
  186.4 33.1 %all-to-all-start.5 = ((bf16[32,32,512]{2,1,0:T(8,128)(2,1)}), bf16[32,32,512]{2,1,0:T(8,128)(2,1)S(1)}, u32[]{:S(2)}, u32[]{:S(2)}) async-start(bf16[32,32,512]{2,1,0:T(8,128)(2,1)} %bitcast.25), calls=%async_computation.5 | async-start | bytes 2097152 | tf_op jit(solution)/shard_map/all_to_all | solution.py:701
  191.3 16.5 %collective-permute-start.6 = (bf16[256,512]{1,0:T(8,128)(2,1)}, bf16[256,512]{1,0:T(8,128)(2,1)S(1)}, u32[]{:S(2)}, u32[]{:S(2)}) collective-permute-start(bf16[256,512]{1,0:T(8,128)(2,1)} %get-tuple-element.80), channel_id=1, source_target_pairs={{0,3},{1,0},{2,1},{3,2},{4,7},{5,4},{6,5},{7,6},{8,11},{9,8},{10,9... | collective-permute-start | bytes 786440 | tf_op jit(solution)/shard_map/ppermute | solution.py:776
  192.9 23.8 %collective-permute-start.7 = (bf16[256,512]{1,0:T(8,128)(2,1)}, bf16[256,512]{1,0:T(8,128)(2,1)S(1)}, u32[]{:S(2)}, u32[]{:S(2)}) collective-permute-start(bf16[256,512]{1,0:T(8,128)(2,1)} %get-tuple-element.81), channel_id=1, source_target_pairs={{0,2},{1,3},{2,0},{3,1},{4,6},{5,7},{6,4},{7,5},{8,10},{9,11},{10,... | collective-permute-start | bytes 786440 | tf_op jit(solution)/shard_map/ppermute | solution.py:776
  193.3 23.4 %collective-permute-start.8 = (bf16[256,512]{1,0:T(8,128)(2,1)S(1)}, bf16[256,512]{1,0:T(8,128)(2,1)S(1)}, u32[]{:S(2)}, u32[]{:S(2)}) collective-permute-start(bf16[256,512]{1,0:T(8,128)(2,1)S(1)} %copy-done.18), channel_id=1, source_target_pairs={{0,1},{1,2},{2,3},{3,0},{4,5},{5,6},{6,7},{7,4},{8,9},{9,10},{10,1... | collective-permute-start | bytes 786440 | tf_op jit(solution)/shard_map/ppermute | solution.py:776
  196.6 20.1 %copy-start.12 = (bf16[1024,1024]{1,0:T(8,128)(2,1)S(1)}, bf16[1024,1024]{1,0:T(8,128)(2,1)}, u32[]{:S(2)}) copy-start(bf16[1024,1024]{1,0:T(8,128)(2,1)} %get-tuple-element.58.from_node_ref) | copy-start | bytes 6291460
  219.5 30.9 %all-to-all-start.4 = ((bf16[32,32,512]{2,1,0:T(8,128)(2,1)}), bf16[32,32,512]{2,1,0:T(8,128)(2,1)}, u32[]{:S(2)}, u32[]{:S(2)}) async-start(bf16[32,32,512]{2,1,0:T(8,128)(2,1)} %bitcast.26), calls=%async_computation.4 | async-start | bytes 2097152 | tf_op jit(solution)/shard_map/all_to_all | solution.py:701
  (13 other events, 72.6 us)
